TPU v7x, 256 devices: a whole 4x4x8 slice. The times are simulated.
256 devices in a mesh: seq: 64 (over z_lo, y, x, core), head: 4 (over z_hi).
Axes of the slice: x: 4, y: 4, z: 8 (z_hi: 4, z_lo: 2; z = z_hi * 2 + z_lo), core: 2. Of those that a mesh axis runs over, the one named last changes fastest.
Arguments:
- queries: bfloat16 [8192, 4096], P('seq', 'head'), may hold values from -500 to 500
- first_key_rows: bfloat16 [8192, 2048], P('seq', 'head'), may hold values from -6 to 6
- first_value_rows: bfloat16 [8192, 2048], P('seq', 'head'), may hold values from -6 to 6
- second_key_rows: bfloat16 [8192, 2048], P('seq', 'head'), may hold values from -6 to 6
- second_value_rows: bfloat16 [8192, 2048], P('seq', 'head'), may hold values from -6 to 6
- out_weight: bfloat16 [4096, 4096], P('head'), may hold values from -6 to 6
Outputs:
- projected: bfloat16 [8192, 4096], P('seq', 'head')
All inputs are finite; a program needn't handle non-finite values.
Results may differ from a plain program's by a relative error of at most 0.015.
The roundings to bfloat16 on the way count: a program that leaves them out, or rounds other values in their place, can miss the bound.
Values may be sent and summed in bfloat16 or wider, within the bound.
No kernel may reach another device: no remote copies, remote signals or barrier semaphores. Data moves between devices by JAX's collectives and lax.ppermute only.
A program may use at most 64 MiB of HBM per device.

v0:
```python
import jax
import jax.numpy as jnp
from jax import lax
from jax.sharding import PartitionSpec as P

HEAD_SIZE = 128
W1 = 512
W2 = 32


def from_behind(shard, axis, by):
    length = lax.axis_size(axis)
    pairs = [(i, i + by) for i in range(length) if 0 <= i + by < length]
    return lax.ppermute(shard, axis, pairs)


def lag_windows(rows, span, count):
    feature_count = rows.shape[1]
    padded = jnp.concatenate([rows, jnp.zeros((1, feature_count), rows.dtype)], axis=0)
    length = padded.shape[0]
    tiled = jnp.broadcast_to(padded[None], (span, length, feature_count)).reshape(
        span * length, feature_count
    )
    return tiled[: span * (length - 1)].reshape(span, length - 1, feature_count)[
        :, span : span + count
    ]


def window_attend(query_block, outer_keys, outer_values, inner_keys, inner_values, first_pos):
    row_count = query_block.shape[0]
    inner_span = inner_keys.shape[0] - row_count
    outer_span = outer_keys.shape[0] - row_count
    scale_factor = query_block.shape[1] ** (-0.5)
    inner_key_win = lag_windows(inner_keys, inner_span, row_count)
    inner_val_win = lag_windows(inner_values, inner_span, row_count)
    blended = (query_block.astype(jnp.float32)[None] * inner_key_win.astype(jnp.float32)).astype(
        jnp.bfloat16
    )
    scores = (
        jnp.einsum("wid,jd->wij", blended, outer_keys, preferred_element_type=jnp.float32)
        * scale_factor
    )
    row_index = lax.broadcasted_iota(jnp.int32, scores.shape, 1)
    col_index = lax.broadcasted_iota(jnp.int32, scores.shape, 2)
    lag_index = lax.broadcasted_iota(jnp.int32, scores.shape, 0)
    allowed = (col_index > row_index) & (col_index <= row_index + outer_span)
    allowed = (
        allowed
        & (first_pos - outer_span + col_index >= 0)
        & (first_pos + row_index - lag_index >= 0)
    )
    scores = jnp.where(allowed, scores, -1e30)
    row_max = jnp.max(scores, axis=(0, 2), keepdims=True)
    expon = jnp.where(allowed, jnp.exp(scores - row_max), 0.0)
    row_total = jnp.sum(expon, axis=(0, 2), keepdims=True)
    weights = (expon / row_total).astype(jnp.bfloat16)
    inner_sum = jnp.einsum("wij,jd->wid", weights, outer_values, preferred_element_type=jnp.float32)
    return jnp.sum(inner_val_win.astype(jnp.float32) * inner_sum, axis=0)


def local(
    queries, first_key_rows, first_value_rows, second_key_rows, second_value_rows, out_weight
):
    row_count = queries.shape[0]
    head_count = queries.shape[1] // HEAD_SIZE
    query_group_width = head_count // (first_key_rows.shape[1] // HEAD_SIZE)
    shard_count = W1 // row_count
    first_pos = lax.axis_index("seq") * row_count
    tail_rows = (second_key_rows[row_count - W2 :], second_value_rows[row_count - W2 :])
    prior_inner = from_behind((tail_rows[0], tail_rows[1]), "seq", 1)
    pieces_keys = []
    pieces_values = []
    for distance in range(shard_count, 0, -1):
        arrived = from_behind((first_key_rows, first_value_rows), "seq", distance)
        pieces_keys.append(arrived[0])
        pieces_values.append(arrived[1])
    prior_keys = jnp.concatenate(pieces_keys, axis=0)
    prior_values = jnp.concatenate(pieces_values, axis=0)
    outer_keys_all = jnp.concatenate([prior_keys, first_key_rows], axis=0)
    outer_vals_all = jnp.concatenate([prior_values, first_value_rows], axis=0)
    inner_keys_all = jnp.concatenate([prior_inner[0], second_key_rows], axis=0)
    inner_vals_all = jnp.concatenate([prior_inner[1], second_value_rows], axis=0)

    def per_head(head):
        kv_start = head // query_group_width * HEAD_SIZE
        return window_attend(
            lax.dynamic_slice_in_dim(queries, head * HEAD_SIZE, HEAD_SIZE, 1),
            lax.dynamic_slice_in_dim(outer_keys_all, kv_start, HEAD_SIZE, 1),
            lax.dynamic_slice_in_dim(outer_vals_all, kv_start, HEAD_SIZE, 1),
            lax.dynamic_slice_in_dim(inner_keys_all, kv_start, HEAD_SIZE, 1),
            lax.dynamic_slice_in_dim(inner_vals_all, kv_start, HEAD_SIZE, 1),
            first_pos,
        ).astype(jnp.bfloat16)

    heads_out = lax.map(per_head, jnp.arange(head_count, dtype=jnp.int32))
    attended = jnp.transpose(heads_out, (1, 0, 2)).reshape(row_count, head_count * HEAD_SIZE)
    shared = lax.psum_scatter(
        lax.dot_general(
            out_weight, attended, (((0,), (1,)), ((), ())), preferred_element_type=jnp.float32
        ).astype(jnp.bfloat16),
        "head",
        scatter_dimension=0,
        tiled=True,
    )
    return jnp.transpose(shared)


def solution(mesh):
    in_specs = (
        P("seq", "head"),
        P("seq", "head"),
        P("seq", "head"),
        P("seq", "head"),
        P("seq", "head"),
        P("head", None),
    )
    out_specs = P("seq", "head")
    return jax.shard_map(local, mesh=mesh, in_specs=in_specs, out_specs=out_specs, check_vma=False)
```

profile of v0, /device:TPU:1, one launch (start us, length us, event | category | flops | bytes accessed | tf_op | source)
XLA Modules:
  0.0 273.0 jit_solution(12211662171619661508)
XLA Ops:
  7.3 4.5 %collective-permute-start.1 = (bf16[32,512]{1,0:T(8,128)(2,1)S(1)}, bf16[32,512]{1,0:T(8,128)(2,1)S(1)}, u32[]{:S(2)}, u32[]{:S(2)}) collective-permute-start(bf16[32,512]{1,0:T(8,128)(2,1)S(1)} %slice.31), channel_id=1, source_target_pairs={{0,4},{4,8},{8,12},{12,16},{16,20},{20,24},{24,28},{28,32},{32,36}... | collective-permute-start | bytes 98312 | tf_op jit(solution)/shard_map/ppermute | solution.py:14
  11.8 3.1 %collective-permute-start.4 = (bf16[128,512]{1,0:T(8,128)(2,1)}, bf16[128,512]{1,0:T(8,128)(2,1)S(1)}, u32[]{:S(2)}, u32[]{:S(2)}) collective-permute-start(bf16[128,512]{1,0:T(8,128)(2,1)} %param.9), channel_id=1, source_target_pairs={{0,8},{4,12},{8,16},{12,20},{16,24},{20,28},{24,32},{28,36},{32,40... | collective-permute-start | bytes 393224 | tf_op jit(solution)/shard_map/ppermute | solution.py:14
  14.9 3.4 %collective-permute-start.3 = (bf16[128,512]{1,0:T(8,128)(2,1)}, bf16[128,512]{1,0:T(8,128)(2,1)S(1)}, u32[]{:S(2)}, u32[]{:S(2)}) collective-permute-start(bf16[128,512]{1,0:T(8,128)(2,1)} %param.9), channel_id=1, source_target_pairs={{0,12},{4,16},{8,20},{12,24},{16,28},{20,32},{24,36},{28,40},{32,4... | collective-permute-start | bytes 393224 | tf_op jit(solution)/shard_map/ppermute | solution.py:14
  18.4 3.4 %collective-permute-start.2 = (bf16[128,512]{1,0:T(8,128)(2,1)}, bf16[128,512]{1,0:T(8,128)(2,1)S(1)}, u32[]{:S(2)}, u32[]{:S(2)}) collective-permute-start(bf16[128,512]{1,0:T(8,128)(2,1)} %param.9), channel_id=1, source_target_pairs={{0,16},{4,20},{8,24},{12,28},{16,32},{20,36},{24,40},{28,44},{32,4... | collective-permute-start | bytes 393224 | tf_op jit(solution)/shard_map/ppermute | solution.py:14
  22.6 3.7 %collective-permute-start = (bf16[32,512]{1,0:T(8,128)(2,1)S(1)}, bf16[32,512]{1,0:T(8,128)(2,1)S(1)}, u32[]{:S(2)}, u32[]{:S(2)}) collective-permute-start(bf16[32,512]{1,0:T(8,128)(2,1)S(1)} %slice.30), channel_id=1, source_target_pairs={{0,4},{4,8},{8,12},{12,16},{16,20},{20,24},{24,28},{28,32},{32,36}... | collective-permute-start | bytes 98312 | tf_op jit(solution)/shard_map/ppermute | solution.py:14
  26.3 4.4 %collective-permute-start.6 = (bf16[128,512]{1,0:T(8,128)(2,1)}, bf16[128,512]{1,0:T(8,128)(2,1)S(1)}, u32[]{:S(2)}, u32[]{:S(2)}) collective-permute-start(bf16[128,512]{1,0:T(8,128)(2,1)} %param.10), channel_id=1, source_target_pairs={{0,16},{4,20},{8,24},{12,28},{16,32},{20,36},{24,40},{28,44},{32,4... | collective-permute-start | bytes 393224 | tf_op jit(solution)/shard_map/ppermute | solution.py:14
  30.7 0.9 pad_maximum_fusion.1
  31.6 3.1 %collective-permute-start.7 = (bf16[128,512]{1,0:T(8,128)(2,1)}, bf16[128,512]{1,0:T(8,128)(2,1)S(1)}, u32[]{:S(2)}, u32[]{:S(2)}) collective-permute-start(bf16[128,512]{1,0:T(8,128)(2,1)} %param.10), channel_id=1, source_target_pairs={{0,12},{4,16},{8,20},{12,24},{16,28},{20,32},{24,36},{28,40},{32,4... | collective-permute-start | bytes 393224 | tf_op jit(solution)/shard_map/ppermute | solution.py:14
  34.7 0.9 pad_maximum_fusion
  35.7 2.5 collective-permute-start.8
  38.2 2.8 %collective-permute-start.9 = (bf16[128,512]{1,0:T(8,128)(2,1)}, bf16[128,512]{1,0:T(8,128)(2,1)S(1)}, u32[]{:S(2)}, u32[]{:S(2)}) collective-permute-start(bf16[128,512]{1,0:T(8,128)(2,1)} %param.10), channel_id=1, source_target_pairs={{0,4},{4,8},{8,12},{12,16},{16,20},{20,24},{24,28},{28,32},{32,36}... | collective-permute-start | bytes 393224 | tf_op jit(solution)/shard_map/ppermute | solution.py:14
  41.5 4.5 %collective-permute-start.5 = (bf16[128,512]{1,0:T(8,128)(2,1)}, bf16[128,512]{1,0:T(8,128)(2,1)S(1)}, u32[]{:S(2)}, u32[]{:S(2)}) collective-permute-start(bf16[128,512]{1,0:T(8,128)(2,1)} %param.9), channel_id=1, source_target_pairs={{0,4},{4,8},{8,12},{12,16},{16,20},{20,24},{24,28},{28,32},{32,36}... | collective-permute-start | bytes 393224 | tf_op jit(solution)/shard_map/ppermute | solution.py:14
  46.1 0.9 constant_dynamic-update-slice_fusion.6
  47.1 1.2 collective-permute-done.5
  48.3 0.9 constant_dynamic-update-slice_fusion.1
  49.3 168.6 %while.12 = (s32[]{:T(128)}, bf16[8,128,128]{1,2,0:T(8,128)(2,1)S(1)}, s32[8]{0:T(128)S(1)}, bf16[160,512]{1,0:T(8,128)(2,1)S(1)}, s32[]{:T(128)}, /*index=5*/s3...) while((s32[]{:T(128)}, ...), condition=%wide.region_4.5_spmd, body=%wide.region_0.4_spmd.sunk | while | flops 1437074688 | bytes 64859496 | solution.py:95
  53.3 0.8 dynamic-slice_convert_fusion.2
  55.0 1.3 reshape.48
  56.3 1.4 slice.49
  57.7 3.8 %fusion.26 = (f32[128]{0:T(128)S(1)}, f32[32,128,640]{2,1,0:T(8,128)S(1)}) fusion(s32[128]{0:T(128)S(1)} %get-tuple-element.220, pred[640]{0:T(1024)(128)(4,1)S(1)} %add_compare_fusion.2, s32[128]{0:T(128)S(1)} %get-tuple-element.221, bf16[640,512]{1,0:T(8,128)(2,1)} %copy-done.3, s32[]{:T(128)S(6)} %select_n.70, ...), kind=kOutput, calls=%fused_computation.9.clone.1 | convolution fusion | flops 698875776 | bytes 11766276 | tf_op jit(solution)/shard_map/while/body/eval_jaxpr/wid,jd->wij/dot_general | solution.py:40
  61.6 4.1 %fusion.27 = f32[128]{0:T(128)S(1)} fusion(f32[32,128,640]{2,1,0:T(8,128)S(1)} %get-tuple-element.223, f32[128]{0:T(128)S(1)} %get-tuple-element.224, s32[128]{0:T(128)S(1)} %get-tuple-element.220, pred[640]{0:T(1024)(128)(4,1)S(1)} %add_compare_fusion.2, s32[128]{0:T(128)S(1)} %get-tuple-element.221), kind=kLoop, calls=%fused_computation.10.clone.1 | loop fusion | flops 31457152 | bytes 10488448 | tf_op jit(solution)/shard_map/while/body/eval_jaxpr/reduce_sum | solution.py:55
  65.7 4.5 %multiply_reduce_fusion.2 = bf16[128,128]{1,0:T(8,128)(2,1)S(1)} fusion(f32[32,128,640]{2,1,0:T(8,128)S(1)} %get-tuple-element.223, f32[128]{0:T(128)S(1)} %fusion.27, f32[128]{0:T(128)S(1)} %get-tuple-element.224, s32[128]{0:T(128)S(1)} %get-tuple-element.220, s32[128]{0:T(128)S(1)} %get-tuple-element.221, ...), kind=kOutput, calls=%fused_computation.12.clone.1 | convolution fusion | flops 706723840 | bytes 11734020 | tf_op jit(solution)/shard_map/while/body/eval_jaxpr/wij,jd->wid/dot_general | solution.py:57
  74.4 0.8 dynamic-slice_convert_fusion.2
  76.0 1.3 reshape.48
  77.3 1.4 slice.49
  78.7 3.9 %fusion.26 = (f32[128]{0:T(128)S(1)}, f32[32,128,640]{2,1,0:T(8,128)S(1)}) fusion(s32[128]{0:T(128)S(1)} %get-tuple-element.220, pred[640]{0:T(1024)(128)(4,1)S(1)} %add_compare_fusion.2, s32[128]{0:T(128)S(1)} %get-tuple-element.221, bf16[640,512]{1,0:T(8,128)(2,1)} %copy-done.3, s32[]{:T(128)S(6)} %select_n.70, ...), kind=kOutput, calls=%fused_computation.9.clone.1 | convolution fusion | flops 698875776 | bytes 11766276 | tf_op jit(solution)/shard_map/while/body/eval_jaxpr/wid,jd->wij/dot_general | solution.py:40
  82.6 4.1 %fusion.27 = f32[128]{0:T(128)S(1)} fusion(f32[32,128,640]{2,1,0:T(8,128)S(1)} %get-tuple-element.223, f32[128]{0:T(128)S(1)} %get-tuple-element.224, s32[128]{0:T(128)S(1)} %get-tuple-element.220, pred[640]{0:T(1024)(128)(4,1)S(1)} %add_compare_fusion.2, s32[128]{0:T(128)S(1)} %get-tuple-element.221), kind=kLoop, calls=%fused_computation.10.clone.1 | loop fusion | flops 31457152 | bytes 10488448 | tf_op jit(solution)/shard_map/while/body/eval_jaxpr/reduce_sum | solution.py:55
  86.8 4.5 %multiply_reduce_fusion.2 = bf16[128,128]{1,0:T(8,128)(2,1)S(1)} fusion(f32[32,128,640]{2,1,0:T(8,128)S(1)} %get-tuple-element.223, f32[128]{0:T(128)S(1)} %fusion.27, f32[128]{0:T(128)S(1)} %get-tuple-element.224, s32[128]{0:T(128)S(1)} %get-tuple-element.220, s32[128]{0:T(128)S(1)} %get-tuple-element.221, ...), kind=kOutput, calls=%fused_computation.12.clone.1 | convolution fusion | flops 706723840 | bytes 11734020 | tf_op jit(solution)/shard_map/while/body/eval_jaxpr/wij,jd->wid/dot_general | solution.py:57
  95.4 0.8 dynamic-slice_convert_fusion.2
  97.1 1.3 reshape.48
  98.4 1.4 slice.49
  99.8 3.9 %fusion.26 = (f32[128]{0:T(128)S(1)}, f32[32,128,640]{2,1,0:T(8,128)S(1)}) fusion(s32[128]{0:T(128)S(1)} %get-tuple-element.220, pred[640]{0:T(1024)(128)(4,1)S(1)} %add_compare_fusion.2, s32[128]{0:T(128)S(1)} %get-tuple-element.221, bf16[640,512]{1,0:T(8,128)(2,1)} %copy-done.3, s32[]{:T(128)S(6)} %select_n.70, ...), kind=kOutput, calls=%fused_computation.9.clone.1 | convolution fusion | flops 698875776 | bytes 11766276 | tf_op jit(solution)/shard_map/while/body/eval_jaxpr/wid,jd->wij/dot_general | solution.py:40
  103.7 4.1 %fusion.27 = f32[128]{0:T(128)S(1)} fusion(f32[32,128,640]{2,1,0:T(8,128)S(1)} %get-tuple-element.223, f32[128]{0:T(128)S(1)} %get-tuple-element.224, s32[128]{0:T(128)S(1)} %get-tuple-element.220, pred[640]{0:T(1024)(128)(4,1)S(1)} %add_compare_fusion.2, s32[128]{0:T(128)S(1)} %get-tuple-element.221), kind=kLoop, calls=%fused_computation.10.clone.1 | loop fusion | flops 31457152 | bytes 10488448 | tf_op jit(solution)/shard_map/while/body/eval_jaxpr/reduce_sum | solution.py:55
  107.9 4.5 %multiply_reduce_fusion.2 = bf16[128,128]{1,0:T(8,128)(2,1)S(1)} fusion(f32[32,128,640]{2,1,0:T(8,128)S(1)} %get-tuple-element.223, f32[128]{0:T(128)S(1)} %fusion.27, f32[128]{0:T(128)S(1)} %get-tuple-element.224, s32[128]{0:T(128)S(1)} %get-tuple-element.220, s32[128]{0:T(128)S(1)} %get-tuple-element.221, ...), kind=kOutput, calls=%fused_computation.12.clone.1 | convolution fusion | flops 706723840 | bytes 11734020 | tf_op jit(solution)/shard_map/while/body/eval_jaxpr/wij,jd->wid/dot_general | solution.py:57
  118.2 1.3 reshape.48
  119.5 1.4 slice.49
  120.9 3.9 %fusion.26 = (f32[128]{0:T(128)S(1)}, f32[32,128,640]{2,1,0:T(8,128)S(1)}) fusion(s32[128]{0:T(128)S(1)} %get-tuple-element.220, pred[640]{0:T(1024)(128)(4,1)S(1)} %add_compare_fusion.2, s32[128]{0:T(128)S(1)} %get-tuple-element.221, bf16[640,512]{1,0:T(8,128)(2,1)} %copy-done.3, s32[]{:T(128)S(6)} %select_n.70, ...), kind=kOutput, calls=%fused_computation.9.clone.1 | convolution fusion | flops 698875776 | bytes 11766276 | tf_op jit(solution)/shard_map/while/body/eval_jaxpr/wid,jd->wij/dot_general | solution.py:40
  124.8 4.1 %fusion.27 = f32[128]{0:T(128)S(1)} fusion(f32[32,128,640]{2,1,0:T(8,128)S(1)} %get-tuple-element.223, f32[128]{0:T(128)S(1)} %get-tuple-element.224, s32[128]{0:T(128)S(1)} %get-tuple-element.220, pred[640]{0:T(1024)(128)(4,1)S(1)} %add_compare_fusion.2, s32[128]{0:T(128)S(1)} %get-tuple-element.221), kind=kLoop, calls=%fused_computation.10.clone.1 | loop fusion | flops 31457152 | bytes 10488448 | tf_op jit(solution)/shard_map/while/body/eval_jaxpr/reduce_sum | solution.py:55
  128.9 4.5 %multiply_reduce_fusion.2 = bf16[128,128]{1,0:T(8,128)(2,1)S(1)} fusion(f32[32,128,640]{2,1,0:T(8,128)S(1)} %get-tuple-element.223, f32[128]{0:T(128)S(1)} %fusion.27, f32[128]{0:T(128)S(1)} %get-tuple-element.224, s32[128]{0:T(128)S(1)} %get-tuple-element.220, s32[128]{0:T(128)S(1)} %get-tuple-element.221, ...), kind=kOutput, calls=%fused_computation.12.clone.1 | convolution fusion | flops 706723840 | bytes 11734020 | tf_op jit(solution)/shard_map/while/body/eval_jaxpr/wij,jd->wid/dot_general | solution.py:57
  137.6 0.8 dynamic-slice_convert_fusion.2
  139.2 1.3 reshape.48
  140.6 1.4 slice.49
  142.0 3.9 %fusion.26 = (f32[128]{0:T(128)S(1)}, f32[32,128,640]{2,1,0:T(8,128)S(1)}) fusion(s32[128]{0:T(128)S(1)} %get-tuple-element.220, pred[640]{0:T(1024)(128)(4,1)S(1)} %add_compare_fusion.2, s32[128]{0:T(128)S(1)} %get-tuple-element.221, bf16[640,512]{1,0:T(8,128)(2,1)} %copy-done.3, s32[]{:T(128)S(6)} %select_n.70, ...), kind=kOutput, calls=%fused_computation.9.clone.1 | convolution fusion | flops 698875776 | bytes 11766276 | tf_op jit(solution)/shard_map/while/body/eval_jaxpr/wid,jd->wij/dot_general | solution.py:40
  145.9 4.1 %fusion.27 = f32[128]{0:T(128)S(1)} fusion(f32[32,128,640]{2,1,0:T(8,128)S(1)} %get-tuple-element.223, f32[128]{0:T(128)S(1)} %get-tuple-element.224, s32[128]{0:T(128)S(1)} %get-tuple-element.220, pred[640]{0:T(1024)(128)(4,1)S(1)} %add_compare_fusion.2, s32[128]{0:T(128)S(1)} %get-tuple-element.221), kind=kLoop, calls=%fused_computation.10.clone.1 | loop fusion | flops 31457152 | bytes 10488448 | tf_op jit(solution)/shard_map/while/body/eval_jaxpr/reduce_sum | solution.py:55
  150.0 4.5 %multiply_reduce_fusion.2 = bf16[128,128]{1,0:T(8,128)(2,1)S(1)} fusion(f32[32,128,640]{2,1,0:T(8,128)S(1)} %get-tuple-element.223, f32[128]{0:T(128)S(1)} %fusion.27, f32[128]{0:T(128)S(1)} %get-tuple-element.224, s32[128]{0:T(128)S(1)} %get-tuple-element.220, s32[128]{0:T(128)S(1)} %get-tuple-element.221, ...), kind=kOutput, calls=%fused_computation.12.clone.1 | convolution fusion | flops 706723840 | bytes 11734020 | tf_op jit(solution)/shard_map/while/body/eval_jaxpr/wij,jd->wid/dot_general | solution.py:57
  158.7 0.8 dynamic-slice_convert_fusion.2
  160.3 1.3 reshape.48
  161.6 1.4 slice.49
  163.0 3.8 %fusion.26 = (f32[128]{0:T(128)S(1)}, f32[32,128,640]{2,1,0:T(8,128)S(1)}) fusion(s32[128]{0:T(128)S(1)} %get-tuple-element.220, pred[640]{0:T(1024)(128)(4,1)S(1)} %add_compare_fusion.2, s32[128]{0:T(128)S(1)} %get-tuple-element.221, bf16[640,512]{1,0:T(8,128)(2,1)} %copy-done.3, s32[]{:T(128)S(6)} %select_n.70, ...), kind=kOutput, calls=%fused_computation.9.clone.1 | convolution fusion | flops 698875776 | bytes 11766276 | tf_op jit(solution)/shard_map/while/body/eval_jaxpr/wid,jd->wij/dot_general | solution.py:40
  166.9 4.1 %fusion.27 = f32[128]{0:T(128)S(1)} fusion(f32[32,128,640]{2,1,0:T(8,128)S(1)} %get-tuple-element.223, f32[128]{0:T(128)S(1)} %get-tuple-element.224, s32[128]{0:T(128)S(1)} %get-tuple-element.220, pred[640]{0:T(1024)(128)(4,1)S(1)} %add_compare_fusion.2, s32[128]{0:T(128)S(1)} %get-tuple-element.221), kind=kLoop, calls=%fused_computation.10.clone.1 | loop fusion | flops 31457152 | bytes 10488448 | tf_op jit(solution)/shard_map/while/body/eval_jaxpr/reduce_sum | solution.py:55
  171.1 4.5 %multiply_reduce_fusion.2 = bf16[128,128]{1,0:T(8,128)(2,1)S(1)} fusion(f32[32,128,640]{2,1,0:T(8,128)S(1)} %get-tuple-element.223, f32[128]{0:T(128)S(1)} %fusion.27, f32[128]{0:T(128)S(1)} %get-tuple-element.224, s32[128]{0:T(128)S(1)} %get-tuple-element.220, s32[128]{0:T(128)S(1)} %get-tuple-element.221, ...), kind=kOutput, calls=%fused_computation.12.clone.1 | convolution fusion | flops 706723840 | bytes 11734020 | tf_op jit(solution)/shard_map/while/body/eval_jaxpr/wij,jd->wid/dot_general | solution.py:57
  179.7 0.8 dynamic-slice_convert_fusion.2
  181.4 1.3 reshape.48
  182.7 1.4 slice.49
  184.1 3.8 %fusion.26 = (f32[128]{0:T(128)S(1)}, f32[32,128,640]{2,1,0:T(8,128)S(1)}) fusion(s32[128]{0:T(128)S(1)} %get-tuple-element.220, pred[640]{0:T(1024)(128)(4,1)S(1)} %add_compare_fusion.2, s32[128]{0:T(128)S(1)} %get-tuple-element.221, bf16[640,512]{1,0:T(8,128)(2,1)} %copy-done.3, s32[]{:T(128)S(6)} %select_n.70, ...), kind=kOutput, calls=%fused_computation.9.clone.1 | convolution fusion | flops 698875776 | bytes 11766276 | tf_op jit(solution)/shard_map/while/body/eval_jaxpr/wid,jd->wij/dot_general | solution.py:40
  188.0 4.1 %fusion.27 = f32[128]{0:T(128)S(1)} fusion(f32[32,128,640]{2,1,0:T(8,128)S(1)} %get-tuple-element.223, f32[128]{0:T(128)S(1)} %get-tuple-element.224, s32[128]{0:T(128)S(1)} %get-tuple-element.220, pred[640]{0:T(1024)(128)(4,1)S(1)} %add_compare_fusion.2, s32[128]{0:T(128)S(1)} %get-tuple-element.221), kind=kLoop, calls=%fused_computation.10.clone.1 | loop fusion | flops 31457152 | bytes 10488448 | tf_op jit(solution)/shard_map/while/body/eval_jaxpr/reduce_sum | solution.py:55
  192.2 4.5 %multiply_reduce_fusion.2 = bf16[128,128]{1,0:T(8,128)(2,1)S(1)} fusion(f32[32,128,640]{2,1,0:T(8,128)S(1)} %get-tuple-element.223, f32[128]{0:T(128)S(1)} %fusion.27, f32[128]{0:T(128)S(1)} %get-tuple-element.224, s32[128]{0:T(128)S(1)} %get-tuple-element.220, s32[128]{0:T(128)S(1)} %get-tuple-element.221, ...), kind=kOutput, calls=%fused_computation.12.clone.1 | convolution fusion | flops 706723840 | bytes 11734020 | tf_op jit(solution)/shard_map/while/body/eval_jaxpr/wij,jd->wid/dot_general | solution.py:57
  202.5 1.3 reshape.48
  203.8 1.4 slice.49
  205.2 3.9 %fusion.26 = (f32[128]{0:T(128)S(1)}, f32[32,128,640]{2,1,0:T(8,128)S(1)}) fusion(s32[128]{0:T(128)S(1)} %get-tuple-element.220, pred[640]{0:T(1024)(128)(4,1)S(1)} %add_compare_fusion.2, s32[128]{0:T(128)S(1)} %get-tuple-element.221, bf16[640,512]{1,0:T(8,128)(2,1)} %copy-done.3, s32[]{:T(128)S(6)} %select_n.70, ...), kind=kOutput, calls=%fused_computation.9.clone.1 | convolution fusion | flops 698875776 | bytes 11766276 | tf_op jit(solution)/shard_map/while/body/eval_jaxpr/wid,jd->wij/dot_general | solution.py:40
  209.1 4.1 %fusion.27 = f32[128]{0:T(128)S(1)} fusion(f32[32,128,640]{2,1,0:T(8,128)S(1)} %get-tuple-element.223, f32[128]{0:T(128)S(1)} %get-tuple-element.224, s32[128]{0:T(128)S(1)} %get-tuple-element.220, pred[640]{0:T(1024)(128)(4,1)S(1)} %add_compare_fusion.2, s32[128]{0:T(128)S(1)} %get-tuple-element.221), kind=kLoop, calls=%fused_computation.10.clone.1 | loop fusion | flops 31457152 | bytes 10488448 | tf_op jit(solution)/shard_map/while/body/eval_jaxpr/reduce_sum | solution.py:55
  213.2 4.5 %multiply_reduce_fusion.2 = bf16[128,128]{1,0:T(8,128)(2,1)S(1)} fusion(f32[32,128,640]{2,1,0:T(8,128)S(1)} %get-tuple-element.223, f32[128]{0:T(128)S(1)} %fusion.27, f32[128]{0:T(128)S(1)} %get-tuple-element.224, s32[128]{0:T(128)S(1)} %get-tuple-element.220, s32[128]{0:T(128)S(1)} %get-tuple-element.221, ...), kind=kOutput, calls=%fused_computation.12.clone.1 | convolution fusion | flops 706723840 | bytes 11734020 | tf_op jit(solution)/shard_map/while/body/eval_jaxpr/wij,jd->wid/dot_general | solution.py:57
  217.9 5.7 %fusion.19 = bf16[4096,128]{0,1:T(8,128)(2,1)} fusion(bf16[128,1024]{0,1:T(8,128)(2,1)S(1)} %bitcast.37, bf16[1024,4096]{1,0:T(8,128)(2,1)} %param.13), kind=kOutput, calls=%fused_computation.35 | convolution fusion | flops 1074266112 | bytes 9699328 | tf_op jit(solution)/shard_map/dot_general | solution.py:98
  223.5 42.6 %reduce-scatter.2.cloned.1.call-done = bf16[1024,128]{0,1:T(8,128)(2,1)} async-done(((bf16[4096,128]{0,1:T(8,128)(2,1)}), bf16[1024,128]{0,1:T(8,128)(2,1)}) %reduce-scatter.2.cloned.1.call-update) | async-done | bytes 262160 | tf_op jit(solution)/shard_map/reduce_scatter | solution.py:97
  (209 shorter events, 17.7 us)
Async XLA Ops:
  6.5 259.6 %reduce-scatter.2.cloned.1.call-start = ((), (), s32[]{:S(2)}) async-start(), calls=%async_computation.1 | async-start | bytes 1310720 | tf_op jit(solution)/shard_map/reduce_scatter | solution.py:97
  7.3 19.0 %collective-permute-start.1 = (bf16[32,512]{1,0:T(8,128)(2,1)S(1)}, bf16[32,512]{1,0:T(8,128)(2,1)S(1)}, u32[]{:S(2)}, u32[]{:S(2)}) collective-permute-start(bf16[32,512]{1,0:T(8,128)(2,1)S(1)} %slice.31), channel_id=1, source_target_pairs={{0,4},{4,8},{8,12},{12,16},{16,20},{20,24},{24,28},{28,32},{32,36}... | collective-permute-start | bytes 98312 | tf_op jit(solution)/shard_map/ppermute | solution.py:14
  11.8 35.3 %collective-permute-start.4 = (bf16[128,512]{1,0:T(8,128)(2,1)}, bf16[128,512]{1,0:T(8,128)(2,1)S(1)}, u32[]{:S(2)}, u32[]{:S(2)}) collective-permute-start(bf16[128,512]{1,0:T(8,128)(2,1)} %param.9), channel_id=1, source_target_pairs={{0,8},{4,12},{8,16},{12,20},{16,24},{20,28},{24,32},{28,36},{32,40... | collective-permute-start | bytes 393224 | tf_op jit(solution)/shard_map/ppermute | solution.py:14
  14.9 32.1 %collective-permute-start.3 = (bf16[128,512]{1,0:T(8,128)(2,1)}, bf16[128,512]{1,0:T(8,128)(2,1)S(1)}, u32[]{:S(2)}, u32[]{:S(2)}) collective-permute-start(bf16[128,512]{1,0:T(8,128)(2,1)} %param.9), channel_id=1, source_target_pairs={{0,12},{4,16},{8,20},{12,24},{16,28},{20,32},{24,36},{28,40},{32,4... | collective-permute-start | bytes 393224 | tf_op jit(solution)/shard_map/ppermute | solution.py:14
  18.4 28.7 %collective-permute-start.2 = (bf16[128,512]{1,0:T(8,128)(2,1)}, bf16[128,512]{1,0:T(8,128)(2,1)S(1)}, u32[]{:S(2)}, u32[]{:S(2)}) collective-permute-start(bf16[128,512]{1,0:T(8,128)(2,1)} %param.9), channel_id=1, source_target_pairs={{0,16},{4,20},{8,24},{12,28},{16,32},{20,36},{24,40},{28,44},{32,4... | collective-permute-start | bytes 393224 | tf_op jit(solution)/shard_map/ppermute | solution.py:14
  22.6 9.0 %collective-permute-start = (bf16[32,512]{1,0:T(8,128)(2,1)S(1)}, bf16[32,512]{1,0:T(8,128)(2,1)S(1)}, u32[]{:S(2)}, u32[]{:S(2)}) collective-permute-start(bf16[32,512]{1,0:T(8,128)(2,1)S(1)} %slice.30), channel_id=1, source_target_pairs={{0,4},{4,8},{8,12},{12,16},{16,20},{20,24},{24,28},{28,32},{32,36}... | collective-permute-start | bytes 98312 | tf_op jit(solution)/shard_map/ppermute | solution.py:14
  26.3 9.4 %collective-permute-start.6 = (bf16[128,512]{1,0:T(8,128)(2,1)}, bf16[128,512]{1,0:T(8,128)(2,1)S(1)}, u32[]{:S(2)}, u32[]{:S(2)}) collective-permute-start(bf16[128,512]{1,0:T(8,128)(2,1)} %param.10), channel_id=1, source_target_pairs={{0,16},{4,20},{8,24},{12,28},{16,32},{20,36},{24,40},{28,44},{32,4... | collective-permute-start | bytes 393224 | tf_op jit(solution)/shard_map/ppermute | solution.py:14
  31.6 6.6 %collective-permute-start.7 = (bf16[128,512]{1,0:T(8,128)(2,1)}, bf16[128,512]{1,0:T(8,128)(2,1)S(1)}, u32[]{:S(2)}, u32[]{:S(2)}) collective-permute-start(bf16[128,512]{1,0:T(8,128)(2,1)} %param.10), channel_id=1, source_target_pairs={{0,12},{4,16},{8,20},{12,24},{16,28},{20,32},{24,36},{28,40},{32,4... | collective-permute-start | bytes 393224 | tf_op jit(solution)/shard_map/ppermute | solution.py:14
  35.7 5.9 %collective-permute-start.8 = (bf16[128,512]{1,0:T(8,128)(2,1)}, bf16[128,512]{1,0:T(8,128)(2,1)S(1)}, u32[]{:S(2)}, u32[]{:S(2)}) collective-permute-start(bf16[128,512]{1,0:T(8,128)(2,1)} %param.10), channel_id=1, source_target_pairs={{0,8},{4,12},{8,16},{12,20},{16,24},{20,28},{24,32},{28,36},{32,40... | collective-permute-start | bytes 393224 | tf_op jit(solution)/shard_map/ppermute | solution.py:14
  38.2 7.9 %collective-permute-start.9 = (bf16[128,512]{1,0:T(8,128)(2,1)}, bf16[128,512]{1,0:T(8,128)(2,1)S(1)}, u32[]{:S(2)}, u32[]{:S(2)}) collective-permute-start(bf16[128,512]{1,0:T(8,128)(2,1)} %param.10), channel_id=1, source_target_pairs={{0,4},{4,8},{8,12},{12,16},{16,20},{20,24},{24,28},{28,32},{32,36}... | collective-permute-start | bytes 393224 | tf_op jit(solution)/shard_map/ppermute | solution.py:14
  41.5 6.8 %collective-permute-start.5 = (bf16[128,512]{1,0:T(8,128)(2,1)}, bf16[128,512]{1,0:T(8,128)(2,1)S(1)}, u32[]{:S(2)}, u32[]{:S(2)}) collective-permute-start(bf16[128,512]{1,0:T(8,128)(2,1)} %param.9), channel_id=1, source_target_pairs={{0,4},{4,8},{8,12},{12,16},{16,20},{20,24},{24,28},{28,32},{32,36}... | collective-permute-start | bytes 393224 | tf_op jit(solution)/shard_map/ppermute | solution.py:14
  49.3 4.0 %copy-start.1 = (bf16[640,512]{1,0:T(8,128)(2,1)}, bf16[640,512]{1,0:T(8,128)(2,1)S(1)}, u32[]{:S(2)}) copy-start(bf16[640,512]{1,0:T(8,128)(2,1)S(1)} %get-tuple-element.269) | copy-start | bytes 1966084 | tf_op jit(solution)/shard_map/while
  49.3 4.8 %copy-start.3 = (bf16[640,512]{1,0:T(8,128)(2,1)}, bf16[640,512]{1,0:T(8,128)(2,1)S(1)}, u32[]{:S(2)}) copy-start(bf16[640,512]{1,0:T(8,128)(2,1)S(1)} %get-tuple-element.268) | copy-start | bytes 1966084 | tf_op jit(solution)/shard_map/while
  54.8 6.8 %copy-start = (bf16[5152,128]{1,0:T(8,128)(2,1)}, bf16[5152,128]{1,0:T(8,128)(2,1)S(1)}, u32[]{:S(2)}) copy-start(bf16[5152,128]{1,0:T(8,128)(2,1)S(1)} %reshape.49) | copy-start | bytes 3956740 | tf_op jit(solution)/shard_map/while
  61.5 4.2 %slice-start = ((bf16[5152,128]{1,0:T(8,128)(2,1)}), bf16[5120,128]{1,0:T(8,128)(2,1)S(1)}, s32[]{:S(2)}) async-start(bf16[5152,128]{1,0:T(8,128)(2,1)} %copy-done), calls=%async_computation.2 | async-start | bytes 2621440 | tf_op jit(solution)/shard_map/while/body/eval_jaxpr/slice | solution.py:24
  61.5 4.2 %copy-start.2 = (bf16[640,512]{1,0:T(8,128)(2,1)S(1)}, bf16[640,512]{1,0:T(8,128)(2,1)}, u32[]{:S(2)}) copy-start(bf16[640,512]{1,0:T(8,128)(2,1)} %copy-done.1) | copy-start | bytes 1966084 | tf_op jit(solution)/shard_map/while
  65.7 4.6 %copy-start.4 = (bf16[640,512]{1,0:T(8,128)(2,1)S(1)}, bf16[640,512]{1,0:T(8,128)(2,1)}, u32[]{:S(2)}) copy-start(bf16[640,512]{1,0:T(8,128)(2,1)} %copy-done.3) | copy-start | bytes 1966084 | tf_op jit(solution)/shard_map/while
  70.4 4.0 %copy-start.1 = (bf16[640,512]{1,0:T(8,128)(2,1)}, bf16[640,512]{1,0:T(8,128)(2,1)S(1)}, u32[]{:S(2)}) copy-start(bf16[640,512]{1,0:T(8,128)(2,1)S(1)} %get-tuple-element.269) | copy-start | bytes 1966084 | tf_op jit(solution)/shard_map/while
  70.4 4.8 %copy-start.3 = (bf16[640,512]{1,0:T(8,128)(2,1)}, bf16[640,512]{1,0:T(8,128)(2,1)S(1)}, u32[]{:S(2)}) copy-start(bf16[640,512]{1,0:T(8,128)(2,1)S(1)} %get-tuple-element.268) | copy-start | bytes 1966084 | tf_op jit(solution)/shard_map/while
  75.8 6.8 %copy-start = (bf16[5152,128]{1,0:T(8,128)(2,1)}, bf16[5152,128]{1,0:T(8,128)(2,1)S(1)}, u32[]{:S(2)}) copy-start(bf16[5152,128]{1,0:T(8,128)(2,1)S(1)} %reshape.49) | copy-start | bytes 3956740 | tf_op jit(solution)/shard_map/while
  82.6 4.2 %slice-start = ((bf16[5152,128]{1,0:T(8,128)(2,1)}), bf16[5120,128]{1,0:T(8,128)(2,1)S(1)}, s32[]{:S(2)}) async-start(bf16[5152,128]{1,0:T(8,128)(2,1)} %copy-done), calls=%async_computation.2 | async-start | bytes 2621440 | tf_op jit(solution)/shard_map/while/body/eval_jaxpr/slice | solution.py:24
  82.6 4.2 %copy-start.2 = (bf16[640,512]{1,0:T(8,128)(2,1)S(1)}, bf16[640,512]{1,0:T(8,128)(2,1)}, u32[]{:S(2)}) copy-start(bf16[640,512]{1,0:T(8,128)(2,1)} %copy-done.1) | copy-start | bytes 1966084 | tf_op jit(solution)/shard_map/while
  86.8 4.6 %copy-start.4 = (bf16[640,512]{1,0:T(8,128)(2,1)S(1)}, bf16[640,512]{1,0:T(8,128)(2,1)}, u32[]{:S(2)}) copy-start(bf16[640,512]{1,0:T(8,128)(2,1)} %copy-done.3) | copy-start | bytes 1966084 | tf_op jit(solution)/shard_map/while
  91.4 4.0 %copy-start.1 = (bf16[640,512]{1,0:T(8,128)(2,1)}, bf16[640,512]{1,0:T(8,128)(2,1)S(1)}, u32[]{:S(2)}) copy-start(bf16[640,512]{1,0:T(8,128)(2,1)S(1)} %get-tuple-element.269) | copy-start | bytes 1966084 | tf_op jit(solution)/shard_map/while
  91.4 4.8 %copy-start.3 = (bf16[640,512]{1,0:T(8,128)(2,1)}, bf16[640,512]{1,0:T(8,128)(2,1)S(1)}, u32[]{:S(2)}) copy-start(bf16[640,512]{1,0:T(8,128)(2,1)S(1)} %get-tuple-element.268) | copy-start | bytes 1966084 | tf_op jit(solution)/shard_map/while
  96.9 6.8 %copy-start = (bf16[5152,128]{1,0:T(8,128)(2,1)}, bf16[5152,128]{1,0:T(8,128)(2,1)S(1)}, u32[]{:S(2)}) copy-start(bf16[5152,128]{1,0:T(8,128)(2,1)S(1)} %reshape.49) | copy-start | bytes 3956740 | tf_op jit(solution)/shard_map/while
  103.7 4.2 %slice-start = ((bf16[5152,128]{1,0:T(8,128)(2,1)}), bf16[5120,128]{1,0:T(8,128)(2,1)S(1)}, s32[]{:S(2)}) async-start(bf16[5152,128]{1,0:T(8,128)(2,1)} %copy-done), calls=%async_computation.2 | async-start | bytes 2621440 | tf_op jit(solution)/shard_map/while/body/eval_jaxpr/slice | solution.py:24
  103.7 4.2 %copy-start.2 = (bf16[640,512]{1,0:T(8,128)(2,1)S(1)}, bf16[640,512]{1,0:T(8,128)(2,1)}, u32[]{:S(2)}) copy-start(bf16[640,512]{1,0:T(8,128)(2,1)} %copy-done.1) | copy-start | bytes 1966084 | tf_op jit(solution)/shard_map/while
  107.9 4.6 %copy-start.4 = (bf16[640,512]{1,0:T(8,128)(2,1)S(1)}, bf16[640,512]{1,0:T(8,128)(2,1)}, u32[]{:S(2)}) copy-start(bf16[640,512]{1,0:T(8,128)(2,1)} %copy-done.3) | copy-start | bytes 1966084 | tf_op jit(solution)/shard_map/while
  112.5 4.0 %copy-start.1 = (bf16[640,512]{1,0:T(8,128)(2,1)}, bf16[640,512]{1,0:T(8,128)(2,1)S(1)}, u32[]{:S(2)}) copy-start(bf16[640,512]{1,0:T(8,128)(2,1)S(1)} %get-tuple-element.269) | copy-start | bytes 1966084 | tf_op jit(solution)/shard_map/while
  112.5 4.8 %copy-start.3 = (bf16[640,512]{1,0:T(8,128)(2,1)}, bf16[640,512]{1,0:T(8,128)(2,1)S(1)}, u32[]{:S(2)}) copy-start(bf16[640,512]{1,0:T(8,128)(2,1)S(1)} %get-tuple-element.268) | copy-start | bytes 1966084 | tf_op jit(solution)/shard_map/while
  118.0 6.8 %copy-start = (bf16[5152,128]{1,0:T(8,128)(2,1)}, bf16[5152,128]{1,0:T(8,128)(2,1)S(1)}, u32[]{:S(2)}) copy-start(bf16[5152,128]{1,0:T(8,128)(2,1)S(1)} %reshape.49) | copy-start | bytes 3956740 | tf_op jit(solution)/shard_map/while
  124.8 4.2 %slice-start = ((bf16[5152,128]{1,0:T(8,128)(2,1)}), bf16[5120,128]{1,0:T(8,128)(2,1)S(1)}, s32[]{:S(2)}) async-start(bf16[5152,128]{1,0:T(8,128)(2,1)} %copy-done), calls=%async_computation.2 | async-start | bytes 2621440 | tf_op jit(solution)/shard_map/while/body/eval_jaxpr/slice | solution.py:24
  124.8 4.2 %copy-start.2 = (bf16[640,512]{1,0:T(8,128)(2,1)S(1)}, bf16[640,512]{1,0:T(8,128)(2,1)}, u32[]{:S(2)}) copy-start(bf16[640,512]{1,0:T(8,128)(2,1)} %copy-done.1) | copy-start | bytes 1966084 | tf_op jit(solution)/shard_map/while
  128.9 4.6 %copy-start.4 = (bf16[640,512]{1,0:T(8,128)(2,1)S(1)}, bf16[640,512]{1,0:T(8,128)(2,1)}, u32[]{:S(2)}) copy-start(bf16[640,512]{1,0:T(8,128)(2,1)} %copy-done.3) | copy-start | bytes 1966084 | tf_op jit(solution)/shard_map/while
  133.6 4.0 %copy-start.1 = (bf16[640,512]{1,0:T(8,128)(2,1)}, bf16[640,512]{1,0:T(8,128)(2,1)S(1)}, u32[]{:S(2)}) copy-start(bf16[640,512]{1,0:T(8,128)(2,1)S(1)} %get-tuple-element.269) | copy-start | bytes 1966084 | tf_op jit(solution)/shard_map/while
  133.6 4.8 %copy-start.3 = (bf16[640,512]{1,0:T(8,128)(2,1)}, bf16[640,512]{1,0:T(8,128)(2,1)S(1)}, u32[]{:S(2)}) copy-start(bf16[640,512]{1,0:T(8,128)(2,1)S(1)} %get-tuple-element.268) | copy-start | bytes 1966084 | tf_op jit(solution)/shard_map/while
  139.0 6.8 %copy-start = (bf16[5152,128]{1,0:T(8,128)(2,1)}, bf16[5152,128]{1,0:T(8,128)(2,1)S(1)}, u32[]{:S(2)}) copy-start(bf16[5152,128]{1,0:T(8,128)(2,1)S(1)} %reshape.49) | copy-start | bytes 3956740 | tf_op jit(solution)/shard_map/while
  145.8 4.2 %slice-start = ((bf16[5152,128]{1,0:T(8,128)(2,1)}), bf16[5120,128]{1,0:T(8,128)(2,1)S(1)}, s32[]{:S(2)}) async-start(bf16[5152,128]{1,0:T(8,128)(2,1)} %copy-done), calls=%async_computation.2 | async-start | bytes 2621440 | tf_op jit(solution)/shard_map/while/body/eval_jaxpr/slice | solution.py:24
  145.8 4.2 %copy-start.2 = (bf16[640,512]{1,0:T(8,128)(2,1)S(1)}, bf16[640,512]{1,0:T(8,128)(2,1)}, u32[]{:S(2)}) copy-start(bf16[640,512]{1,0:T(8,128)(2,1)} %copy-done.1) | copy-start | bytes 1966084 | tf_op jit(solution)/shard_map/while
  150.0 4.6 %copy-start.4 = (bf16[640,512]{1,0:T(8,128)(2,1)S(1)}, bf16[640,512]{1,0:T(8,128)(2,1)}, u32[]{:S(2)}) copy-start(bf16[640,512]{1,0:T(8,128)(2,1)} %copy-done.3) | copy-start | bytes 1966084 | tf_op jit(solution)/shard_map/while
  154.6 4.0 %copy-start.1 = (bf16[640,512]{1,0:T(8,128)(2,1)}, bf16[640,512]{1,0:T(8,128)(2,1)S(1)}, u32[]{:S(2)}) copy-start(bf16[640,512]{1,0:T(8,128)(2,1)S(1)} %get-tuple-element.269) | copy-start | bytes 1966084 | tf_op jit(solution)/shard_map/while
  154.7 4.8 %copy-start.3 = (bf16[640,512]{1,0:T(8,128)(2,1)}, bf16[640,512]{1,0:T(8,128)(2,1)S(1)}, u32[]{:S(2)}) copy-start(bf16[640,512]{1,0:T(8,128)(2,1)S(1)} %get-tuple-element.268) | copy-start | bytes 1966084 | tf_op jit(solution)/shard_map/while
  160.1 6.8 %copy-start = (bf16[5152,128]{1,0:T(8,128)(2,1)}, bf16[5152,128]{1,0:T(8,128)(2,1)S(1)}, u32[]{:S(2)}) copy-start(bf16[5152,128]{1,0:T(8,128)(2,1)S(1)} %reshape.49) | copy-start | bytes 3956740 | tf_op jit(solution)/shard_map/while
  166.9 4.2 %slice-start = ((bf16[5152,128]{1,0:T(8,128)(2,1)}), bf16[5120,128]{1,0:T(8,128)(2,1)S(1)}, s32[]{:S(2)}) async-start(bf16[5152,128]{1,0:T(8,128)(2,1)} %copy-done), calls=%async_computation.2 | async-start | bytes 2621440 | tf_op jit(solution)/shard_map/while/body/eval_jaxpr/slice | solution.py:24
  166.9 4.2 %copy-start.2 = (bf16[640,512]{1,0:T(8,128)(2,1)S(1)}, bf16[640,512]{1,0:T(8,128)(2,1)}, u32[]{:S(2)}) copy-start(bf16[640,512]{1,0:T(8,128)(2,1)} %copy-done.1) | copy-start | bytes 1966084 | tf_op jit(solution)/shard_map/while
  171.1 4.6 %copy-start.4 = (bf16[640,512]{1,0:T(8,128)(2,1)S(1)}, bf16[640,512]{1,0:T(8,128)(2,1)}, u32[]{:S(2)}) copy-start(bf16[640,512]{1,0:T(8,128)(2,1)} %copy-done.3) | copy-start | bytes 1966084 | tf_op jit(solution)/shard_map/while
  175.7 4.0 %copy-start.1 = (bf16[640,512]{1,0:T(8,128)(2,1)}, bf16[640,512]{1,0:T(8,128)(2,1)S(1)}, u32[]{:S(2)}) copy-start(bf16[640,512]{1,0:T(8,128)(2,1)S(1)} %get-tuple-element.269) | copy-start | bytes 1966084 | tf_op jit(solution)/shard_map/while
  175.7 4.8 %copy-start.3 = (bf16[640,512]{1,0:T(8,128)(2,1)}, bf16[640,512]{1,0:T(8,128)(2,1)S(1)}, u32[]{:S(2)}) copy-start(bf16[640,512]{1,0:T(8,128)(2,1)S(1)} %get-tuple-element.268) | copy-start | bytes 1966084 | tf_op jit(solution)/shard_map/while
  181.2 6.8 %copy-start = (bf16[5152,128]{1,0:T(8,128)(2,1)}, bf16[5152,128]{1,0:T(8,128)(2,1)S(1)}, u32[]{:S(2)}) copy-start(bf16[5152,128]{1,0:T(8,128)(2,1)S(1)} %reshape.49) | copy-start | bytes 3956740 | tf_op jit(solution)/shard_map/while
  188.0 4.2 %slice-start = ((bf16[5152,128]{1,0:T(8,128)(2,1)}), bf16[5120,128]{1,0:T(8,128)(2,1)S(1)}, s32[]{:S(2)}) async-start(bf16[5152,128]{1,0:T(8,128)(2,1)} %copy-done), calls=%async_computation.2 | async-start | bytes 2621440 | tf_op jit(solution)/shard_map/while/body/eval_jaxpr/slice | solution.py:24
  188.0 4.2 %copy-start.2 = (bf16[640,512]{1,0:T(8,128)(2,1)S(1)}, bf16[640,512]{1,0:T(8,128)(2,1)}, u32[]{:S(2)}) copy-start(bf16[640,512]{1,0:T(8,128)(2,1)} %copy-done.1) | copy-start | bytes 1966084 | tf_op jit(solution)/shard_map/while
  192.2 4.6 %copy-start.4 = (bf16[640,512]{1,0:T(8,128)(2,1)S(1)}, bf16[640,512]{1,0:T(8,128)(2,1)}, u32[]{:S(2)}) copy-start(bf16[640,512]{1,0:T(8,128)(2,1)} %copy-done.3) | copy-start | bytes 1966084 | tf_op jit(solution)/shard_map/while
  196.8 4.0 %copy-start.1 = (bf16[640,512]{1,0:T(8,128)(2,1)}, bf16[640,512]{1,0:T(8,128)(2,1)S(1)}, u32[]{:S(2)}) copy-start(bf16[640,512]{1,0:T(8,128)(2,1)S(1)} %get-tuple-element.269) | copy-start | bytes 1966084 | tf_op jit(solution)/shard_map/while
  196.8 4.8 %copy-start.3 = (bf16[640,512]{1,0:T(8,128)(2,1)}, bf16[640,512]{1,0:T(8,128)(2,1)S(1)}, u32[]{:S(2)}) copy-start(bf16[640,512]{1,0:T(8,128)(2,1)S(1)} %get-tuple-element.268) | copy-start | bytes 1966084 | tf_op jit(solution)/shard_map/while
  202.3 6.8 %copy-start = (bf16[5152,128]{1,0:T(8,128)(2,1)}, bf16[5152,128]{1,0:T(8,128)(2,1)S(1)}, u32[]{:S(2)}) copy-start(bf16[5152,128]{1,0:T(8,128)(2,1)S(1)} %reshape.49) | copy-start | bytes 3956740 | tf_op jit(solution)/shard_map/while
  209.1 4.2 %slice-start = ((bf16[5152,128]{1,0:T(8,128)(2,1)}), bf16[5120,128]{1,0:T(8,128)(2,1)S(1)}, s32[]{:S(2)}) async-start(bf16[5152,128]{1,0:T(8,128)(2,1)} %copy-done), calls=%async_computation.2 | async-start | bytes 2621440 | tf_op jit(solution)/shard_map/while/body/eval_jaxpr/slice | solution.py:24
  209.1 4.2 %copy-start.2 = (bf16[640,512]{1,0:T(8,128)(2,1)S(1)}, bf16[640,512]{1,0:T(8,128)(2,1)}, u32[]{:S(2)}) copy-start(bf16[640,512]{1,0:T(8,128)(2,1)} %copy-done.1) | copy-start | bytes 1966084 | tf_op jit(solution)/shard_map/while
  213.2 4.6 %copy-start.4 = (bf16[640,512]{1,0:T(8,128)(2,1)S(1)}, bf16[640,512]{1,0:T(8,128)(2,1)}, u32[]{:S(2)}) copy-start(bf16[640,512]{1,0:T(8,128)(2,1)} %copy-done.3) | copy-start | bytes 1966084 | tf_op jit(solution)/shard_map/while
Sparse Core Ops, SparseCore 0:
  223.7 42.4 reduce-scatter.1
where the time goes:
time: 276 us; the launch traced here: 273 us
  matrix products  72.2 us (26%)
  waiting for transfers between devices  44.4 us (16%)
  other arithmetic  41.2 us (15%)
  local copies, waits for them, and re-layouts  39 us (14%)
  starting transfers between devices  35.5 us (13%)
  loops' own time  27.2 us (10%)
  between operations  13.6 us (5%)
    reduce_scatter x1, waiting for transfers between devices, local(): lax.psum_scatter(lax.dot_general(out_weight, attended, (((0,), (1,)), (()...  42.6 us
    dot_general x8, matrix products, window_attend(): jnp.einsum('wij,jd->wid', weights, outer_values, preferred_element_type=j...  35.7 us
    ppermute x10, starting transfers between devices, from_behind(): return lax.ppermute(shard, axis, pairs)  35.5 us
    reduce_sum x8, other arithmetic, window_attend(): row_total = jnp.sum(expon, axis=(0, 2), keepdims=True)  33 us
    dot_general x8, matrix products, window_attend(): jnp.einsum('wid,jd->wij', blended, outer_keys, preferred_element_type=jnp...  30.8 us
    another operation x1, loops' own time, local(): heads_out = lax.map(per_head, jnp.arange(head_count, dtype=jnp.int32))  27.2 us
    reshape x16, local copies, waits for them, and re-layouts, lag_windows(): jnp.broadcast_to(padded[None], (span, length, feature_count))  14.1 us
    slice x24, local copies, waits for them, and re-layouts, lag_windows(): tiled[:span * (length - 1)].reshape(span, length - 1, feature_count)  11.2 us
  transfers between devices with their start and end apart: 11, of which 3 were waited for; matrix products, arithmetic and copies ran while one was open for 1% of the time, Pallas kernels for 0%

commit v1 on v0

v1 whole, which is shorter than its diff:
```python
import math

import jax
import jax.numpy as jnp
from jax import lax
from jax.experimental import pallas as pl
from jax.experimental.pallas import tpu as pltpu
from jax.sharding import PartitionSpec as P

HS = 128
W1 = 512
W2 = 32
R = 128
L = 8
M = L * R
NCH = W2 // L
KEYS = W1 + R
C = math.log2(math.e) / math.sqrt(HS)
BIG = 1e30
F32 = jnp.float32
BF16 = jnp.bfloat16


def attn_body(
    sh_ref, q_ref, ko, vo, kx0, vx0, kp2, vp2, kx2, vx2, kp4, vp4, kx4, vx4,
    k2o, v2o, k2t, v2t, o_ref,
    ks, vs, k2f, v2f, pen, a0, a1, s0, s1, p0, p1, r0, r1, m_ref, l_ref, acc,
):
    g = pl.program_id(0)
    sh = sh_ref[0]
    even = lax.rem(sh, 2) == 0
    row = lax.broadcasted_iota(jnp.int32, (R, HS), 0)
    col = lax.broadcasted_iota(jnp.int32, (R, HS), 1)
    up = col > row
    upb = jnp.where(up, 1.0, 0.0).astype(BF16)
    tp = [jnp.where(sh - 4 + t < 0, BIG, 0.0).astype(F32) for t in range(4)]

    @pl.when(g == 0)
    def _():
        base = jnp.where(up, tp[0], 0.0)
        for w in range(W2):
            pen[pl.ds(w * R, R), :] = jnp.where((row < w) & (sh == 0), BIG, base)

    for dst, p4, x4, p2, x2, x0, own in (
        (ks, kp4, kx4, kp2, kx2, kx0, ko),
        (vs, vp4, vx4, vp2, vx2, vx0, vo),
    ):
        dst[0:128, :] = p4[...]
        dst[256:384, :] = p2[...]
        dst[512:640, :] = own[...]

        @pl.when(even)
        def _():
            dst[128:256, :] = x4[...]
            dst[384:512, :] = x2[...]

        @pl.when(jnp.logical_not(even))
        def _():
            dst[128:256, :] = x2[...]
            dst[384:512, :] = x0[...]

    k2f[0:W2, :] = k2t[...].astype(F32)
    k2f[W2:, :] = k2o[...].astype(F32)
    v2f[0:W2, :] = v2t[...].astype(F32)
    v2f[W2:, :] = v2o[...].astype(F32)
    A, S, Pm, Rr = [a0, a1], [s0, s1], [p0, p1], [r0, r1]
    units = [(hh, c) for hh in range(2) for c in range(NCH)]

    def qk(u):
        hh, c = units[u]
        a, s = A[u % 2], S[u % 2]
        qf = q_ref[:, hh * HS : (hh + 1) * HS].astype(F32)
        for x in range(L):
            w = c * L + x
            a[x * R : (x + 1) * R, :] = (qf * k2f[W2 - w : W2 - w + R, :]).astype(BF16)
        s[...] = lax.dot_general(
            a[...], ks[...], (((1,), (1,)), ((), ())), preferred_element_type=F32
        )

    def soft(u):
        hh, c = units[u]
        s, p = S[u % 2], Pm[u % 2]
        mt = [None] * 4
        for x in range(L):
            w = c * L + x
            rs = slice(x * R, (x + 1) * R)
            sm = jnp.where(up, s[rs, 0:128], s[rs, 512:640]) - pen[w * R : (w + 1) * R, :]
            s[rs, 0:128] = sm
            mt[0] = sm if x == 0 else jnp.maximum(mt[0], sm)
            for t in range(1, 4):
                b = s[rs, t * 128 : (t + 1) * 128]
                mt[t] = b if x == 0 else jnp.maximum(mt[t], b)
        mx = mt[0]
        for t in range(1, 4):
            mx = jnp.maximum(mx, mt[t] - tp[t])
        mrow = jnp.max(mx, axis=1, keepdims=True)
        if c == 0:
            mnew, al = jnp.broadcast_to(mrow, (R, HS)), None
        else:
            mold = m_ref[...]
            mnew = jnp.maximum(mold, mrow)
            al = jnp.exp2((mold - mnew) * C)
        m_ref[...] = mnew
        mc = mnew * C
        ls = None
        for x in range(L):
            rs = slice(x * R, (x + 1) * R)
            for t in range(4):
                sub = mc if t == 0 else mc + tp[t]
                e = jnp.exp2(s[rs, t * 128 : (t + 1) * 128] * C - sub)
                ls = e if ls is None else ls + e
                eb = e.astype(BF16)
                if t == 0:
                    e0 = eb * upb
                    p[rs, 0:128] = e0
                    p[rs, 512:640] = eb - e0
                else:
                    p[rs, t * 128 : (t + 1) * 128] = eb
        l_ref[...] = ls if c == 0 else l_ref[...] * al + ls
        return al

    def pv(u, al):
        hh, c = units[u]
        p, r = Pm[u % 2], Rr[u % 2]
        r[...] = lax.dot_general(
            p[...], vs[...], (((1,), (0,)), ((), ())), preferred_element_type=F32
        )
        o = None
        for x in range(L):
            w = c * L + x
            t = v2f[W2 - w : W2 - w + R, :] * r[x * R : (x + 1) * R, :]
            o = t if o is None else o + t
        if c > 0:
            o = acc[...] * al + o
        if c < NCH - 1:
            acc[...] = o
        else:
            total = jnp.sum(l_ref[...], axis=1, keepdims=True)
            o_ref[:, hh * HS : (hh + 1) * HS] = (o / total).astype(BF16)

    qk(0)
    for u in range(len(units)):
        if u + 1 < len(units):
            qk(u + 1)
        pv(u, soft(u))


def attend(shard, q, kv, x0, p2, x2, p4, x4, k2, v2, tail):
    groups = kv.shape[1] // HS
    kblock = pl.BlockSpec((R, HS), lambda g: (0, g))
    vblock = pl.BlockSpec((R, HS), lambda g: (1, g))
    pairs = []
    for piece in (kv, x0, p2, x2, p4, x4):
        pairs += [piece, piece]
    return pl.pallas_call(
        attn_body,
        out_shape=jax.ShapeDtypeStruct(q.shape, BF16),
        grid=(groups,),
        in_specs=[
            pl.BlockSpec(memory_space=pltpu.SMEM),
            pl.BlockSpec((R, 2 * HS), lambda g: (0, g)),
        ]
        + [kblock, vblock] * 6
        + [
            kblock,
            kblock,
            pl.BlockSpec((W2, HS), lambda g: (0, g)),
            pl.BlockSpec((W2, HS), lambda g: (1, g)),
        ],
        out_specs=pl.BlockSpec((R, 2 * HS), lambda g: (0, g)),
        scratch_shapes=[pltpu.VMEM((KEYS, HS), BF16)] * 2
        + [pltpu.VMEM((W2 + R, HS), F32)] * 2
        + [pltpu.VMEM((W2 * R, HS), F32)]
        + [pltpu.VMEM((M, HS), BF16)] * 2
        + [pltpu.VMEM((M, KEYS), F32)] * 2
        + [pltpu.VMEM((M, KEYS), BF16)] * 2
        + [pltpu.VMEM((M, HS), F32)] * 2
        + [pltpu.VMEM((R, HS), F32)] * 3,
        compiler_params=pltpu.CompilerParams(vmem_limit_bytes=24 * 2**20),
        cost_estimate=pl.CostEstimate(
            flops=4 * W2 * R * KEYS * HS * 2 * groups,
            bytes_accessed=3 * 2**20,
            transcendentals=W2 * R * W1 * 2 * groups,
        ),
        name="attn",
    )(shard, q, *pairs, k2, v2, tail, tail)


def proj_body(i_ref, a_ref, w_ref, o_ref):
    o_ref[...] = lax.dot_general(
        a_ref[...], w_ref[...], (((1,), (0,)), ((), ())), preferred_element_type=F32
    ).astype(BF16)


def project(block, attended, weight):
    rows, depth = attended.shape
    width = weight.shape[1] // 4
    tile = 256
    return pl.pallas_call(
        proj_body,
        out_shape=jax.ShapeDtypeStruct((rows, width), BF16),
        grid_spec=pltpu.PrefetchScalarGridSpec(
            num_scalar_prefetch=1,
            grid=(width // tile,),
            in_specs=[
                pl.BlockSpec((rows, depth), lambda j, i: (0, 0)),
                pl.BlockSpec((depth, tile), lambda j, i: (0, i[0] * (width // tile) + j)),
            ],
            out_specs=pl.BlockSpec((rows, tile), lambda j, i: (0, j)),
        ),
        cost_estimate=pl.CostEstimate(
            flops=2 * rows * depth * width, bytes_accessed=2 * depth * width, transcendentals=0
        ),
        name="proj",
    )(block, attended, weight)


def local(queries, first_key_rows, first_value_rows, second_key_rows, second_value_rows, out_weight):
    seq = lax.axis_size("seq")
    shard = lax.axis_index("seq").astype(jnp.int32).reshape(1)
    me = lax.axis_index("head").astype(jnp.int32)

    def behind(x, by):
        return lax.ppermute(x, "seq", [(i, (i + by) % seq) for i in range(seq)])

    def swap(x):
        return lax.ppermute(x, "seq", [(i, i ^ 1) for i in range(seq)])

    kv = jnp.concatenate([first_key_rows, first_value_rows], axis=0)
    tail = jnp.concatenate([second_key_rows[R - W2 :], second_value_rows[R - W2 :]], axis=0)
    p2 = behind(kv, 2)
    p4 = behind(kv, 4)
    t1 = behind(tail, 1)
    x0 = swap(kv)
    x2 = swap(p2)
    x4 = swap(p4)
    attended = attend(
        shard, queries, kv, x0, p2, x2, p4, x4, second_key_rows, second_value_rows, t1
    )
    got = []
    for d in (2, 1, 3):
        piece = project(lax.rem(me + d, 4).reshape(1), attended, out_weight)
        got.append(lax.ppermute(piece, "head", [(i, (i + d) % 4) for i in range(4)]))
    total = project(me.reshape(1), attended, out_weight).astype(F32)
    for piece in got:
        total = total + piece.astype(F32)
    return total.astype(BF16)


def solution(mesh):
    in_specs = (P("seq", "head"),) * 5 + (P("head", None),)
    return jax.shard_map(
        local, mesh=mesh, in_specs=in_specs, out_specs=P("seq", "head"), check_vma=False
    )
```

time: 276 us -> 101 us (0.37)
  matrix products: 72.2 us -> 0 us
  Pallas kernels: 0 us -> 50 us
  other arithmetic: 41.2 us -> 1.83 us
  local copies, waits for them, and re-layouts: 39 us -> 6.8 us
  waiting for transfers between devices: 44.4 us -> 16.6 us
  loops' own time: 27.2 us -> 0 us
  between operations: 13.6 us -> 0.05 us
  starting transfers between devices: 35.5 us -> 24.9 us
    dot_general x17 -> x0, matrix products: 72.2 us -> none  [the longest x8 35.7 us: window_attend(): jnp.einsum('wij,jd->wid', weights, outer_values, preferred_element_type=j...]
    pallas_call x0 -> x5, Pallas kernels: none -> 50 us  [the longest x1 34.3 us: attend(): pl.pallas_call(attn_body, out_shape=jax.ShapeDtypeStruct(q.shape, BF16),...]
    reduce_scatter x1 -> x0, waiting for transfers between devices: 42.6 us -> none  [local(): lax.psum_scatter(lax.dot_general(out_weight, attended, (((0,), (1,)), (()...]
    reduce_sum x8 -> x0, other arithmetic: 33 us -> none  [window_attend(): row_total = jnp.sum(expon, axis=(0, 2), keepdims=True)]
    another operation x1 -> x0, loops' own time: 27.2 us -> none  [local(): heads_out = lax.map(per_head, jnp.arange(head_count, dtype=jnp.int32))]
    ppermute x10 -> x9, waiting for transfers between devices: 1.74 us -> 16.6 us  [the longest x3 9.5 us: behind(): return lax.ppermute(x, 'seq', [(i, (i + by) % seq) for i in range(seq)])]
    reshape x16 -> x0, local copies, waits for them, and re-layouts: 14.1 us -> none  [lag_windows(): jnp.broadcast_to(padded[None], (span, length, feature_count))]
    slice x26 -> x2, local copies, waits for them, and re-layouts: 12.8 us -> 1.52 us  [the longest x1 0.76 us: local(): second_key_rows[R - W2:]]
  transfers between devices with their start and end apart: 11 -> 9, of which waited for: 3 -> 4; matrix products, arithmetic and copies ran while one was open for 1% -> 2% of each run, Pallas kernels for 0% -> 12%
where the time goes in v1:
time: 101 us; the launch traced here: 100 us
  Pallas kernels  50 us (50%)
  starting transfers between devices  24.9 us (25%)
  waiting for transfers between devices  16.6 us (16%)
  local copies, waits for them, and re-layouts  6.8 us (7%)
  other arithmetic  1.83 us (2%)
    pallas_call x1, Pallas kernels, attend(): pl.pallas_call(attn_body, out_shape=jax.ShapeDtypeStruct(q.shape, BF16),...  34.3 us
    pallas_call x4, Pallas kernels, project(): pl.pallas_call(proj_body, out_shape=jax.ShapeDtypeStruct((rows, width), B...  15.7 us
    ppermute x3, starting transfers between devices, local(): lax.ppermute(piece, 'head', [(i, (i + d) % 4) for i in range(4)])  10.6 us
    ppermute x3, waiting for transfers between devices, behind(): return lax.ppermute(x, 'seq', [(i, (i + by) % seq) for i in range(seq)])  9.5 us
    ppermute x3, starting transfers between devices, swap(): return lax.ppermute(x, 'seq', [(i, i ^ 1) for i in range(seq)])  7.33 us
    ppermute x3, waiting for transfers between devices, local(): lax.ppermute(piece, 'head', [(i, (i + d) % 4) for i in range(4)])  7.09 us
    ppermute x3, starting transfers between devices, behind(): return lax.ppermute(x, 'seq', [(i, (i + by) % seq) for i in range(seq)])  7.04 us
    unnamed x9, local copies, waits for them, and re-layouts  4.36 us
  transfers between devices with their start and end apart: 9, of which 4 were waited for; matrix products, arithmetic and copies ran while one was open for 2% of the time, Pallas kernels for 12%

profile of v1, /device:TPU:1, one launch (start us, length us, event | category | flops | bytes accessed | tf_op | source)
XLA Modules:
  0.0 100.3 jit_solution(12968252872849751558)
XLA Ops:
  0.0 0.9 constant_dynamic-update-slice_fusion.1
  0.9 0.9 constant_dynamic-update-slice_fusion.ko.vo
  1.8 2.1 %collective-permute-start.1 = (bf16[256,512]{1,0:T(8,128)(2,1)S(1)}, bf16[256,512]{1,0:T(8,128)(2,1)S(1)}, u32[]{:S(2)}, u32[]{:S(2)}) collective-permute-start(bf16[256,512]{1,0:T(8,128)(2,1)S(1)} %constant_dynamic-update-slice_fusion.ko.vo), channel_id=1, source_target_pairs={{0,8},{4,12},{8,16},{12,20},{16,24},{20,28},{24,32},{28,36},{32,40... | collective-permute-start | bytes 786440 | tf_op jit(solution)/shard_map/ppermute | solution.py:224
  3.9 2.5 %collective-permute-start.3 = (bf16[256,512]{1,0:T(8,128)(2,1)S(1)}, bf16[256,512]{1,0:T(8,128)(2,1)S(1)}, u32[]{:S(2)}, u32[]{:S(2)}) collective-permute-start(bf16[256,512]{1,0:T(8,128)(2,1)S(1)} %constant_dynamic-update-slice_fusion.ko.vo), channel_id=1, source_target_pairs={{0,16},{4,20},{8,24},{12,28},{16,32},{20,36},{24,40},{28,44},{32,4... | collective-permute-start | bytes 786440 | tf_op jit(solution)/shard_map/ppermute | solution.py:224
  6.4 1.2 %collective-permute-start = (bf16[256,512]{1,0:T(8,128)(2,1)S(1)}, bf16[256,512]{1,0:T(8,128)(2,1)S(1)}, u32[]{:S(2)}, u32[]{:S(2)}) collective-permute-start(bf16[256,512]{1,0:T(8,128)(2,1)S(1)} %constant_dynamic-update-slice_fusion.ko.vo), channel_id=1, source_target_pairs={{0,4},{4,0},{8,12},{12,8},{16,20},{20,16},{24,28},{28,24},{32,36},... | collective-permute-start | bytes 786440 | tf_op jit(solution)/shard_map/ppermute | solution.py:227
  7.6 8.2 %collective-permute-done.1.kp2.vp2 = bf16[256,512]{1,0:T(8,128)(2,1)S(1)} collective-permute-done((bf16[256,512]{1,0:T(8,128)(2,1)S(1)}, bf16[256,512]{1,0:T(8,128)(2,1)S(1)}, u32[]{:S(2)}, u32[]{:S(2)}) %collective-permute-start.1) | collective-permute-done | bytes 262176 | tf_op jit(solution)/shard_map/ppermute | solution.py:224
  15.8 5.7 %collective-permute-start.2 = (bf16[256,512]{1,0:T(8,128)(2,1)S(1)}, bf16[256,512]{1,0:T(8,128)(2,1)S(1)}, u32[]{:S(2)}, u32[]{:S(2)}) collective-permute-start(bf16[256,512]{1,0:T(8,128)(2,1)S(1)} %collective-permute-done.1.kp2.vp2), channel_id=1, source_target_pairs={{0,4},{4,0},{8,12},{12,8},{16,20},{20,16},{24,28},{28,24},{32,36},... | collective-permute-start | bytes 786440 | tf_op jit(solution)/shard_map/ppermute | solution.py:227
  21.5 0.0 collective-permute-done.3.kp4.vp4
  21.5 0.4 collective-permute-start.4
  21.9 0.8 slice.6
  22.7 0.8 slice.7
  23.4 2.5 %collective-permute-start.5 = (bf16[64,512]{1,0:T(8,128)(2,1)S(1)}, bf16[64,512]{1,0:T(8,128)(2,1)S(1)}, u32[]{:S(2)}, u32[]{:S(2)}) collective-permute-start(bf16[64,512]{1,0:T(8,128)(2,1)S(1)} %pad_maximum_fusion), channel_id=1, source_target_pairs={{0,4},{4,8},{8,12},{12,16},{16,20},{20,24},{24,28},{28,32},{32,36}... | collective-permute-start | bytes 196616 | tf_op jit(solution)/shard_map/ppermute | solution.py:224
  25.9 1.3 %collective-permute-done.5.k2t.v2t = bf16[64,512]{1,0:T(8,128)(2,1)S(1)} collective-permute-done((bf16[64,512]{1,0:T(8,128)(2,1)S(1)}, bf16[64,512]{1,0:T(8,128)(2,1)S(1)}, u32[]{:S(2)}, u32[]{:S(2)}) %collective-permute-start.5) | collective-permute-done | bytes 65568 | tf_op jit(solution)/shard_map/ppermute | solution.py:224
  27.2 0.0 collective-permute-done.kx0.vx0
  27.2 0.0 collective-permute-done.2.kx2.vx2
  27.2 0.0 collective-permute-done.4.kx4.vx4
  27.2 0.0 copy-start.1
  27.3 0.9 copy-done.1
  28.2 0.0 copy-start.2
  28.2 0.9 copy-done.2
  29.1 0.0 copy-start.3
  29.1 0.9 copy-done.3
  30.0 34.3 %attn.1.a_ref = bf16[128,1024]{1,0:T(8,128)(2,1)S(1)} custom-call(s32[1]{0:T(128)} %bitcast.1.sh_ref, bf16[128,1024]{1,0:T(8,128)(2,1)S(1)} %copy-done.3, bf16[256,512]{1,0:T(8,128)(2,1)S(1)} %constant_dynamic-update-slice_fusion.ko.vo, bf16[256,512]{1,0:T(8,128)(2,1)S(1)} %constant_dynamic-update-slice_fusion.ko.vo, ...), custom_call_target="tpu_custom_call" | custom-call | flops 10737418240 | bytes 3145728 | tf_op jit(solution)/shard_map/attn/pallas_call | solution.py:155
  64.3 0.0 copy-start
  64.3 0.7 copy-done
  65.0 4.0 %proj.5 = bf16[128,1024]{1,0:T(8,128)(2,1)} custom-call(s32[1]{0:T(128)} %bitcast.2.i_ref, bf16[128,1024]{1,0:T(8,128)(2,1)} %copy-done, bf16[1024,4096]{1,0:T(8,128)(2,1)} %w_ref.7), custom_call_target="tpu_custom_call" | custom-call | flops 268435456 | bytes 2097152 | tf_op jit(solution)/shard_map/proj/pallas_call | solution.py:199
  69.0 7.0 %collective-permute-start.6 = (bf16[128,1024]{1,0:T(8,128)(2,1)}, bf16[128,1024]{1,0:T(8,128)(2,1)S(1)}, u32[]{:S(2)}, u32[]{:S(2)}) collective-permute-start(bf16[128,1024]{1,0:T(8,128)(2,1)} %proj.5), channel_id=1, source_target_pairs={{0,2},{1,3},{2,0},{3,1},{4,6},{5,7},{6,4},{7,5},{8,10},{9,11},{10,... | collective-permute-start | bytes 786440 | tf_op jit(solution)/shard_map/ppermute | solution.py:243
  76.0 3.9 %proj.6 = bf16[128,1024]{1,0:T(8,128)(2,1)} custom-call(s32[1]{0:T(128)} %bitcast.3.i_ref, bf16[128,1024]{1,0:T(8,128)(2,1)} %copy-done, bf16[1024,4096]{1,0:T(8,128)(2,1)} %w_ref.7), custom_call_target="tpu_custom_call" | custom-call | flops 268435456 | bytes 2097152 | tf_op jit(solution)/shard_map/proj/pallas_call | solution.py:199
  79.9 1.2 %collective-permute-start.7 = (bf16[128,1024]{1,0:T(8,128)(2,1)}, bf16[128,1024]{1,0:T(8,128)(2,1)S(1)}, u32[]{:S(2)}, u32[]{:S(2)}) collective-permute-start(bf16[128,1024]{1,0:T(8,128)(2,1)} %proj.6), channel_id=1, source_target_pairs={{0,1},{1,2},{2,3},{3,0},{4,5},{5,6},{6,7},{7,4},{8,9},{9,10},{10,1... | collective-permute-start | bytes 786440 | tf_op jit(solution)/shard_map/ppermute | solution.py:243
  81.1 3.9 %proj.7 = bf16[128,1024]{1,0:T(8,128)(2,1)} custom-call(s32[1]{0:T(128)} %bitcast.4.i_ref, bf16[128,1024]{1,0:T(8,128)(2,1)} %copy-done, bf16[1024,4096]{1,0:T(8,128)(2,1)} %w_ref.7), custom_call_target="tpu_custom_call" | custom-call | flops 268435456 | bytes 2097152 | tf_op jit(solution)/shard_map/proj/pallas_call | solution.py:199
  85.0 2.4 %collective-permute-start.8 = (bf16[128,1024]{1,0:T(8,128)(2,1)}, bf16[128,1024]{1,0:T(8,128)(2,1)S(1)}, u32[]{:S(2)}, u32[]{:S(2)}) collective-permute-start(bf16[128,1024]{1,0:T(8,128)(2,1)} %proj.7), channel_id=1, source_target_pairs={{0,3},{1,0},{2,1},{3,2},{4,7},{5,4},{6,5},{7,6},{8,11},{9,8},{10,9... | collective-permute-start | bytes 786440 | tf_op jit(solution)/shard_map/ppermute | solution.py:243
  87.4 3.9 %proj.4 = bf16[128,1024]{1,0:T(8,128)(2,1)} custom-call(s32[1]{0:T(128)} %bitcast.i_ref, bf16[128,1024]{1,0:T(8,128)(2,1)} %copy-done, bf16[1024,4096]{1,0:T(8,128)(2,1)} %w_ref.7), custom_call_target="tpu_custom_call" | custom-call | flops 268435456 | bytes 2097152 | tf_op jit(solution)/shard_map/proj/pallas_call | solution.py:199
  91.3 0.0 collective-permute-done.6
  91.4 2.0 %collective-permute-done.7 = bf16[128,1024]{1,0:T(8,128)(2,1)S(1)} collective-permute-done((bf16[128,1024]{1,0:T(8,128)(2,1)}, bf16[128,1024]{1,0:T(8,128)(2,1)S(1)}, u32[]{:S(2)}, u32[]{:S(2)}) %collective-permute-start.7) | collective-permute-done | bytes 262176 | tf_op jit(solution)/shard_map/ppermute | solution.py:243
  93.4 5.1 %collective-permute-done.8 = bf16[128,1024]{1,0:T(8,128)(2,1)S(1)} collective-permute-done((bf16[128,1024]{1,0:T(8,128)(2,1)}, bf16[128,1024]{1,0:T(8,128)(2,1)S(1)}, u32[]{:S(2)}, u32[]{:S(2)}) %collective-permute-start.8) | collective-permute-done | bytes 262176 | tf_op jit(solution)/shard_map/ppermute | solution.py:243
  98.4 1.8 %add_convert_fusion = bf16[128,1024]{1,0:T(8,128)(2,1)} fusion(bf16[128,1024]{1,0:T(8,128)(2,1)S(1)} %collective-permute-done.8, bf16[128,1024]{1,0:T(8,128)(2,1)S(1)} %collective-permute-done.7, bf16[128,1024]{1,0:T(8,128)(2,1)S(1)} %collective-permute-done.6, bf16[128,1024]{1,0:T(8,128)(2,1)} %proj.4), kind=kLoop, calls=%fused_computation | loop fusion | flops 1048576 | bytes 1310720 | tf_op jit(solution)/shard_map/convert_element_type | solution.py:247
  (1 shorter events, 0.0 us)
Async XLA Ops:
  1.8 14.0 %collective-permute-start.1 = (bf16[256,512]{1,0:T(8,128)(2,1)S(1)}, bf16[256,512]{1,0:T(8,128)(2,1)S(1)}, u32[]{:S(2)}, u32[]{:S(2)}) collective-permute-start(bf16[256,512]{1,0:T(8,128)(2,1)S(1)} %constant_dynamic-update-slice_fusion.ko.vo), channel_id=1, source_target_pairs={{0,8},{4,12},{8,16},{12,20},{16,24},{20,28},{24,32},{28,36},{32,40... | collective-permute-start | bytes 786440 | tf_op jit(solution)/shard_map/ppermute | solution.py:224
  3.9 17.6 %collective-permute-start.3 = (bf16[256,512]{1,0:T(8,128)(2,1)S(1)}, bf16[256,512]{1,0:T(8,128)(2,1)S(1)}, u32[]{:S(2)}, u32[]{:S(2)}) collective-permute-start(bf16[256,512]{1,0:T(8,128)(2,1)S(1)} %constant_dynamic-update-slice_fusion.ko.vo), channel_id=1, source_target_pairs={{0,16},{4,20},{8,24},{12,28},{16,32},{20,36},{24,40},{28,44},{32,4... | collective-permute-start | bytes 786440 | tf_op jit(solution)/shard_map/ppermute | solution.py:224
  6.4 20.8 %collective-permute-start = (bf16[256,512]{1,0:T(8,128)(2,1)S(1)}, bf16[256,512]{1,0:T(8,128)(2,1)S(1)}, u32[]{:S(2)}, u32[]{:S(2)}) collective-permute-start(bf16[256,512]{1,0:T(8,128)(2,1)S(1)} %constant_dynamic-update-slice_fusion.ko.vo), channel_id=1, source_target_pairs={{0,4},{4,0},{8,12},{12,8},{16,20},{20,16},{24,28},{28,24},{32,36},... | collective-permute-start | bytes 786440 | tf_op jit(solution)/shard_map/ppermute | solution.py:227
  15.8 11.4 %collective-permute-start.2 = (bf16[256,512]{1,0:T(8,128)(2,1)S(1)}, bf16[256,512]{1,0:T(8,128)(2,1)S(1)}, u32[]{:S(2)}, u32[]{:S(2)}) collective-permute-start(bf16[256,512]{1,0:T(8,128)(2,1)S(1)} %collective-permute-done.1.kp2.vp2), channel_id=1, source_target_pairs={{0,4},{4,0},{8,12},{12,8},{16,20},{20,16},{24,28},{28,24},{32,36},... | collective-permute-start | bytes 786440 | tf_op jit(solution)/shard_map/ppermute | solution.py:227
  21.5 5.7 %collective-permute-start.4 = (bf16[256,512]{1,0:T(8,128)(2,1)S(1)}, bf16[256,512]{1,0:T(8,128)(2,1)S(1)}, u32[]{:S(2)}, u32[]{:S(2)}) collective-permute-start(bf16[256,512]{1,0:T(8,128)(2,1)S(1)} %collective-permute-done.3.kp4.vp4), channel_id=1, source_target_pairs={{0,4},{4,0},{8,12},{12,8},{16,20},{20,16},{24,28},{28,24},{32,36},... | collective-permute-start | bytes 786440 | tf_op jit(solution)/shard_map/ppermute | solution.py:227
  23.4 3.8 %collective-permute-start.5 = (bf16[64,512]{1,0:T(8,128)(2,1)S(1)}, bf16[64,512]{1,0:T(8,128)(2,1)S(1)}, u32[]{:S(2)}, u32[]{:S(2)}) collective-permute-start(bf16[64,512]{1,0:T(8,128)(2,1)S(1)} %pad_maximum_fusion), channel_id=1, source_target_pairs={{0,4},{4,8},{8,12},{12,16},{16,20},{20,24},{24,28},{28,32},{32,36}... | collective-permute-start | bytes 196616 | tf_op jit(solution)/shard_map/ppermute | solution.py:224
  27.2 0.9 copy-start.1
  28.2 0.9 copy-start.2
  29.1 0.9 copy-start.3
  64.3 0.7 copy-start
  69.0 22.4 %collective-permute-start.6 = (bf16[128,1024]{1,0:T(8,128)(2,1)}, bf16[128,1024]{1,0:T(8,128)(2,1)S(1)}, u32[]{:S(2)}, u32[]{:S(2)}) collective-permute-start(bf16[128,1024]{1,0:T(8,128)(2,1)} %proj.5), channel_id=1, source_target_pairs={{0,2},{1,3},{2,0},{3,1},{4,6},{5,7},{6,4},{7,5},{8,10},{9,11},{10,... | collective-permute-start | bytes 786440 | tf_op jit(solution)/shard_map/ppermute | solution.py:243
  79.9 13.5 %collective-permute-start.7 = (bf16[128,1024]{1,0:T(8,128)(2,1)}, bf16[128,1024]{1,0:T(8,128)(2,1)S(1)}, u32[]{:S(2)}, u32[]{:S(2)}) collective-permute-start(bf16[128,1024]{1,0:T(8,128)(2,1)} %proj.6), channel_id=1, source_target_pairs={{0,1},{1,2},{2,3},{3,0},{4,5},{5,6},{6,7},{7,4},{8,9},{9,10},{10,1... | collective-permute-start | bytes 786440 | tf_op jit(solution)/shard_map/ppermute | solution.py:243
  85.0 13.4 %collective-permute-start.8 = (bf16[128,1024]{1,0:T(8,128)(2,1)}, bf16[128,1024]{1,0:T(8,128)(2,1)S(1)}, u32[]{:S(2)}, u32[]{:S(2)}) collective-permute-start(bf16[128,1024]{1,0:T(8,128)(2,1)} %proj.7), channel_id=1, source_target_pairs={{0,3},{1,0},{2,1},{3,2},{4,7},{5,4},{6,5},{7,6},{8,11},{9,8},{10,9... | collective-permute-start | bytes 786440 | tf_op jit(solution)/shard_map/ppermute | solution.py:243

commit v2 on v0

v2 whole, which is shorter than its diff:
```python
import math

import jax
import jax.numpy as jnp
from jax import lax
from jax.experimental import pallas as pl
from jax.experimental.pallas import tpu as pltpu
from jax.sharding import PartitionSpec as P

HS = 128
W1 = 512
W2 = 32
R = 128
IB = 32
LANES = W2 * IB
KEYS = W1 + R
NT = 512
KS = LANES // NT
LT = NT // 128
CH = 16
CHAIN = False
C = math.log2(math.e) / math.sqrt(HS)
BIG = 1e30
F32 = jnp.float32
BF16 = jnp.bfloat16
PARAMS = pltpu.CompilerParams(vmem_limit_bytes=60 * 2**20)


def attn_body(blocks, *refs):
    refs = list(refs)
    sh_ref, q_ref, k2o, k2t, v2o, v2t = (refs.pop(0) for _ in range(6))
    pieces = [(refs.pop(0), refs.pop(0)) for _ in range(6)]
    w_hbm = refs.pop(0)
    outs = [refs.pop(0) for _ in range(4)]
    ks, vt, k2f, v2f, w2t, penA, penB, a0, a1, s0, s1, p0, p1, m_ref, att, wbuf, wsem = refs
    g, last = pl.program_id(0), pl.num_programs(0) - 1
    depth = w_hbm.shape[0] // 4

    def fetch(i):
        rows = slice(i * depth, (i + 1) * depth)
        return pltpu.make_async_copy(w_hbm.at[rows, :], wbuf.at[rows, :], wsem.at[i])

    @pl.when(g == 0)
    def _():
        for i in range(4):
            fetch(i).start()

    sh, me = sh_ref[0], sh_ref[1]
    tp = [jnp.where(sh - 4 + t < 0, BIG, 0.0).astype(F32) for t in range(4)]

    def put(tile, piece):
        rows = slice(tile * R, (tile + 1) * R)
        ks[rows, :] = piece[0][...]
        vt[0:HS, rows] = piece[1][...].T

    own, x0, p2, x2, p4, x4 = pieces
    even = lax.rem(sh, 2) == 0
    put(0, p4)
    put(2, p2)

    @pl.when(even)
    def _():
        put(1, x4)
        put(3, x2)

    @pl.when(jnp.logical_not(even))
    def _():
        put(1, x2)
        put(3, x0)

    put(4, own)

    @pl.when(pl.program_id(0) == 0)
    def _():
        vt[HS:, :] = jnp.ones((16, KEYS), BF16)
        r = lax.broadcasted_iota(jnp.int32, (IB, LANES), 0)
        lane = lax.broadcasted_iota(jnp.int32, (IB, LANES), 1)
        ii, w = lax.rem(lane, IB), lax.div(lane, IB)
        penA[...] = jnp.where(r > ii, tp[0], BIG)
        penB[0] = jnp.where((r > ii) | ((sh == 0) & (w > ii)), BIG, 0.0)
        penB[1] = jnp.where(r > ii, BIG, 0.0)

    k2f[0:W2, :] = k2t[...].astype(F32)
    k2f[W2:, :] = k2o[...].astype(F32)
    v2f[0:W2, :] = v2t[...].astype(F32)
    v2f[W2:, :] = v2o[...].astype(F32)
    for x, b in enumerate(blocks):
        for w in range(0, W2, 4):
            at = W2 + IB * b - w
            blk = jnp.concatenate([v2f[at - y : at - y + IB, :] for y in range(4)], 0)
            w2t[x, :, w * IB : (w + 4) * IB] = blk.T

    A, S, Pm = [a0, a1], [s0, s1], [p0, p1]
    units = [(hh, x) for hh in range(2) for x in range(len(blocks))]
    n = W1 + IB

    def pen(b, r, k):
        cols = slice(k * NT, (k + 1) * NT)
        if r < IB:
            return penA[r : r + 8, cols]
        if r >= W1:
            return penB[0 if b == 0 else 1, r - W1 : r - W1 + 8, cols]
        return None

    def qk(u, k):
        hh, b = units[u][0], blocks[units[u][1]]
        a, s, lo = A[u % 2], S[u % 2], IB * b
        qf = q_ref[lo : lo + IB, hh * HS : (hh + 1) * HS].astype(F32)
        cols = slice(k * NT, (k + 1) * NT)
        for w in range(k * NT // IB, (k + 1) * NT // IB):
            at = W2 + lo - w
            a[w * IB : (w + 1) * IB, :] = (qf * k2f[at : at + IB, :]).astype(BF16)
        x = lax.dot_general(
            ks[lo : lo + n, :], a[cols, :], (((1,), (1,)), ((), ())), preferred_element_type=F32
        )
        s[:, cols] = x
        top = {}
        for r in range(0, n, 8):
            y, pe = x[r : r + 8, :], pen(b, r, k)
            key = "m" if pe is not None else (lo + r) // R
            if pe is not None:
                y = y - pe
            top[key] = y if key not in top else jnp.maximum(top[key], y)
        m8 = None
        for key, y in top.items():
            if key != "m" and key != 4:
                y = y - tp[key]
            for t in range(LT):
                z = y[:, t * 128 : (t + 1) * 128]
                m8 = z if m8 is None else jnp.maximum(m8, z)
        return m8

    def qk_all(u):
        m8 = qk(u, 0)
        for k in range(1, KS):
            m8 = jnp.maximum(m8, qk(u, k))
        m1 = jnp.max(m8, axis=0, keepdims=True)
        m1 = jnp.maximum(m1, pltpu.roll(m1, 32, 1))
        m1 = jnp.maximum(m1, pltpu.roll(m1, 64, 1))
        m_ref[u % 2] = jnp.broadcast_to(m1 * C, (8, HS))

    def ex(u, k):
        b = blocks[units[u][1]]
        s, p, lo = S[u % 2], Pm[u % 2], IB * b
        cols = slice(k * NT, (k + 1) * NT)
        mb = jnp.concatenate([m_ref[u % 2]] * LT, axis=1)
        for r in range(0, n, CH):
            es = []
            for r8 in range(r, r + CH, 8):
                pe, t = pen(b, r8, k), (lo + r8) // R
                sub = mb + pe if pe is not None else (mb + tp[t] if t < 4 else mb)
                es.append(jnp.exp2(s[r8 : r8 + 8, cols] * C - sub))
            p[r : r + CH, cols] = jnp.concatenate(es, 0).astype(BF16)

    def pv_all(u):
        hh, x = units[u]
        lo, p = IB * blocks[x], Pm[u % 2]
        o = l = None
        for k in range(KS):
            cols = slice(k * NT, (k + 1) * NT)
            rt = lax.dot_general(
                vt[:, lo : lo + n], p[:, cols], (((1,), (0,)), ((), ())), preferred_element_type=F32
            )
            for t in range(LT):
                part = slice(t * 128, (t + 1) * 128)
                y = rt[0:HS, part] * w2t[x, :, k * NT + t * 128 : k * NT + (t + 1) * 128]
                z = rt[HS : HS + 8, part]
                o, l = (y, z) if o is None else (o + y, l + z)
        l = l[0:1, :]
        l = l + pltpu.roll(l, 32, 1)
        l = l + pltpu.roll(l, 64, 1)
        o = o + pltpu.roll(o, 32, 1)
        o = o + pltpu.roll(o, 64, 1)
        o = (o / l).T
        start = pl.multiple_of((2 * g + hh) * HS, HS)
        att[IB * x : IB * (x + 1), pl.ds(start, HS)] = o[0:IB, :].astype(BF16)

    for t in range(-1, len(units) + 1):

        @pl.when(sh >= 0)
        def _():
            if t + 1 < len(units):
                qk_all(t + 1)
            if 0 <= t < len(units):
                for k in range(KS):
                    ex(t, k)
            if t >= 1:
                pv_all(t - 1)

    @pl.when(g == last)
    def _():
        for i in range(4):
            fetch(i).wait()
        width = outs[0].shape[1]
        for d, out in enumerate(outs):
            start = pl.multiple_of(lax.rem(me + d, 4) * width, width)
            out[...] = lax.dot_general(
                att[...], wbuf[:, pl.ds(start, width)], (((1,), (0,)), ((), ())),
                preferred_element_type=F32,
            ).astype(BF16)


def attend(where, q, k2, v2, tail, pieces, weight):
    groups = k2.shape[1] // HS
    width = weight.shape[1] // 4
    nb = R // IB
    kblock = pl.BlockSpec((R, HS), lambda g: (0, g))
    vblock = pl.BlockSpec((R, HS), lambda g: (1, g))
    args = []
    for piece in pieces:
        args += [piece, piece]
    return pl.pallas_call(
        lambda *refs: attn_body(tuple(range(nb)), *refs),
        out_shape=(jax.ShapeDtypeStruct((R, width), BF16),) * 4,
        grid=(groups,),
        in_specs=[
            pl.BlockSpec(memory_space=pltpu.SMEM),
            pl.BlockSpec((R, 2 * HS), lambda g: (0, g)),
            kblock,
            pl.BlockSpec((W2, HS), lambda g: (0, g)),
            kblock,
            pl.BlockSpec((W2, HS), lambda g: (1, g)),
        ]
        + [kblock, vblock] * len(pieces)
        + [pl.BlockSpec(memory_space=pl.ANY)],
        out_specs=(pl.BlockSpec((R, width), lambda g: (0, 0)),) * 4,
        scratch_shapes=[pltpu.VMEM((KEYS, HS), BF16), pltpu.VMEM((HS + 16, KEYS), BF16)]
        + [pltpu.VMEM((W2 + R, HS), F32)] * 2
        + [pltpu.VMEM((nb, HS, LANES), F32)]
        + [pltpu.VMEM((IB, LANES), F32), pltpu.VMEM((2, IB, LANES), F32)]
        + [pltpu.VMEM((LANES, HS), BF16)] * 2
        + [pltpu.VMEM((W1 + IB, LANES), F32)] * 2
        + [pltpu.VMEM((W1 + IB, LANES), BF16)] * 2
        + [pltpu.VMEM((2, 8, HS), F32), pltpu.VMEM(q.shape, BF16)]
        + [pltpu.VMEM(weight.shape, BF16), pltpu.SemaphoreType.DMA((4,))],
        compiler_params=PARAMS,
        cost_estimate=pl.CostEstimate(
            flops=4 * W2 * R * KEYS * HS * 2 * groups * 4,
            bytes_accessed=12 * 2**20,
            transcendentals=W2 * R * W1 * 2 * groups,
        ),
        name="attn",
    )(where, q, k2, tail, v2, tail, *args, weight)


def pack_body(k_ref, v_ref, k2_ref, v2_ref, kv_ref, t_ref):
    kv_ref[0:R, :] = k_ref[...]
    kv_ref[R:, :] = v_ref[...]
    t_ref[0:W2, :] = k2_ref[...]
    t_ref[W2:, :] = v2_ref[...]


def pack(k, v, k2, v2):
    width, cols = k.shape[1], 2 * HS
    block = pl.BlockSpec((R, cols), lambda i: (0, i))
    last = pl.BlockSpec((W2, cols), lambda i: (R // W2 - 1, i))
    return pl.pallas_call(
        pack_body,
        out_shape=(
            jax.ShapeDtypeStruct((2 * R, width), BF16),
            jax.ShapeDtypeStruct((2 * W2, width), BF16),
        ),
        grid=(width // cols,),
        in_specs=[block, block, last, last],
        out_specs=(
            pl.BlockSpec((2 * R, cols), lambda i: (0, i)),
            pl.BlockSpec((2 * W2, cols), lambda i: (0, i)),
        ),
        compiler_params=PARAMS,
        name="pack",
    )(k, v, k2, v2)


def add_body(*refs):
    x = [r[...].astype(F32) for r in refs[:-1]]
    refs[-1][...] = (x[0] + x[1] + x[2] + x[3]).astype(BF16)


def local(queries, first_key_rows, first_value_rows, second_key_rows, second_value_rows, out_weight):
    seq = lax.axis_size("seq")
    where = jnp.stack([lax.axis_index("seq"), lax.axis_index("head")]).astype(jnp.int32)

    def behind(x, by):
        return lax.ppermute(x, "seq", [(i, (i + by) % seq) for i in range(seq)])

    def swap(x):
        return lax.ppermute(x, "seq", [(i, i ^ 1) for i in range(seq)])

    kv, tail = pack(first_key_rows, first_value_rows, second_key_rows, second_value_rows)
    p2 = behind(kv, 2)
    p4 = behind(p2, 2) if CHAIN else behind(kv, 4)
    x0 = swap(kv)
    t1 = behind(tail, 1)
    x2 = swap(p2)
    x4 = swap(p4)
    pieces = attend(
        where, queries, second_key_rows, second_value_rows, t1, (kv, x0, p2, x2, p4, x4), out_weight
    )
    got = [pieces[0]]
    for d in (2, 1, 3):
        got.append(lax.ppermute(pieces[d], "head", [(i, (i + d) % 4) for i in range(4)]))
    cols = queries.shape[1] // 2
    block = pl.BlockSpec((R, cols), lambda i: (0, i))
    return pl.pallas_call(
        add_body,
        out_shape=jax.ShapeDtypeStruct(queries.shape, BF16),
        grid=(2,),
        in_specs=[block] * 4,
        out_specs=block,
        compiler_params=PARAMS,
        name="add",
    )(*got)


def solution(mesh):
    in_specs = (P("seq", "head"),) * 5 + (P("head", None),)
    return jax.shard_map(
        local, mesh=mesh, in_specs=in_specs, out_specs=P("seq", "head"), check_vma=False
    )
```

time: 276 us -> 92.4 us (0.33); the launches traced: 273 us -> 92.2 us
  matrix products: 72.2 us -> 0 us
  other arithmetic: 41.2 us -> 0.65 us
  local copies, waits for them, and re-layouts: 39 us -> 2.22 us
  Pallas kernels: 0 us -> 36.7 us
  loops' own time: 27.2 us -> 0 us
  starting transfers between devices: 35.5 us -> 20.5 us
  between operations: 13.6 us -> 0.06 us
  waiting for transfers between devices: 44.4 us -> 32.1 us
    dot_general x17 -> x0, matrix products: 72.2 us -> none  [the longest x8 35.7 us: window_attend(): jnp.einsum('wij,jd->wid', weights, outer_values, preferred_element_type=j...]
    reduce_scatter x1 -> x0, waiting for transfers between devices: 42.6 us -> none  [local(): lax.psum_scatter(lax.dot_general(out_weight, attended, (((0,), (1,)), (()...]
    pallas_call x0 -> x3, Pallas kernels: none -> 36.7 us  [the longest x1 33 us: attend(): pl.pallas_call(lambda *refs: attn_body(tuple(range(nb)), *refs), out_shap...]
    reduce_sum x8 -> x0, other arithmetic: 33 us -> none  [window_attend(): row_total = jnp.sum(expon, axis=(0, 2), keepdims=True)]
    ppermute x10 -> x9, waiting for transfers between devices: 1.74 us -> 32.1 us  [the longest x3 20.5 us: local(): lax.ppermute(pieces[d], 'head', [(i, (i + d) % 4) for i in range(4)])]
    another operation x1 -> x0, loops' own time: 27.2 us -> none  [local(): heads_out = lax.map(per_head, jnp.arange(head_count, dtype=jnp.int32))]
    ppermute x10 -> x9, starting transfers between devices: 35.5 us -> 20.5 us  [the longest x3 10.5 us: local(): lax.ppermute(pieces[d], 'head', [(i, (i + d) % 4) for i in range(4)])]
    reshape x16 -> x0, local copies, waits for them, and re-layouts: 14.1 us -> none  [lag_windows(): jnp.broadcast_to(padded[None], (span, length, feature_count))]
  transfers between devices with their start and end apart: 11 -> 9, of which waited for: 3 -> 6; matrix products, arithmetic and copies ran while one was open for 1% -> 1% of each run, Pallas kernels for 0% -> 0%
where the time goes in v2:
time: 92.4 us; the launch traced here: 92.2 us
  Pallas kernels  36.7 us (40%)
  waiting for transfers between devices  32.1 us (35%)
  starting transfers between devices  20.5 us (22%)
  local copies, waits for them, and re-layouts  2.22 us (2%)
    pallas_call x1, Pallas kernels, attend(): pl.pallas_call(lambda *refs: attn_body(tuple(range(nb)), *refs), out_shap...  33 us
    ppermute x3, waiting for transfers between devices, local(): lax.ppermute(pieces[d], 'head', [(i, (i + d) % 4) for i in range(4)])  20.5 us
    ppermute x3, waiting for transfers between devices, behind(): return lax.ppermute(x, 'seq', [(i, (i + by) % seq) for i in range(seq)])  11.6 us
    ppermute x3, starting transfers between devices, local(): lax.ppermute(pieces[d], 'head', [(i, (i + d) % 4) for i in range(4)])  10.5 us
    ppermute x3, starting transfers between devices, swap(): return lax.ppermute(x, 'seq', [(i, i ^ 1) for i in range(seq)])  6.11 us
    ppermute x3, starting transfers between devices, behind(): return lax.ppermute(x, 'seq', [(i, (i + by) % seq) for i in range(seq)])  3.88 us
    unnamed x18, local copies, waits for them, and re-layouts  2.22 us
    pallas_call x1, Pallas kernels, local(): pl.pallas_call(add_body, out_shape=jax.ShapeDtypeStruct(queries.shape, BF...  2.01 us
  transfers between devices with their start and end apart: 9, of which 6 were waited for; matrix products, arithmetic and copies ran while one was open for 1% of the time, Pallas kernels for 0%

profile of v2, /device:TPU:1, one launch (start us, length us, event | category | flops | bytes accessed | tf_op | source)
XLA Modules:
  0.0 92.2 jit_solution(10042433557737927861)
XLA Ops:
  0.0 1.7 %pack.1 = (bf16[256,512]{1,0:T(8,128)(2,1)}, bf16[64,512]{1,0:T(8,128)(2,1)}) custom-call(bf16[128,512]{1,0:T(8,128)(2,1)} %k_ref.1, bf16[128,512]{1,0:T(8,128)(2,1)} %v_ref.1, bf16[128,512]{1,0:T(8,128)(2,1)} %refs_2_.1, bf16[128,512]{1,0:T(8,128)(2,1)} %refs_4_.1), custom_call_target="tpu_custom_call" | custom-call | tf_op jit(solution)/shard_map/pack/pallas_call | solution.py:257
  1.7 3.6 %collective-permute-start.4 = (bf16[256,512]{1,0:T(8,128)(2,1)}, bf16[256,512]{1,0:T(8,128)(2,1)S(1)}, u32[]{:S(2)}, u32[]{:S(2)}) collective-permute-start(bf16[256,512]{1,0:T(8,128)(2,1)} %get-tuple-element.12.refs_6_.refs_7_), channel_id=1, source_target_pairs={{0,16},{4,20},{8,24},{12,28},{16,32},{20,36},{24,40},{28,44},{32,4... | collective-permute-start | bytes 786440 | tf_op jit(solution)/shard_map/ppermute | solution.py:284
  5.2 0.3 collective-permute-start.2
  5.5 1.2 %collective-permute-start.1 = (bf16[256,512]{1,0:T(8,128)(2,1)}, bf16[256,512]{1,0:T(8,128)(2,1)S(1)}, u32[]{:S(2)}, u32[]{:S(2)}) collective-permute-start(bf16[256,512]{1,0:T(8,128)(2,1)} %get-tuple-element.12.refs_6_.refs_7_), channel_id=1, source_target_pairs={{0,4},{4,0},{8,12},{12,8},{16,20},{20,16},{24,28},{28,24},{32,36},... | collective-permute-start | bytes 786440 | tf_op jit(solution)/shard_map/ppermute | solution.py:287
  6.8 7.1 %collective-permute-done.4.refs_14_.refs_15_ = bf16[256,512]{1,0:T(8,128)(2,1)S(1)} collective-permute-done((bf16[256,512]{1,0:T(8,128)(2,1)}, bf16[256,512]{1,0:T(8,128)(2,1)S(1)}, u32[]{:S(2)}, u32[]{:S(2)}) %collective-permute-start.4) | collective-permute-done | bytes 262176 | tf_op jit(solution)/shard_map/ppermute | solution.py:284
  13.9 0.0 copy-start.3
  13.9 3.3 %collective-permute-start.5 = (bf16[256,512]{1,0:T(8,128)(2,1)S(1)}, bf16[256,512]{1,0:T(8,128)(2,1)S(1)}, u32[]{:S(2)}, u32[]{:S(2)}) collective-permute-start(bf16[256,512]{1,0:T(8,128)(2,1)S(1)} %collective-permute-done.4.refs_14_.refs_15_), channel_id=1, source_target_pairs={{0,4},{4,0},{8,12},{12,8},{16,20},{20,16},{24,28},{28,24},{32,36},... | collective-permute-start | bytes 786440 | tf_op jit(solution)/shard_map/ppermute | solution.py:287
  17.2 3.5 %collective-permute-done.2.refs_10_.refs_11_ = bf16[256,512]{1,0:T(8,128)(2,1)S(1)} collective-permute-done((bf16[256,512]{1,0:T(8,128)(2,1)}, bf16[256,512]{1,0:T(8,128)(2,1)S(1)}, u32[]{:S(2)}, u32[]{:S(2)}) %collective-permute-start.2) | collective-permute-done | bytes 262176 | tf_op jit(solution)/shard_map/ppermute | solution.py:284
  20.6 0.0 copy-start.4
  20.6 1.6 %collective-permute-start.3 = (bf16[256,512]{1,0:T(8,128)(2,1)S(1)}, bf16[256,512]{1,0:T(8,128)(2,1)S(1)}, u32[]{:S(2)}, u32[]{:S(2)}) collective-permute-start(bf16[256,512]{1,0:T(8,128)(2,1)S(1)} %collective-permute-done.2.refs_10_.refs_11_), channel_id=1, source_target_pairs={{0,4},{4,0},{8,12},{12,8},{16,20},{20,16},{24,28},{28,24},{32,36},... | collective-permute-start | bytes 786440 | tf_op jit(solution)/shard_map/ppermute | solution.py:287
  22.2 0.0 collective-permute-start
  22.2 0.7 pad_add_fusion.refs_0_
  22.9 1.0 %collective-permute-done.refs_3_.refs_5_ = bf16[64,512]{1,0:T(8,128)(2,1)S(1)} collective-permute-done((bf16[64,512]{1,0:T(8,128)(2,1)}, bf16[64,512]{1,0:T(8,128)(2,1)S(1)}, u32[]{:S(2)}, u32[]{:S(2)}) %collective-permute-start) | collective-permute-done | bytes 65568 | tf_op jit(solution)/shard_map/ppermute | solution.py:284
  23.9 0.0 copy-start.8
  23.9 0.0 collective-permute-done.1.refs_8_.refs_9_
  23.9 0.0 copy-start.5
  23.9 0.0 collective-permute-done.5.refs_16_.refs_17_
  23.9 0.0 copy-start.6
  23.9 0.0 collective-permute-done.3.refs_12_.refs_13_
  23.9 0.0 copy-done.3
  23.9 0.0 copy-done.4
  23.9 0.6 copy-done.8
  24.5 0.1 copy-done.5
  24.6 0.1 copy-done.6
  24.7 0.0 copy-start.7
  24.7 0.7 copy-done.7
  25.4 33.0 %attn.1 = (bf16[128,1024]{1,0:T(8,128)(2,1)}, bf16[128,1024]{1,0:T(8,128)(2,1)}, bf16[128,1024]{1,0:T(8,128)(2,1)}, bf16[128,1024]{1,0:T(8,128)(2,1)}) custom-call(s32[2]{0:T(128)} %pad_add_fusion.refs_0_, bf16[128,1024]{1,0:T(8,128)(2,1)} %refs_1_.1, bf16[128,512]{1,0:T(8,128)(2,1)} %refs_2_.1, bf16[64,512]{1,0:T(8,128)(2,1)} %copy-done.8, ...), custom_call_target="tpu_custom_call" | custom-call | flops 42949672960 | bytes 12582912 | tf_op jit(solution)/shard_map/attn/pallas_call | solution.py:212
  58.4 7.0 %collective-permute-start.6 = (bf16[128,1024]{1,0:T(8,128)(2,1)}, bf16[128,1024]{1,0:T(8,128)(2,1)S(1)}, u32[]{:S(2)}, u32[]{:S(2)}) collective-permute-start(bf16[128,1024]{1,0:T(8,128)(2,1)} %get-tuple-element.14), channel_id=1, source_target_pairs={{0,2},{1,3},{2,0},{3,1},{4,6},{5,7},{6,4},{7,5},{8,10},{9,11},{10,... | collective-permute-start | bytes 786440 | tf_op jit(solution)/shard_map/ppermute | solution.py:301
  65.4 1.2 %collective-permute-start.7 = (bf16[128,1024]{1,0:T(8,128)(2,1)}, bf16[128,1024]{1,0:T(8,128)(2,1)S(1)}, u32[]{:S(2)}, u32[]{:S(2)}) collective-permute-start(bf16[128,1024]{1,0:T(8,128)(2,1)} %get-tuple-element.15), channel_id=1, source_target_pairs={{0,1},{1,2},{2,3},{3,0},{4,5},{5,6},{6,7},{7,4},{8,9},{9,10},{10,1... | collective-permute-start | bytes 786440 | tf_op jit(solution)/shard_map/ppermute | solution.py:301
  66.6 2.4 %collective-permute-start.8 = (bf16[128,1024]{1,0:T(8,128)(2,1)}, bf16[128,1024]{1,0:T(8,128)(2,1)S(1)}, u32[]{:S(2)}, u32[]{:S(2)}) collective-permute-start(bf16[128,1024]{1,0:T(8,128)(2,1)} %get-tuple-element.16), channel_id=1, source_target_pairs={{0,3},{1,0},{2,1},{3,2},{4,7},{5,4},{6,5},{7,6},{8,11},{9,8},{10,9... | collective-permute-start | bytes 786440 | tf_op jit(solution)/shard_map/ppermute | solution.py:301
  69.0 0.6 collective-permute-done.6.refs_1_
  69.6 0.0 copy-start
  69.6 10.8 %collective-permute-done.7.refs_2_ = bf16[128,1024]{1,0:T(8,128)(2,1)S(1)} collective-permute-done((bf16[128,1024]{1,0:T(8,128)(2,1)}, bf16[128,1024]{1,0:T(8,128)(2,1)S(1)}, u32[]{:S(2)}, u32[]{:S(2)}) %collective-permute-start.7) | collective-permute-done | bytes 262176 | tf_op jit(solution)/shard_map/ppermute | solution.py:301
  80.4 0.0 copy-start.1
  80.4 9.1 %collective-permute-done.8.refs_3_ = bf16[128,1024]{1,0:T(8,128)(2,1)S(1)} collective-permute-done((bf16[128,1024]{1,0:T(8,128)(2,1)}, bf16[128,1024]{1,0:T(8,128)(2,1)S(1)}, u32[]{:S(2)}, u32[]{:S(2)}) %collective-permute-start.8) | collective-permute-done | bytes 262176 | tf_op jit(solution)/shard_map/ppermute | solution.py:301
  89.5 0.0 copy-start.2
  89.5 0.0 copy-done
  89.5 0.0 copy-done.1
  89.5 0.7 copy-done.2
  90.2 2.0 %add.3 = bf16[128,1024]{1,0:T(8,128)(2,1)} custom-call(bf16[128,1024]{1,0:T(8,128)(2,1)} %get-tuple-element.13.refs_0_, bf16[128,1024]{1,0:T(8,128)(2,1)} %copy-done, bf16[128,1024]{1,0:T(8,128)(2,1)} %copy-done.1, bf16[128,1024]{1,0:T(8,128)(2,1)} %copy-done.2), custom_call_target="tpu_custom_call" | custom-call | tf_op jit(solution)/shard_map/add/pallas_call | solution.py:304
Async XLA Ops:
  1.7 12.2 %collective-permute-start.4 = (bf16[256,512]{1,0:T(8,128)(2,1)}, bf16[256,512]{1,0:T(8,128)(2,1)S(1)}, u32[]{:S(2)}, u32[]{:S(2)}) collective-permute-start(bf16[256,512]{1,0:T(8,128)(2,1)} %get-tuple-element.12.refs_6_.refs_7_), channel_id=1, source_target_pairs={{0,16},{4,20},{8,24},{12,28},{16,32},{20,36},{24,40},{28,44},{32,4... | collective-permute-start | bytes 786440 | tf_op jit(solution)/shard_map/ppermute | solution.py:284
  5.2 15.4 %collective-permute-start.2 = (bf16[256,512]{1,0:T(8,128)(2,1)}, bf16[256,512]{1,0:T(8,128)(2,1)S(1)}, u32[]{:S(2)}, u32[]{:S(2)}) collective-permute-start(bf16[256,512]{1,0:T(8,128)(2,1)} %get-tuple-element.12.refs_6_.refs_7_), channel_id=1, source_target_pairs={{0,8},{4,12},{8,16},{12,20},{16,24},{20,28},{24,32},{28,36},{32,40... | collective-permute-start | bytes 786440 | tf_op jit(solution)/shard_map/ppermute | solution.py:284
  5.5 18.3 %collective-permute-start.1 = (bf16[256,512]{1,0:T(8,128)(2,1)}, bf16[256,512]{1,0:T(8,128)(2,1)S(1)}, u32[]{:S(2)}, u32[]{:S(2)}) collective-permute-start(bf16[256,512]{1,0:T(8,128)(2,1)} %get-tuple-element.12.refs_6_.refs_7_), channel_id=1, source_target_pairs={{0,4},{4,0},{8,12},{12,8},{16,20},{20,16},{24,28},{28,24},{32,36},... | collective-permute-start | bytes 786440 | tf_op jit(solution)/shard_map/ppermute | solution.py:287
  13.9 10.0 %copy-start.3 = (bf16[256,512]{1,0:T(8,128)(2,1)}, bf16[256,512]{1,0:T(8,128)(2,1)S(1)}, u32[]{:S(2)}) copy-start(bf16[256,512]{1,0:T(8,128)(2,1)S(1)} %collective-permute-done.4.refs_14_.refs_15_) | copy-start | bytes 786436
  13.9 10.0 %collective-permute-start.5 = (bf16[256,512]{1,0:T(8,128)(2,1)S(1)}, bf16[256,512]{1,0:T(8,128)(2,1)S(1)}, u32[]{:S(2)}, u32[]{:S(2)}) collective-permute-start(bf16[256,512]{1,0:T(8,128)(2,1)S(1)} %collective-permute-done.4.refs_14_.refs_15_), channel_id=1, source_target_pairs={{0,4},{4,0},{8,12},{12,8},{16,20},{20,16},{24,28},{28,24},{32,36},... | collective-permute-start | bytes 786440 | tf_op jit(solution)/shard_map/ppermute | solution.py:287
  20.6 3.3 %copy-start.4 = (bf16[256,512]{1,0:T(8,128)(2,1)}, bf16[256,512]{1,0:T(8,128)(2,1)S(1)}, u32[]{:S(2)}) copy-start(bf16[256,512]{1,0:T(8,128)(2,1)S(1)} %collective-permute-done.2.refs_10_.refs_11_) | copy-start | bytes 786436
  20.6 3.2 %collective-permute-start.3 = (bf16[256,512]{1,0:T(8,128)(2,1)S(1)}, bf16[256,512]{1,0:T(8,128)(2,1)S(1)}, u32[]{:S(2)}, u32[]{:S(2)}) collective-permute-start(bf16[256,512]{1,0:T(8,128)(2,1)S(1)} %collective-permute-done.2.refs_10_.refs_11_), channel_id=1, source_target_pairs={{0,4},{4,0},{8,12},{12,8},{16,20},{20,16},{24,28},{28,24},{32,36},... | collective-permute-start | bytes 786440 | tf_op jit(solution)/shard_map/ppermute | solution.py:287
  22.2 1.7 %collective-permute-start = (bf16[64,512]{1,0:T(8,128)(2,1)}, bf16[64,512]{1,0:T(8,128)(2,1)S(1)}, u32[]{:S(2)}, u32[]{:S(2)}) collective-permute-start(bf16[64,512]{1,0:T(8,128)(2,1)} %get-tuple-element.11), channel_id=1, source_target_pairs={{0,4},{4,8},{8,12},{12,16},{16,20},{20,24},{24,28},{28,32},{32,36}... | collective-permute-start | bytes 196616 | tf_op jit(solution)/shard_map/ppermute | solution.py:284
  23.9 0.6 copy-start.8
  23.9 0.7 copy-start.5
  23.9 0.8 copy-start.6
  24.7 0.7 copy-start.7
  58.4 11.1 %collective-permute-start.6 = (bf16[128,1024]{1,0:T(8,128)(2,1)}, bf16[128,1024]{1,0:T(8,128)(2,1)S(1)}, u32[]{:S(2)}, u32[]{:S(2)}) collective-permute-start(bf16[128,1024]{1,0:T(8,128)(2,1)} %get-tuple-element.14), channel_id=1, source_target_pairs={{0,2},{1,3},{2,0},{3,1},{4,6},{5,7},{6,4},{7,5},{8,10},{9,11},{10,... | collective-permute-start | bytes 786440 | tf_op jit(solution)/shard_map/ppermute | solution.py:301
  65.4 15.0 %collective-permute-start.7 = (bf16[128,1024]{1,0:T(8,128)(2,1)}, bf16[128,1024]{1,0:T(8,128)(2,1)S(1)}, u32[]{:S(2)}, u32[]{:S(2)}) collective-permute-start(bf16[128,1024]{1,0:T(8,128)(2,1)} %get-tuple-element.15), channel_id=1, source_target_pairs={{0,1},{1,2},{2,3},{3,0},{4,5},{5,6},{6,7},{7,4},{8,9},{9,10},{10,1... | collective-permute-start | bytes 786440 | tf_op jit(solution)/shard_map/ppermute | solution.py:301
  66.6 22.9 %collective-permute-start.8 = (bf16[128,1024]{1,0:T(8,128)(2,1)}, bf16[128,1024]{1,0:T(8,128)(2,1)S(1)}, u32[]{:S(2)}, u32[]{:S(2)}) collective-permute-start(bf16[128,1024]{1,0:T(8,128)(2,1)} %get-tuple-element.16), channel_id=1, source_target_pairs={{0,3},{1,0},{2,1},{3,2},{4,7},{5,4},{6,5},{7,6},{8,11},{9,8},{10,9... | collective-permute-start | bytes 786440 | tf_op jit(solution)/shard_map/ppermute | solution.py:301
  69.6 19.9 %copy-start = (bf16[128,1024]{1,0:T(8,128)(2,1)}, bf16[128,1024]{1,0:T(8,128)(2,1)S(1)}, u32[]{:S(2)}) copy-start(bf16[128,1024]{1,0:T(8,128)(2,1)S(1)} %collective-permute-done.6.refs_1_) | copy-start | bytes 786436
  80.4 9.1 %copy-start.1 = (bf16[128,1024]{1,0:T(8,128)(2,1)}, bf16[128,1024]{1,0:T(8,128)(2,1)S(1)}, u32[]{:S(2)}) copy-start(bf16[128,1024]{1,0:T(8,128)(2,1)S(1)} %collective-permute-done.7.refs_2_) | copy-start | bytes 786436
  89.5 0.7 copy-start.2

commit v3 on v2

--- a/solution.py
+++ b/solution.py
@@ -6,6 +6,7 @@
 from jax.experimental import pallas as pl
 from jax.experimental.pallas import tpu as pltpu
 from jax.sharding import PartitionSpec as P
+
 
 HS = 128
 W1 = 512
@@ -18,34 +19,42 @@
 KS = LANES // NT
 LT = NT // 128
 CH = 16
-CHAIN = False
 C = math.log2(math.e) / math.sqrt(HS)
 BIG = 1e30
 F32 = jnp.float32
 BF16 = jnp.bfloat16
-PARAMS = pltpu.CompilerParams(vmem_limit_bytes=60 * 2**20)
-
-
-def attn_body(blocks, *refs):
+PARAMS = pltpu.CompilerParams(vmem_limit_bytes=46 * 2**20)
+SMALL = pltpu.CompilerParams(vmem_limit_bytes=8 * 2**20)
+
+
+def attn_body(blocks, final, *refs):
     refs = list(refs)
-    sh_ref, q_ref, k2o, k2t, v2o, v2t = (refs.pop(0) for _ in range(6))
+    sh_ref, me_ref, q_ref, k2o, v2o = (refs.pop(0) for _ in range(5))
+    tails = [(refs.pop(0), refs.pop(0)) for _ in range(2)]
     pieces = [(refs.pop(0), refs.pop(0)) for _ in range(6)]
-    w_hbm = refs.pop(0)
-    outs = [refs.pop(0) for _ in range(4)]
-    ks, vt, k2f, v2f, w2t, penA, penB, a0, a1, s0, s1, p0, p1, m_ref, att, wbuf, wsem = refs
     g, last = pl.program_id(0), pl.num_programs(0) - 1
-    depth = w_hbm.shape[0] // 4
-
-    def fetch(i):
-        rows = slice(i * depth, (i + 1) * depth)
-        return pltpu.make_async_copy(w_hbm.at[rows, :], wbuf.at[rows, :], wsem.at[i])
-
-    @pl.when(g == 0)
-    def _():
-        for i in range(4):
-            fetch(i).start()
-
-    sh, me = sh_ref[0], sh_ref[1]
+    if final:
+        done_ref, w_hbm = refs.pop(0), refs.pop(0)
+        outs = [refs.pop(0) for _ in range(4)]
+        att, wbuf, wsem = refs[-3:]
+        refs = refs[:-3]
+        depth = w_hbm.shape[0] // 4
+
+        def fetch(i):
+            rows = slice(i * depth, (i + 1) * depth)
+            return pltpu.make_async_copy(w_hbm.at[rows, :], wbuf.at[rows, :], wsem.at[i])
+
+        @pl.when(g == 0)
+        def _():
+            for i in range(4):
+                fetch(i).start()
+            att[:, 0 : done_ref.shape[1]] = done_ref[...]
+
+    else:
+        o_ref = refs.pop(0)
+    ks, vt, k2f, v2f, w2t, penA, penB, a0, a1, s0, s1, p0, p1, m_ref = refs
+
+    sh, me = sh_ref[0], me_ref[0]
     tp = [jnp.where(sh - 4 + t < 0, BIG, 0.0).astype(F32) for t in range(4)]
 
     def put(tile, piece):
@@ -62,11 +71,15 @@
     def _():
         put(1, x4)
         put(3, x2)
+        k2f[0:W2, :] = tails[1][0][...].astype(F32)
+        v2f[0:W2, :] = tails[1][1][...].astype(F32)
 
     @pl.when(jnp.logical_not(even))
     def _():
         put(1, x2)
         put(3, x0)
+        k2f[0:W2, :] = tails[0][0][...].astype(F32)
+        v2f[0:W2, :] = tails[0][1][...].astype(F32)
 
     put(4, own)
 
@@ -80,9 +93,7 @@
         penB[0] = jnp.where((r > ii) | ((sh == 0) & (w > ii)), BIG, 0.0)
         penB[1] = jnp.where(r > ii, BIG, 0.0)
 
-    k2f[0:W2, :] = k2t[...].astype(F32)
     k2f[W2:, :] = k2o[...].astype(F32)
-    v2f[0:W2, :] = v2t[...].astype(F32)
     v2f[W2:, :] = v2o[...].astype(F32)
     for x, b in enumerate(blocks):
         for w in range(0, W2, 4):
@@ -172,8 +183,11 @@
         o = o + pltpu.roll(o, 32, 1)
         o = o + pltpu.roll(o, 64, 1)
         o = (o / l).T
-        start = pl.multiple_of((2 * g + hh) * HS, HS)
-        att[IB * x : IB * (x + 1), pl.ds(start, HS)] = o[0:IB, :].astype(BF16)
+        rows, o = slice(IB * x, IB * (x + 1)), o[0:IB, :].astype(BF16)
+        if final:
+            att[rows, pl.ds(pl.multiple_of(done_ref.shape[1] + (2 * g + hh) * HS, HS), HS)] = o
+        else:
+            o_ref[rows, hh * HS : (hh + 1) * HS] = o
 
     for t in range(-1, len(units) + 1):
 
@@ -186,6 +200,9 @@
                     ex(t, k)
             if t >= 1:
                 pv_all(t - 1)
+
+    if not final:
+        return
 
     @pl.when(g == last)
     def _():
@@ -200,73 +217,89 @@
             ).astype(BF16)
 
 
-def attend(where, q, k2, v2, tail, pieces, weight):
-    groups = k2.shape[1] // HS
-    width = weight.shape[1] // 4
+def attend(half, shard, me, q, k2, v2, pieces, done=None, weight=None):
+    final = weight is not None
+    groups = k2.shape[1] // HS // 2
+    g0 = half * groups
     nb = R // IB
     kblock = pl.BlockSpec((R, HS), lambda g: (0, g))
     vblock = pl.BlockSpec((R, HS), lambda g: (1, g))
-    args = []
+    own = pl.BlockSpec((R, HS), lambda g: (0, g0 + g))
+    args = [shard, me, q, k2, v2, pieces[1], pieces[1], pieces[3], pieces[3]]
     for piece in pieces:
         args += [piece, piece]
+    specs = [
+        pl.BlockSpec(memory_space=pltpu.SMEM),
+        pl.BlockSpec(memory_space=pltpu.SMEM),
+        pl.BlockSpec((R, 2 * HS), lambda g: (0, g0 + g)),
+        own,
+        own,
+    ]
+    specs += [
+        pl.BlockSpec((W2, HS), lambda g: (2 * R // W2, g)),
+        pl.BlockSpec((W2, HS), lambda g: (2 * R // W2 + 1, g)),
+    ] * 2
+    specs += [kblock, vblock] * len(pieces)
+    scratch = [pltpu.VMEM((KEYS, HS), BF16), pltpu.VMEM((HS + 16, KEYS), BF16)]
+    scratch += [pltpu.VMEM((W2 + R, HS), F32)] * 2
+    scratch += [pltpu.VMEM((nb, HS, LANES), F32)]
+    scratch += [pltpu.VMEM((IB, LANES), F32), pltpu.VMEM((2, IB, LANES), F32)]
+    scratch += [pltpu.VMEM((LANES, HS), BF16)] * 2
+    scratch += [pltpu.VMEM((W1 + IB, LANES), F32)] * 2
+    scratch += [pltpu.VMEM((W1 + IB, LANES), BF16)] * 2
+    scratch += [pltpu.VMEM((2, 8, HS), F32)]
+    if final:
+        width = weight.shape[1] // 4
+        out_shape = (jax.ShapeDtypeStruct((R, width), BF16),) * 4
+        out_specs = (pl.BlockSpec((R, width), lambda g: (0, 0)),) * 4
+        args += [done, weight]
+        specs += [pl.BlockSpec(done.shape, lambda g: (0, 0)), pl.BlockSpec(memory_space=pl.ANY)]
+        scratch += [pltpu.VMEM(q.shape, BF16), pltpu.VMEM(weight.shape, BF16)]
+        scratch += [pltpu.SemaphoreType.DMA((4,))]
+    else:
+        out_shape = jax.ShapeDtypeStruct((R, 2 * HS * groups), BF16)
+        out_specs = pl.BlockSpec((R, 2 * HS), lambda g: (0, g))
     return pl.pallas_call(
-        lambda *refs: attn_body(tuple(range(nb)), *refs),
-        out_shape=(jax.ShapeDtypeStruct((R, width), BF16),) * 4,
+        lambda *refs: attn_body(tuple(range(nb)), final, *refs),
+        out_shape=out_shape,
         grid=(groups,),
-        in_specs=[
-            pl.BlockSpec(memory_space=pltpu.SMEM),
-            pl.BlockSpec((R, 2 * HS), lambda g: (0, g)),
-            kblock,
-            pl.BlockSpec((W2, HS), lambda g: (0, g)),
-            kblock,
-            pl.BlockSpec((W2, HS), lambda g: (1, g)),
-        ]
-        + [kblock, vblock] * len(pieces)
-        + [pl.BlockSpec(memory_space=pl.ANY)],
-        out_specs=(pl.BlockSpec((R, width), lambda g: (0, 0)),) * 4,
-        scratch_shapes=[pltpu.VMEM((KEYS, HS), BF16), pltpu.VMEM((HS + 16, KEYS), BF16)]
-        + [pltpu.VMEM((W2 + R, HS), F32)] * 2
-        + [pltpu.VMEM((nb, HS, LANES), F32)]
-        + [pltpu.VMEM((IB, LANES), F32), pltpu.VMEM((2, IB, LANES), F32)]
-        + [pltpu.VMEM((LANES, HS), BF16)] * 2
-        + [pltpu.VMEM((W1 + IB, LANES), F32)] * 2
-        + [pltpu.VMEM((W1 + IB, LANES), BF16)] * 2
-        + [pltpu.VMEM((2, 8, HS), F32), pltpu.VMEM(q.shape, BF16)]
-        + [pltpu.VMEM(weight.shape, BF16), pltpu.SemaphoreType.DMA((4,))],
+        in_specs=specs,
+        out_specs=out_specs,
+        scratch_shapes=scratch,
         compiler_params=PARAMS,
         cost_estimate=pl.CostEstimate(
             flops=4 * W2 * R * KEYS * HS * 2 * groups * 4,
             bytes_accessed=12 * 2**20,
             transcendentals=W2 * R * W1 * 2 * groups,
         ),
-        name="attn",
-    )(where, q, k2, tail, v2, tail, *args, weight)
-
-
-def pack_body(k_ref, v_ref, k2_ref, v2_ref, kv_ref, t_ref):
-    kv_ref[0:R, :] = k_ref[...]
-    kv_ref[R:, :] = v_ref[...]
-    t_ref[0:W2, :] = k2_ref[...]
-    t_ref[W2:, :] = v2_ref[...]
+    )(*args)
+
+
+def pack_body(k_ref, v_ref, k2_ref, v2_ref, *outs):
+    cols = outs[0].shape[1]
+    for half in range(2):
+        here = slice(half * cols, (half + 1) * cols)
+        kv_ref, all_ref = outs[2 * half : 2 * half + 2]
+        for ref in (kv_ref, all_ref):
+            ref[0:R, :] = k_ref[:, here]
+            ref[R : 2 * R, :] = v_ref[:, here]
+        all_ref[2 * R : 2 * R + W2, :] = k2_ref[:, here]
+        all_ref[2 * R + W2 :, :] = v2_ref[:, here]
 
 
 def pack(k, v, k2, v2):
-    width, cols = k.shape[1], 2 * HS
-    block = pl.BlockSpec((R, cols), lambda i: (0, i))
-    last = pl.BlockSpec((W2, cols), lambda i: (R // W2 - 1, i))
+    width = k.shape[1]
+    cols = width // 2
+    block = pl.BlockSpec((R, width), lambda i: (0, 0))
+    last = pl.BlockSpec((W2, width), lambda i: (R // W2 - 1, 0))
+    shapes = [(2 * R, cols), (2 * R + 2 * W2, cols)] * 2
     return pl.pallas_call(
         pack_body,
-        out_shape=(
-            jax.ShapeDtypeStruct((2 * R, width), BF16),
-            jax.ShapeDtypeStruct((2 * W2, width), BF16),
-        ),
-        grid=(width // cols,),
+        out_shape=tuple(jax.ShapeDtypeStruct(x, BF16) for x in shapes),
+        grid=(1,),
         in_specs=[block, block, last, last],
-        out_specs=(
-            pl.BlockSpec((2 * R, cols), lambda i: (0, i)),
-            pl.BlockSpec((2 * W2, cols), lambda i: (0, i)),
-        ),
-        compiler_params=PARAMS,
+        out_specs=tuple(pl.BlockSpec(x, lambda i: (0, 0)) for x in shapes),
+        compiler_params=SMALL,
         name="pack",
     )(k, v, k2, v2)
 
@@ -278,7 +311,8 @@
 
 def local(queries, first_key_rows, first_value_rows, second_key_rows, second_value_rows, out_weight):
     seq = lax.axis_size("seq")
-    where = jnp.stack([lax.axis_index("seq"), lax.axis_index("head")]).astype(jnp.int32)
+    shard = lax.axis_index("seq").astype(jnp.int32).reshape(1)
+    me = lax.axis_index("head").astype(jnp.int32).reshape(1)
 
     def behind(x, by):
         return lax.ppermute(x, "seq", [(i, (i + by) % seq) for i in range(seq)])
@@ -286,16 +320,26 @@
     def swap(x):
         return lax.ppermute(x, "seq", [(i, i ^ 1) for i in range(seq)])
 
-    kv, tail = pack(first_key_rows, first_value_rows, second_key_rows, second_value_rows)
-    p2 = behind(kv, 2)
-    p4 = behind(p2, 2) if CHAIN else behind(kv, 4)
-    x0 = swap(kv)
-    t1 = behind(tail, 1)
-    x2 = swap(p2)
-    x4 = swap(p4)
-    pieces = attend(
-        where, queries, second_key_rows, second_value_rows, t1, (kv, x0, p2, x2, p4, x4), out_weight
+    kva, alla, kvb, allb = pack(
+        first_key_rows, first_value_rows, second_key_rows, second_value_rows
     )
+    p2a = behind(alla, 2)
+    p4a = behind(kva, 4)
+    x0a = swap(alla)
+    p2a, p4a, sendb, kvsend = lax.optimization_barrier((p2a, p4a, allb, kvb))
+    x2a = swap(p2a)
+    x4a = swap(p4a)
+    p2b = behind(sendb, 2)
+    p4b = behind(kvsend, 4)
+    x0b = swap(sendb)
+    common = (shard, me) + tuple(
+        pltpu.with_memory_space_constraint(x, pltpu.HBM)
+        for x in (queries, second_key_rows, second_value_rows)
+    )
+    done = attend(0, *common, (kva, x0a, p2a, x2a, p4a, x4a))
+    x2b = swap(p2b)
+    x4b = swap(p4b)
+    pieces = attend(1, *common, (kvb, x0b, p2b, x2b, p4b, x4b), done, out_weight)
     got = [pieces[0]]
     for d in (2, 1, 3):
         got.append(lax.ppermute(pieces[d], "head", [(i, (i + d) % 4) for i in range(4)]))
@@ -307,7 +351,7 @@
         grid=(2,),
         in_specs=[block] * 4,
         out_specs=block,
-        compiler_params=PARAMS,
+        compiler_params=SMALL,
         name="add",
     )(*got)
 

time: 92.4 us -> 96.5 us (1.044)
  waiting for transfers between devices: 32.1 us -> 36 us
  Pallas kernels: 36.7 us -> 34.2 us
  starting transfers between devices: 20.5 us -> 22.5 us
  local copies, waits for them, and re-layouts: 2.22 us -> 3.61 us
    ppermute x3 -> x4, waiting for transfers between devices: 11.6 us -> 15.3 us  [behind(): return lax.ppermute(x, 'seq', [(i, (i + by) % seq) for i in range(seq)])]
    ppermute x3 -> x4, starting transfers between devices: 3.88 us -> 5.75 us  [behind(): return lax.ppermute(x, 'seq', [(i, (i + by) % seq) for i in range(seq)])]
    pallas_call x2 -> x3, Pallas kernels: 34.7 us -> 33.2 us  [the longest x2 33.2 us: attend(): pl.pallas_call(lambda *refs: attn_body(tuple(range(nb)), final, *refs), o...]
    unnamed x18 -> x8, local copies, waits for them, and re-layouts: 2.22 us -> 3.61 us
    pallas_call x1, Pallas kernels: 2.01 us -> 0.91 us  [local(): pl.pallas_call(add_body, out_shape=jax.ShapeDtypeStruct(queries.shape, BF...]
    ppermute x3 -> x6, starting transfers between devices: 6.11 us -> 6.85 us  [swap(): return lax.ppermute(x, 'seq', [(i, i ^ 1) for i in range(seq)])]
  transfers between devices with their start and end apart: 9 -> 13, of which waited for: 6 -> 5; matrix products, arithmetic and copies ran while one was open for 1% -> 0% of each run, Pallas kernels for 0% -> 16%
where the time goes in v3:
time: 96.5 us; the launch traced here: 96.3 us
  waiting for transfers between devices  36 us (37%)
  Pallas kernels  34.2 us (35%)
  starting transfers between devices  22.5 us (23%)
  local copies, waits for them, and re-layouts  3.61 us (4%)
    pallas_call x2, Pallas kernels, attend(): pl.pallas_call(lambda *refs: attn_body(tuple(range(nb)), final, *refs), o...  33.2 us
    ppermute x3, waiting for transfers between devices, local(): lax.ppermute(pieces[d], 'head', [(i, (i + d) % 4) for i in range(4)])  20.6 us
    ppermute x4, waiting for transfers between devices, behind(): return lax.ppermute(x, 'seq', [(i, (i + by) % seq) for i in range(seq)])  15.3 us
    ppermute x3, starting transfers between devices, local(): lax.ppermute(pieces[d], 'head', [(i, (i + d) % 4) for i in range(4)])  9.9 us
    ppermute x6, starting transfers between devices, swap(): return lax.ppermute(x, 'seq', [(i, i ^ 1) for i in range(seq)])  6.85 us
    ppermute x4, starting transfers between devices, behind(): return lax.ppermute(x, 'seq', [(i, (i + by) % seq) for i in range(seq)])  5.75 us
    unnamed x8, local copies, waits for them, and re-layouts  3.61 us
  transfers between devices with their start and end apart: 13, of which 5 were waited for; matrix products, arithmetic and copies ran while one was open for 0% of the time, Pallas kernels for 16%

profile of v3, /device:TPU:1, one launch (start us, length us, event | category | flops | bytes accessed | tf_op | source)
XLA Modules:
  0.0 96.3 jit_solution(7846327615483382980)
XLA Ops:
  0.0 0.0 copy-start
  0.0 0.9 copy-done
  0.9 0.0 copy-start.1
  0.9 0.9 copy-done.1
  1.8 0.0 copy-start.2
  1.8 0.9 copy-done.2
  2.7 0.0 copy-start.3
  2.7 0.9 copy-done.3
  3.7 2.1 %collective-permute-start = (bf16[320,256]{1,0:T(8,128)(2,1)S(1)}, bf16[320,256]{1,0:T(8,128)(2,1)S(1)}, u32[]{:S(2)}, u32[]{:S(2)}) collective-permute-start(bf16[320,256]{1,0:T(8,128)(2,1)S(1)} %get-tuple-element.17), channel_id=1, source_target_pairs={{0,8},{4,12},{8,16},{12,20},{16,24},{20,28},{24,32},{28,36},{32,40... | collective-permute-start | bytes 491528 | tf_op jit(solution)/shard_map/ppermute | solution.py:318
  5.8 2.5 %collective-permute-start.1 = (bf16[256,256]{1,0:T(8,128)(2,1)S(1)}, bf16[256,256]{1,0:T(8,128)(2,1)S(1)}, u32[]{:S(2)}, u32[]{:S(2)}) collective-permute-start(bf16[256,256]{1,0:T(8,128)(2,1)S(1)} %get-tuple-element.18.refs_9_.refs_10_), channel_id=1, source_target_pairs={{0,16},{4,20},{8,24},{12,28},{16,32},{20,36},{24,40},{28,44},{32,4... | collective-permute-start | bytes 393224 | tf_op jit(solution)/shard_map/ppermute | solution.py:318
  8.2 1.2 %collective-permute-start.7 = (bf16[320,256]{1,0:T(8,128)(2,1)S(1)}, bf16[320,256]{1,0:T(8,128)(2,1)S(1)}, u32[]{:S(2)}, u32[]{:S(2)}) collective-permute-start(bf16[320,256]{1,0:T(8,128)(2,1)S(1)} %get-tuple-element.17), channel_id=1, source_target_pairs={{0,4},{4,0},{8,12},{12,8},{16,20},{20,16},{24,28},{28,24},{32,36},... | collective-permute-start | bytes 491528 | tf_op jit(solution)/shard_map/ppermute | solution.py:321
  9.5 5.8 %collective-permute-done.1.refs_17_.refs_18_ = bf16[256,256]{1,0:T(8,128)(2,1)S(1)} collective-permute-done((bf16[256,256]{1,0:T(8,128)(2,1)S(1)}, bf16[256,256]{1,0:T(8,128)(2,1)S(1)}, u32[]{:S(2)}, u32[]{:S(2)}) %collective-permute-start.1) | collective-permute-done | bytes 131104 | tf_op jit(solution)/shard_map/ppermute | solution.py:318
  15.3 0.0 collective-permute-done.refs_13_.refs_14_
  15.3 1.2 %collective-permute-start.3 = (bf16[320,256]{1,0:T(8,128)(2,1)S(1)}, bf16[320,256]{1,0:T(8,128)(2,1)S(1)}, u32[]{:S(2)}, u32[]{:S(2)}) collective-permute-start(bf16[320,256]{1,0:T(8,128)(2,1)S(1)} %get-tuple-element.21), channel_id=1, source_target_pairs={{0,8},{4,12},{8,16},{12,20},{16,24},{20,28},{24,32},{28,36},{32,40... | collective-permute-start | bytes 491528 | tf_op jit(solution)/shard_map/ppermute | solution.py:318
  16.5 3.9 %collective-permute-start.8 = (bf16[320,256]{1,0:T(8,128)(2,1)S(1)}, bf16[320,256]{1,0:T(8,128)(2,1)S(1)}, u32[]{:S(2)}, u32[]{:S(2)}) collective-permute-start(bf16[320,256]{1,0:T(8,128)(2,1)S(1)} %collective-permute-done.refs_13_.refs_14_), channel_id=1, source_target_pairs={{0,4},{4,0},{8,12},{12,8},{16,20},{20,16},{24,28},{28,24},{32,36},... | collective-permute-start | bytes 491528 | tf_op jit(solution)/shard_map/ppermute | solution.py:321
  20.4 0.0 collective-permute-start.5
  20.4 0.0 collective-permute-start.9
  20.4 0.0 collective-permute-done.7.refs_5_.refs_6_.refs_11_.refs_12_
  20.4 0.5 collective-permute-start.2
  20.9 9.5 %collective-permute-done.5.refs_17_.refs_18_ = bf16[256,256]{1,0:T(8,128)(2,1)S(1)} collective-permute-done((bf16[256,256]{1,0:T(8,128)(2,1)S(1)}, bf16[256,256]{1,0:T(8,128)(2,1)S(1)}, u32[]{:S(2)}, u32[]{:S(2)}) %collective-permute-start.5) | collective-permute-done | bytes 131104 | tf_op jit(solution)/shard_map/ppermute | solution.py:318
  30.4 1.2 %collective-permute-start.6 = (bf16[256,256]{1,0:T(8,128)(2,1)S(1)}, bf16[256,256]{1,0:T(8,128)(2,1)S(1)}, u32[]{:S(2)}, u32[]{:S(2)}) collective-permute-start(bf16[256,256]{1,0:T(8,128)(2,1)S(1)} %collective-permute-done.5.refs_17_.refs_18_), channel_id=1, source_target_pairs={{0,4},{4,0},{8,12},{12,8},{16,20},{20,16},{24,28},{28,24},{32,36},... | collective-permute-start | bytes 393224 | tf_op jit(solution)/shard_map/ppermute | solution.py:321
  31.6 0.0 collective-permute-done.3.refs_13_.refs_14_
  31.6 0.0 collective-permute-start.4
  31.6 0.0 collective-permute-done.9.refs_19_.refs_20_
  31.6 0.0 collective-permute-done.8.refs_7_.refs_8_.refs_15_.refs_16_
  31.6 15.8 %shard_map.64.refs_21_ = bf16[128,512]{1,0:T(8,128)(2,1)S(1)} custom-call(s32[1]{0:T(128)} %bitcast.refs_0_, s32[1]{0:T(128)} %bitcast.1.refs_1_, bf16[128,1024]{1,0:T(8,128)(2,1)} %refs_2_.3, bf16[128,512]{1,0:T(8,128)(2,1)} %refs_3_.3, bf16[128,512]{1,0:T(8,128)(2,1)} %refs_4_.3, ...), custom_call_target="tpu_custom_call" | custom-call | flops 21474836480 | bytes 12582912 | tf_op jit(solution)/shard_map/pallas_call | solution.py:262
  47.4 0.0 collective-permute-done.2.refs_5_.refs_6_.refs_11_.refs_12_
  47.5 0.0 collective-permute-done.6.refs_19_.refs_20_
  47.5 0.0 collective-permute-done.4.refs_7_.refs_8_.refs_15_.refs_16_
  47.5 17.4 %shard_map.65 = (bf16[128,1024]{1,0:T(8,128)(2,1)S(1)}, bf16[128,1024]{1,0:T(8,128)(2,1)S(1)}, bf16[128,1024]{1,0:T(8,128)(2,1)S(1)}, bf16[128,1024]{1,0:T(8,128)(2,1)S(1)}) custom-call(s32[1]{0:T(128)} %bitcast.refs_0_, s32[1]{0:T(128)} %bitcast.1.refs_1_, bf16[128,1024]{1,0:T(8,128)(2,1)} %refs_2_.3, bf16[128,512]{1,0:T(8,128)(2,1)} %refs_3_.3, ...), custom_call_target="tpu_custom_call" | custom-call | flops 21474836480 | bytes 12582912 | tf_op jit(solution)/shard_map/pallas_call | solution.py:262
  64.9 6.3 %collective-permute-start.10 = (bf16[128,1024]{1,0:T(8,128)(2,1)S(1)}, bf16[128,1024]{1,0:T(8,128)(2,1)S(1)}, u32[]{:S(2)}, u32[]{:S(2)}) collective-permute-start(bf16[128,1024]{1,0:T(8,128)(2,1)S(1)} %get-tuple-element.26), channel_id=1, source_target_pairs={{0,2},{1,3},{2,0},{3,1},{4,6},{5,7},{6,4},{7,5},{8,10},{9,11},{10,... | collective-permute-start | bytes 786440 | tf_op jit(solution)/shard_map/ppermute | solution.py:345
  71.2 1.2 %collective-permute-start.11 = (bf16[128,1024]{1,0:T(8,128)(2,1)S(1)}, bf16[128,1024]{1,0:T(8,128)(2,1)S(1)}, u32[]{:S(2)}, u32[]{:S(2)}) collective-permute-start(bf16[128,1024]{1,0:T(8,128)(2,1)S(1)} %get-tuple-element.27), channel_id=1, source_target_pairs={{0,1},{1,2},{2,3},{3,0},{4,5},{5,6},{6,7},{7,4},{8,9},{9,10},{10,1... | collective-permute-start | bytes 786440 | tf_op jit(solution)/shard_map/ppermute | solution.py:345
  72.4 2.4 %collective-permute-start.12 = (bf16[128,1024]{1,0:T(8,128)(2,1)S(1)}, bf16[128,1024]{1,0:T(8,128)(2,1)S(1)}, u32[]{:S(2)}, u32[]{:S(2)}) collective-permute-start(bf16[128,1024]{1,0:T(8,128)(2,1)S(1)} %get-tuple-element.28), channel_id=1, source_target_pairs={{0,3},{1,0},{2,1},{3,2},{4,7},{5,4},{6,5},{7,6},{8,11},{9,8},{10,9... | collective-permute-start | bytes 786440 | tf_op jit(solution)/shard_map/ppermute | solution.py:345
  74.8 4.3 %collective-permute-done.10.refs_1_ = bf16[128,1024]{1,0:T(8,128)(2,1)S(1)} collective-permute-done((bf16[128,1024]{1,0:T(8,128)(2,1)S(1)}, bf16[128,1024]{1,0:T(8,128)(2,1)S(1)}, u32[]{:S(2)}, u32[]{:S(2)}) %collective-permute-start.10) | collective-permute-done | bytes 262176 | tf_op jit(solution)/shard_map/ppermute | solution.py:345
  79.1 11.5 %collective-permute-done.11.refs_2_ = bf16[128,1024]{1,0:T(8,128)(2,1)S(1)} collective-permute-done((bf16[128,1024]{1,0:T(8,128)(2,1)S(1)}, bf16[128,1024]{1,0:T(8,128)(2,1)S(1)}, u32[]{:S(2)}, u32[]{:S(2)}) %collective-permute-start.11) | collective-permute-done | bytes 262176 | tf_op jit(solution)/shard_map/ppermute | solution.py:345
  90.6 4.8 %collective-permute-done.12.refs_3_ = bf16[128,1024]{1,0:T(8,128)(2,1)S(1)} collective-permute-done((bf16[128,1024]{1,0:T(8,128)(2,1)S(1)}, bf16[128,1024]{1,0:T(8,128)(2,1)S(1)}, u32[]{:S(2)}, u32[]{:S(2)}) %collective-permute-start.12) | collective-permute-done | bytes 262176 | tf_op jit(solution)/shard_map/ppermute | solution.py:345
  95.4 0.9 add.1
  (1 shorter events, 0.0 us)
Async XLA Ops:
  0.0 0.9 copy-start
  0.9 0.9 copy-start.1
  1.8 0.9 copy-start.2
  2.7 0.9 copy-start.3
  3.7 11.6 %collective-permute-start = (bf16[320,256]{1,0:T(8,128)(2,1)S(1)}, bf16[320,256]{1,0:T(8,128)(2,1)S(1)}, u32[]{:S(2)}, u32[]{:S(2)}) collective-permute-start(bf16[320,256]{1,0:T(8,128)(2,1)S(1)} %get-tuple-element.17), channel_id=1, source_target_pairs={{0,8},{4,12},{8,16},{12,20},{16,24},{20,28},{24,32},{28,36},{32,40... | collective-permute-start | bytes 491528 | tf_op jit(solution)/shard_map/ppermute | solution.py:318
  5.8 9.5 %collective-permute-start.1 = (bf16[256,256]{1,0:T(8,128)(2,1)S(1)}, bf16[256,256]{1,0:T(8,128)(2,1)S(1)}, u32[]{:S(2)}, u32[]{:S(2)}) collective-permute-start(bf16[256,256]{1,0:T(8,128)(2,1)S(1)} %get-tuple-element.18.refs_9_.refs_10_), channel_id=1, source_target_pairs={{0,16},{4,20},{8,24},{12,28},{16,32},{20,36},{24,40},{28,44},{32,4... | collective-permute-start | bytes 393224 | tf_op jit(solution)/shard_map/ppermute | solution.py:318
  8.2 12.2 %collective-permute-start.7 = (bf16[320,256]{1,0:T(8,128)(2,1)S(1)}, bf16[320,256]{1,0:T(8,128)(2,1)S(1)}, u32[]{:S(2)}, u32[]{:S(2)}) collective-permute-start(bf16[320,256]{1,0:T(8,128)(2,1)S(1)} %get-tuple-element.17), channel_id=1, source_target_pairs={{0,4},{4,0},{8,12},{12,8},{16,20},{20,16},{24,28},{28,24},{32,36},... | collective-permute-start | bytes 491528 | tf_op jit(solution)/shard_map/ppermute | solution.py:321
  15.3 16.3 %collective-permute-start.3 = (bf16[320,256]{1,0:T(8,128)(2,1)S(1)}, bf16[320,256]{1,0:T(8,128)(2,1)S(1)}, u32[]{:S(2)}, u32[]{:S(2)}) collective-permute-start(bf16[320,256]{1,0:T(8,128)(2,1)S(1)} %get-tuple-element.21), channel_id=1, source_target_pairs={{0,8},{4,12},{8,16},{12,20},{16,24},{20,28},{24,32},{28,36},{32,40... | collective-permute-start | bytes 491528 | tf_op jit(solution)/shard_map/ppermute | solution.py:318
  16.5 15.1 %collective-permute-start.8 = (bf16[320,256]{1,0:T(8,128)(2,1)S(1)}, bf16[320,256]{1,0:T(8,128)(2,1)S(1)}, u32[]{:S(2)}, u32[]{:S(2)}) collective-permute-start(bf16[320,256]{1,0:T(8,128)(2,1)S(1)} %collective-permute-done.refs_13_.refs_14_), channel_id=1, source_target_pairs={{0,4},{4,0},{8,12},{12,8},{16,20},{20,16},{24,28},{28,24},{32,36},... | collective-permute-start | bytes 491528 | tf_op jit(solution)/shard_map/ppermute | solution.py:321
  20.4 10.0 %collective-permute-start.5 = (bf16[256,256]{1,0:T(8,128)(2,1)S(1)}, bf16[256,256]{1,0:T(8,128)(2,1)S(1)}, u32[]{:S(2)}, u32[]{:S(2)}) collective-permute-start(bf16[256,256]{1,0:T(8,128)(2,1)S(1)} %get-tuple-element.22.refs_9_.refs_10_), channel_id=1, source_target_pairs={{0,16},{4,20},{8,24},{12,28},{16,32},{20,36},{24,40},{28,44},{32,4... | collective-permute-start | bytes 393224 | tf_op jit(solution)/shard_map/ppermute | solution.py:318
  20.4 11.2 %collective-permute-start.9 = (bf16[256,256]{1,0:T(8,128)(2,1)S(1)}, bf16[256,256]{1,0:T(8,128)(2,1)S(1)}, u32[]{:S(2)}, u32[]{:S(2)}) collective-permute-start(bf16[256,256]{1,0:T(8,128)(2,1)S(1)} %collective-permute-done.1.refs_17_.refs_18_), channel_id=1, source_target_pairs={{0,4},{4,0},{8,12},{12,8},{16,20},{20,16},{24,28},{28,24},{32,36},... | collective-permute-start | bytes 393224 | tf_op jit(solution)/shard_map/ppermute | solution.py:321
  20.4 27.0 %collective-permute-start.2 = (bf16[320,256]{1,0:T(8,128)(2,1)S(1)}, bf16[320,256]{1,0:T(8,128)(2,1)S(1)}, u32[]{:S(2)}, u32[]{:S(2)}) collective-permute-start(bf16[320,256]{1,0:T(8,128)(2,1)S(1)} %get-tuple-element.21), channel_id=1, source_target_pairs={{0,4},{4,0},{8,12},{12,8},{16,20},{20,16},{24,28},{28,24},{32,36},... | collective-permute-start | bytes 491528 | tf_op jit(solution)/shard_map/ppermute | solution.py:321
  30.4 17.0 %collective-permute-start.6 = (bf16[256,256]{1,0:T(8,128)(2,1)S(1)}, bf16[256,256]{1,0:T(8,128)(2,1)S(1)}, u32[]{:S(2)}, u32[]{:S(2)}) collective-permute-start(bf16[256,256]{1,0:T(8,128)(2,1)S(1)} %collective-permute-done.5.refs_17_.refs_18_), channel_id=1, source_target_pairs={{0,4},{4,0},{8,12},{12,8},{16,20},{20,16},{24,28},{28,24},{32,36},... | collective-permute-start | bytes 393224 | tf_op jit(solution)/shard_map/ppermute | solution.py:321
  31.6 15.9 %collective-permute-start.4 = (bf16[320,256]{1,0:T(8,128)(2,1)S(1)}, bf16[320,256]{1,0:T(8,128)(2,1)S(1)}, u32[]{:S(2)}, u32[]{:S(2)}) collective-permute-start(bf16[320,256]{1,0:T(8,128)(2,1)S(1)} %collective-permute-done.3.refs_13_.refs_14_), channel_id=1, source_target_pairs={{0,4},{4,0},{8,12},{12,8},{16,20},{20,16},{24,28},{28,24},{32,36},... | collective-permute-start | bytes 491528 | tf_op jit(solution)/shard_map/ppermute | solution.py:321
  64.9 14.2 %collective-permute-start.10 = (bf16[128,1024]{1,0:T(8,128)(2,1)S(1)}, bf16[128,1024]{1,0:T(8,128)(2,1)S(1)}, u32[]{:S(2)}, u32[]{:S(2)}) collective-permute-start(bf16[128,1024]{1,0:T(8,128)(2,1)S(1)} %get-tuple-element.26), channel_id=1, source_target_pairs={{0,2},{1,3},{2,0},{3,1},{4,6},{5,7},{6,4},{7,5},{8,10},{9,11},{10,... | collective-permute-start | bytes 786440 | tf_op jit(solution)/shard_map/ppermute | solution.py:345
  71.2 19.4 %collective-permute-start.11 = (bf16[128,1024]{1,0:T(8,128)(2,1)S(1)}, bf16[128,1024]{1,0:T(8,128)(2,1)S(1)}, u32[]{:S(2)}, u32[]{:S(2)}) collective-permute-start(bf16[128,1024]{1,0:T(8,128)(2,1)S(1)} %get-tuple-element.27), channel_id=1, source_target_pairs={{0,1},{1,2},{2,3},{3,0},{4,5},{5,6},{6,7},{7,4},{8,9},{9,10},{10,1... | collective-permute-start | bytes 786440 | tf_op jit(solution)/shard_map/ppermute | solution.py:345
  72.4 23.0 %collective-permute-start.12 = (bf16[128,1024]{1,0:T(8,128)(2,1)S(1)}, bf16[128,1024]{1,0:T(8,128)(2,1)S(1)}, u32[]{:S(2)}, u32[]{:S(2)}) collective-permute-start(bf16[128,1024]{1,0:T(8,128)(2,1)S(1)} %get-tuple-element.28), channel_id=1, source_target_pairs={{0,3},{1,0},{2,1},{3,2},{4,7},{5,4},{6,5},{7,6},{8,11},{9,8},{10,9... | collective-permute-start | bytes 786440 | tf_op jit(solution)/shard_map/ppermute | solution.py:345

commit v4 on v3

--- a/solution.py
+++ b/solution.py
@@ -320,6 +320,12 @@
     def swap(x):
         return lax.ppermute(x, "seq", [(i, i ^ 1) for i in range(seq)])
 
+    queries, first_key_rows, first_value_rows, second_key_rows, second_value_rows = (
+        pltpu.with_memory_space_constraint(x, pltpu.HBM)
+        for x in (
+            queries, first_key_rows, first_value_rows, second_key_rows, second_value_rows
+        )
+    )
     kva, alla, kvb, allb = pack(
         first_key_rows, first_value_rows, second_key_rows, second_value_rows
     )
@@ -332,10 +338,7 @@
     p2b = behind(sendb, 2)
     p4b = behind(kvsend, 4)
     x0b = swap(sendb)
-    common = (shard, me) + tuple(
-        pltpu.with_memory_space_constraint(x, pltpu.HBM)
-        for x in (queries, second_key_rows, second_value_rows)
-    )
+    common = (shard, me, queries, second_key_rows, second_value_rows)
     done = attend(0, *common, (kva, x0a, p2a, x2a, p4a, x4a))
     x2b = swap(p2b)
     x4b = swap(p4b)

time: 96.5 us -> 93.8 us (0.972)
  local copies, waits for them, and re-layouts: 3.61 us -> 0 us
    unnamed x8 -> x0, local copies, waits for them, and re-layouts: 3.61 us -> none
    pallas_call x1, Pallas kernels: 0.04 us -> 1.01 us  [pack(): pl.pallas_call(pack_body, out_shape=tuple((jax.ShapeDtypeStruct(x, BF16)...]
  transfers between devices with their start and end apart: 13 -> 13, of which waited for: 5 -> 5; matrix products, arithmetic and copies ran while one was open for 0% -> 0% of each run, Pallas kernels for 16% -> 17%
where the time goes in v4:
time: 93.8 us; the launch traced here: 93.6 us
  waiting for transfers between devices  36 us (38%)
  Pallas kernels  35.1 us (37%)
  starting transfers between devices  22.5 us (24%)
    pallas_call x2, Pallas kernels, attend(): pl.pallas_call(lambda *refs: attn_body(tuple(range(nb)), final, *refs), o...  33.2 us
    ppermute x3, waiting for transfers between devices, local(): lax.ppermute(pieces[d], 'head', [(i, (i + d) % 4) for i in range(4)])  20.6 us
    ppermute x4, waiting for transfers between devices, behind(): return lax.ppermute(x, 'seq', [(i, (i + by) % seq) for i in range(seq)])  15.3 us
    ppermute x3, starting transfers between devices, local(): lax.ppermute(pieces[d], 'head', [(i, (i + d) % 4) for i in range(4)])  9.89 us
    ppermute x6, starting transfers between devices, swap(): return lax.ppermute(x, 'seq', [(i, i ^ 1) for i in range(seq)])  6.85 us
    ppermute x4, starting transfers between devices, behind(): return lax.ppermute(x, 'seq', [(i, (i + by) % seq) for i in range(seq)])  5.75 us
  transfers between devices with their start and end apart: 13, of which 5 were waited for; matrix products, arithmetic and copies ran while one was open for 0% of the time, Pallas kernels for 17%

profile of v4, /device:TPU:1, one launch (start us, length us, event | category | flops | bytes accessed | tf_op | source)
XLA Modules:
  0.0 93.6 jit_solution(17725393740925038256)
XLA Ops:
  0.0 1.0 %pack.1 = (bf16[256,256]{1,0:T(8,128)(2,1)S(1)}, bf16[320,256]{1,0:T(8,128)(2,1)S(1)}, bf16[256,256]{1,0:T(8,128)(2,1)S(1)}, bf16[320,256]{1,0:T(8,128)(2,1)S(1)}) custom-call(bf16[128,512]{1,0:T(8,128)(2,1)} %k_ref.1, bf16[128,512]{1,0:T(8,128)(2,1)} %v_ref.1, bf16[128,512]{1,0:T(8,128)(2,1)} %refs_3_.3, bf16[128,512]{1,0:T(8,128)(2,1)} %refs_4_.3), custom_call_target="tpu_custom_call" | custom-call | tf_op jit(solution)/shard_map/pack/pallas_call | solution.py:296
  1.0 2.1 %collective-permute-start = (bf16[320,256]{1,0:T(8,128)(2,1)S(1)}, bf16[320,256]{1,0:T(8,128)(2,1)S(1)}, u32[]{:S(2)}, u32[]{:S(2)}) collective-permute-start(bf16[320,256]{1,0:T(8,128)(2,1)S(1)} %get-tuple-element.17), channel_id=1, source_target_pairs={{0,8},{4,12},{8,16},{12,20},{16,24},{20,28},{24,32},{28,36},{32,40... | collective-permute-start | bytes 491528 | tf_op jit(solution)/shard_map/ppermute | solution.py:318
  3.1 2.5 %collective-permute-start.1 = (bf16[256,256]{1,0:T(8,128)(2,1)S(1)}, bf16[256,256]{1,0:T(8,128)(2,1)S(1)}, u32[]{:S(2)}, u32[]{:S(2)}) collective-permute-start(bf16[256,256]{1,0:T(8,128)(2,1)S(1)} %get-tuple-element.18.refs_9_.refs_10_), channel_id=1, source_target_pairs={{0,16},{4,20},{8,24},{12,28},{16,32},{20,36},{24,40},{28,44},{32,4... | collective-permute-start | bytes 393224 | tf_op jit(solution)/shard_map/ppermute | solution.py:318
  5.6 1.2 %collective-permute-start.7 = (bf16[320,256]{1,0:T(8,128)(2,1)S(1)}, bf16[320,256]{1,0:T(8,128)(2,1)S(1)}, u32[]{:S(2)}, u32[]{:S(2)}) collective-permute-start(bf16[320,256]{1,0:T(8,128)(2,1)S(1)} %get-tuple-element.17), channel_id=1, source_target_pairs={{0,4},{4,0},{8,12},{12,8},{16,20},{20,16},{24,28},{28,24},{32,36},... | collective-permute-start | bytes 491528 | tf_op jit(solution)/shard_map/ppermute | solution.py:321
  6.8 5.8 %collective-permute-done.1.refs_17_.refs_18_ = bf16[256,256]{1,0:T(8,128)(2,1)S(1)} collective-permute-done((bf16[256,256]{1,0:T(8,128)(2,1)S(1)}, bf16[256,256]{1,0:T(8,128)(2,1)S(1)}, u32[]{:S(2)}, u32[]{:S(2)}) %collective-permute-start.1) | collective-permute-done | bytes 131104 | tf_op jit(solution)/shard_map/ppermute | solution.py:318
  12.6 0.0 collective-permute-done.refs_13_.refs_14_
  12.6 1.2 %collective-permute-start.3 = (bf16[320,256]{1,0:T(8,128)(2,1)S(1)}, bf16[320,256]{1,0:T(8,128)(2,1)S(1)}, u32[]{:S(2)}, u32[]{:S(2)}) collective-permute-start(bf16[320,256]{1,0:T(8,128)(2,1)S(1)} %get-tuple-element.21), channel_id=1, source_target_pairs={{0,8},{4,12},{8,16},{12,20},{16,24},{20,28},{24,32},{28,36},{32,40... | collective-permute-start | bytes 491528 | tf_op jit(solution)/shard_map/ppermute | solution.py:318
  13.8 3.9 %collective-permute-start.8 = (bf16[320,256]{1,0:T(8,128)(2,1)S(1)}, bf16[320,256]{1,0:T(8,128)(2,1)S(1)}, u32[]{:S(2)}, u32[]{:S(2)}) collective-permute-start(bf16[320,256]{1,0:T(8,128)(2,1)S(1)} %collective-permute-done.refs_13_.refs_14_), channel_id=1, source_target_pairs={{0,4},{4,0},{8,12},{12,8},{16,20},{20,16},{24,28},{28,24},{32,36},... | collective-permute-start | bytes 491528 | tf_op jit(solution)/shard_map/ppermute | solution.py:321
  17.8 0.0 collective-permute-start.5
  17.8 0.0 collective-permute-start.9
  17.8 0.0 collective-permute-done.7.refs_5_.refs_6_.refs_11_.refs_12_
  17.8 0.5 collective-permute-start.2
  18.3 9.5 %collective-permute-done.5.refs_17_.refs_18_ = bf16[256,256]{1,0:T(8,128)(2,1)S(1)} collective-permute-done((bf16[256,256]{1,0:T(8,128)(2,1)S(1)}, bf16[256,256]{1,0:T(8,128)(2,1)S(1)}, u32[]{:S(2)}, u32[]{:S(2)}) %collective-permute-start.5) | collective-permute-done | bytes 131104 | tf_op jit(solution)/shard_map/ppermute | solution.py:318
  27.8 1.2 %collective-permute-start.6 = (bf16[256,256]{1,0:T(8,128)(2,1)S(1)}, bf16[256,256]{1,0:T(8,128)(2,1)S(1)}, u32[]{:S(2)}, u32[]{:S(2)}) collective-permute-start(bf16[256,256]{1,0:T(8,128)(2,1)S(1)} %collective-permute-done.5.refs_17_.refs_18_), channel_id=1, source_target_pairs={{0,4},{4,0},{8,12},{12,8},{16,20},{20,16},{24,28},{28,24},{32,36},... | collective-permute-start | bytes 393224 | tf_op jit(solution)/shard_map/ppermute | solution.py:321
  28.9 0.0 collective-permute-done.3.refs_13_.refs_14_
  28.9 0.0 collective-permute-start.4
  28.9 0.0 collective-permute-done.9.refs_19_.refs_20_
  28.9 0.0 collective-permute-done.8.refs_7_.refs_8_.refs_15_.refs_16_
  29.0 15.8 %shard_map.64.refs_21_ = bf16[128,512]{1,0:T(8,128)(2,1)S(1)} custom-call(s32[1]{0:T(128)} %bitcast.refs_0_, s32[1]{0:T(128)} %bitcast.1.refs_1_, bf16[128,1024]{1,0:T(8,128)(2,1)} %refs_2_.3, bf16[128,512]{1,0:T(8,128)(2,1)} %refs_3_.3, bf16[128,512]{1,0:T(8,128)(2,1)} %refs_4_.3, ...), custom_call_target="tpu_custom_call" | custom-call | flops 21474836480 | bytes 12582912 | tf_op jit(solution)/shard_map/pallas_call | solution.py:262
  44.8 0.0 collective-permute-done.2.refs_5_.refs_6_.refs_11_.refs_12_
  44.8 0.0 collective-permute-done.6.refs_19_.refs_20_
  44.8 0.0 collective-permute-done.4.refs_7_.refs_8_.refs_15_.refs_16_
  44.8 17.4 %shard_map.65 = (bf16[128,1024]{1,0:T(8,128)(2,1)S(1)}, bf16[128,1024]{1,0:T(8,128)(2,1)S(1)}, bf16[128,1024]{1,0:T(8,128)(2,1)S(1)}, bf16[128,1024]{1,0:T(8,128)(2,1)S(1)}) custom-call(s32[1]{0:T(128)} %bitcast.refs_0_, s32[1]{0:T(128)} %bitcast.1.refs_1_, bf16[128,1024]{1,0:T(8,128)(2,1)} %refs_2_.3, bf16[128,512]{1,0:T(8,128)(2,1)} %refs_3_.3, ...), custom_call_target="tpu_custom_call" | custom-call | flops 21474836480 | bytes 12582912 | tf_op jit(solution)/shard_map/pallas_call | solution.py:262
  62.2 6.3 %collective-permute-start.10 = (bf16[128,1024]{1,0:T(8,128)(2,1)S(1)}, bf16[128,1024]{1,0:T(8,128)(2,1)S(1)}, u32[]{:S(2)}, u32[]{:S(2)}) collective-permute-start(bf16[128,1024]{1,0:T(8,128)(2,1)S(1)} %get-tuple-element.26), channel_id=1, source_target_pairs={{0,2},{1,3},{2,0},{3,1},{4,6},{5,7},{6,4},{7,5},{8,10},{9,11},{10,... | collective-permute-start | bytes 786440 | tf_op jit(solution)/shard_map/ppermute | solution.py:348
  68.5 1.2 %collective-permute-start.11 = (bf16[128,1024]{1,0:T(8,128)(2,1)S(1)}, bf16[128,1024]{1,0:T(8,128)(2,1)S(1)}, u32[]{:S(2)}, u32[]{:S(2)}) collective-permute-start(bf16[128,1024]{1,0:T(8,128)(2,1)S(1)} %get-tuple-element.27), channel_id=1, source_target_pairs={{0,1},{1,2},{2,3},{3,0},{4,5},{5,6},{6,7},{7,4},{8,9},{9,10},{10,1... | collective-permute-start | bytes 786440 | tf_op jit(solution)/shard_map/ppermute | solution.py:348
  69.7 2.4 %collective-permute-start.12 = (bf16[128,1024]{1,0:T(8,128)(2,1)S(1)}, bf16[128,1024]{1,0:T(8,128)(2,1)S(1)}, u32[]{:S(2)}, u32[]{:S(2)}) collective-permute-start(bf16[128,1024]{1,0:T(8,128)(2,1)S(1)} %get-tuple-element.28), channel_id=1, source_target_pairs={{0,3},{1,0},{2,1},{3,2},{4,7},{5,4},{6,5},{7,6},{8,11},{9,8},{10,9... | collective-permute-start | bytes 786440 | tf_op jit(solution)/shard_map/ppermute | solution.py:348
  72.1 4.3 %collective-permute-done.10.refs_1_ = bf16[128,1024]{1,0:T(8,128)(2,1)S(1)} collective-permute-done((bf16[128,1024]{1,0:T(8,128)(2,1)S(1)}, bf16[128,1024]{1,0:T(8,128)(2,1)S(1)}, u32[]{:S(2)}, u32[]{:S(2)}) %collective-permute-start.10) | collective-permute-done | bytes 262176 | tf_op jit(solution)/shard_map/ppermute | solution.py:348
  76.4 11.5 %collective-permute-done.11.refs_2_ = bf16[128,1024]{1,0:T(8,128)(2,1)S(1)} collective-permute-done((bf16[128,1024]{1,0:T(8,128)(2,1)S(1)}, bf16[128,1024]{1,0:T(8,128)(2,1)S(1)}, u32[]{:S(2)}, u32[]{:S(2)}) %collective-permute-start.11) | collective-permute-done | bytes 262176 | tf_op jit(solution)/shard_map/ppermute | solution.py:348
  88.0 4.8 %collective-permute-done.12.refs_3_ = bf16[128,1024]{1,0:T(8,128)(2,1)S(1)} collective-permute-done((bf16[128,1024]{1,0:T(8,128)(2,1)S(1)}, bf16[128,1024]{1,0:T(8,128)(2,1)S(1)}, u32[]{:S(2)}, u32[]{:S(2)}) %collective-permute-start.12) | collective-permute-done | bytes 262176 | tf_op jit(solution)/shard_map/ppermute | solution.py:348
  92.7 0.9 add.1
Async XLA Ops:
  1.0 11.6 %collective-permute-start = (bf16[320,256]{1,0:T(8,128)(2,1)S(1)}, bf16[320,256]{1,0:T(8,128)(2,1)S(1)}, u32[]{:S(2)}, u32[]{:S(2)}) collective-permute-start(bf16[320,256]{1,0:T(8,128)(2,1)S(1)} %get-tuple-element.17), channel_id=1, source_target_pairs={{0,8},{4,12},{8,16},{12,20},{16,24},{20,28},{24,32},{28,36},{32,40... | collective-permute-start | bytes 491528 | tf_op jit(solution)/shard_map/ppermute | solution.py:318
  3.1 9.5 %collective-permute-start.1 = (bf16[256,256]{1,0:T(8,128)(2,1)S(1)}, bf16[256,256]{1,0:T(8,128)(2,1)S(1)}, u32[]{:S(2)}, u32[]{:S(2)}) collective-permute-start(bf16[256,256]{1,0:T(8,128)(2,1)S(1)} %get-tuple-element.18.refs_9_.refs_10_), channel_id=1, source_target_pairs={{0,16},{4,20},{8,24},{12,28},{16,32},{20,36},{24,40},{28,44},{32,4... | collective-permute-start | bytes 393224 | tf_op jit(solution)/shard_map/ppermute | solution.py:318
  5.6 12.2 %collective-permute-start.7 = (bf16[320,256]{1,0:T(8,128)(2,1)S(1)}, bf16[320,256]{1,0:T(8,128)(2,1)S(1)}, u32[]{:S(2)}, u32[]{:S(2)}) collective-permute-start(bf16[320,256]{1,0:T(8,128)(2,1)S(1)} %get-tuple-element.17), channel_id=1, source_target_pairs={{0,4},{4,0},{8,12},{12,8},{16,20},{20,16},{24,28},{28,24},{32,36},... | collective-permute-start | bytes 491528 | tf_op jit(solution)/shard_map/ppermute | solution.py:321
  12.6 16.3 %collective-permute-start.3 = (bf16[320,256]{1,0:T(8,128)(2,1)S(1)}, bf16[320,256]{1,0:T(8,128)(2,1)S(1)}, u32[]{:S(2)}, u32[]{:S(2)}) collective-permute-start(bf16[320,256]{1,0:T(8,128)(2,1)S(1)} %get-tuple-element.21), channel_id=1, source_target_pairs={{0,8},{4,12},{8,16},{12,20},{16,24},{20,28},{24,32},{28,36},{32,40... | collective-permute-start | bytes 491528 | tf_op jit(solution)/shard_map/ppermute | solution.py:318
  13.8 15.1 %collective-permute-start.8 = (bf16[320,256]{1,0:T(8,128)(2,1)S(1)}, bf16[320,256]{1,0:T(8,128)(2,1)S(1)}, u32[]{:S(2)}, u32[]{:S(2)}) collective-permute-start(bf16[320,256]{1,0:T(8,128)(2,1)S(1)} %collective-permute-done.refs_13_.refs_14_), channel_id=1, source_target_pairs={{0,4},{4,0},{8,12},{12,8},{16,20},{20,16},{24,28},{28,24},{32,36},... | collective-permute-start | bytes 491528 | tf_op jit(solution)/shard_map/ppermute | solution.py:321
  17.8 10.0 %collective-permute-start.5 = (bf16[256,256]{1,0:T(8,128)(2,1)S(1)}, bf16[256,256]{1,0:T(8,128)(2,1)S(1)}, u32[]{:S(2)}, u32[]{:S(2)}) collective-permute-start(bf16[256,256]{1,0:T(8,128)(2,1)S(1)} %get-tuple-element.22.refs_9_.refs_10_), channel_id=1, source_target_pairs={{0,16},{4,20},{8,24},{12,28},{16,32},{20,36},{24,40},{28,44},{32,4... | collective-permute-start | bytes 393224 | tf_op jit(solution)/shard_map/ppermute | solution.py:318
  17.8 11.2 %collective-permute-start.9 = (bf16[256,256]{1,0:T(8,128)(2,1)S(1)}, bf16[256,256]{1,0:T(8,128)(2,1)S(1)}, u32[]{:S(2)}, u32[]{:S(2)}) collective-permute-start(bf16[256,256]{1,0:T(8,128)(2,1)S(1)} %collective-permute-done.1.refs_17_.refs_18_), channel_id=1, source_target_pairs={{0,4},{4,0},{8,12},{12,8},{16,20},{20,16},{24,28},{28,24},{32,36},... | collective-permute-start | bytes 393224 | tf_op jit(solution)/shard_map/ppermute | solution.py:321
  17.8 27.0 %collective-permute-start.2 = (bf16[320,256]{1,0:T(8,128)(2,1)S(1)}, bf16[320,256]{1,0:T(8,128)(2,1)S(1)}, u32[]{:S(2)}, u32[]{:S(2)}) collective-permute-start(bf16[320,256]{1,0:T(8,128)(2,1)S(1)} %get-tuple-element.21), channel_id=1, source_target_pairs={{0,4},{4,0},{8,12},{12,8},{16,20},{20,16},{24,28},{28,24},{32,36},... | collective-permute-start | bytes 491528 | tf_op jit(solution)/shard_map/ppermute | solution.py:321
  27.8 17.0 %collective-permute-start.6 = (bf16[256,256]{1,0:T(8,128)(2,1)S(1)}, bf16[256,256]{1,0:T(8,128)(2,1)S(1)}, u32[]{:S(2)}, u32[]{:S(2)}) collective-permute-start(bf16[256,256]{1,0:T(8,128)(2,1)S(1)} %collective-permute-done.5.refs_17_.refs_18_), channel_id=1, source_target_pairs={{0,4},{4,0},{8,12},{12,8},{16,20},{20,16},{24,28},{28,24},{32,36},... | collective-permute-start | bytes 393224 | tf_op jit(solution)/shard_map/ppermute | solution.py:321
  28.9 15.9 %collective-permute-start.4 = (bf16[320,256]{1,0:T(8,128)(2,1)S(1)}, bf16[320,256]{1,0:T(8,128)(2,1)S(1)}, u32[]{:S(2)}, u32[]{:S(2)}) collective-permute-start(bf16[320,256]{1,0:T(8,128)(2,1)S(1)} %collective-permute-done.3.refs_13_.refs_14_), channel_id=1, source_target_pairs={{0,4},{4,0},{8,12},{12,8},{16,20},{20,16},{24,28},{28,24},{32,36},... | collective-permute-start | bytes 491528 | tf_op jit(solution)/shard_map/ppermute | solution.py:321
  62.2 14.2 %collective-permute-start.10 = (bf16[128,1024]{1,0:T(8,128)(2,1)S(1)}, bf16[128,1024]{1,0:T(8,128)(2,1)S(1)}, u32[]{:S(2)}, u32[]{:S(2)}) collective-permute-start(bf16[128,1024]{1,0:T(8,128)(2,1)S(1)} %get-tuple-element.26), channel_id=1, source_target_pairs={{0,2},{1,3},{2,0},{3,1},{4,6},{5,7},{6,4},{7,5},{8,10},{9,11},{10,... | collective-permute-start | bytes 786440 | tf_op jit(solution)/shard_map/ppermute | solution.py:348
  68.5 19.4 %collective-permute-start.11 = (bf16[128,1024]{1,0:T(8,128)(2,1)S(1)}, bf16[128,1024]{1,0:T(8,128)(2,1)S(1)}, u32[]{:S(2)}, u32[]{:S(2)}) collective-permute-start(bf16[128,1024]{1,0:T(8,128)(2,1)S(1)} %get-tuple-element.27), channel_id=1, source_target_pairs={{0,1},{1,2},{2,3},{3,0},{4,5},{5,6},{6,7},{7,4},{8,9},{9,10},{10,1... | collective-permute-start | bytes 786440 | tf_op jit(solution)/shard_map/ppermute | solution.py:348
  69.7 23.0 %collective-permute-start.12 = (bf16[128,1024]{1,0:T(8,128)(2,1)S(1)}, bf16[128,1024]{1,0:T(8,128)(2,1)S(1)}, u32[]{:S(2)}, u32[]{:S(2)}) collective-permute-start(bf16[128,1024]{1,0:T(8,128)(2,1)S(1)} %get-tuple-element.28), channel_id=1, source_target_pairs={{0,3},{1,0},{2,1},{3,2},{4,7},{5,4},{6,5},{7,6},{8,11},{9,8},{10,9... | collective-permute-start | bytes 786440 | tf_op jit(solution)/shard_map/ppermute | solution.py:348

commit v5 on v4

--- a/solution.py
+++ b/solution.py
@@ -217,11 +217,13 @@
             ).astype(BF16)
 
 
-def attend(half, shard, me, q, k2, v2, pieces, done=None, weight=None):
+def attend(half, part, shard, me, q, k2, v2, pieces, done=None, weight=None):
     final = weight is not None
     groups = k2.shape[1] // HS // 2
     g0 = half * groups
-    nb = R // IB
+    blocks = tuple(range(R // IB)) if part is None else (2 * part, 2 * part + 1)
+    nb = len(blocks)
+    rows = nb * IB
     kblock = pl.BlockSpec((R, HS), lambda g: (0, g))
     vblock = pl.BlockSpec((R, HS), lambda g: (1, g))
     own = pl.BlockSpec((R, HS), lambda g: (0, g0 + g))
@@ -250,17 +252,20 @@
     scratch += [pltpu.VMEM((2, 8, HS), F32)]
     if final:
         width = weight.shape[1] // 4
-        out_shape = (jax.ShapeDtypeStruct((R, width), BF16),) * 4
-        out_specs = (pl.BlockSpec((R, width), lambda g: (0, 0)),) * 4
+        out_shape = (jax.ShapeDtypeStruct((rows, width), BF16),) * 4
+        out_specs = (pl.BlockSpec((rows, width), lambda g: (0, 0)),) * 4
         args += [done, weight]
-        specs += [pl.BlockSpec(done.shape, lambda g: (0, 0)), pl.BlockSpec(memory_space=pl.ANY)]
-        scratch += [pltpu.VMEM(q.shape, BF16), pltpu.VMEM(weight.shape, BF16)]
+        specs += [
+            pl.BlockSpec((rows, done.shape[1]), lambda g: (part, 0)),
+            pl.BlockSpec(memory_space=pl.ANY),
+        ]
+        scratch += [pltpu.VMEM((rows, q.shape[1]), BF16), pltpu.VMEM(weight.shape, BF16)]
         scratch += [pltpu.SemaphoreType.DMA((4,))]
     else:
         out_shape = jax.ShapeDtypeStruct((R, 2 * HS * groups), BF16)
         out_specs = pl.BlockSpec((R, 2 * HS), lambda g: (0, g))
     return pl.pallas_call(
-        lambda *refs: attn_body(tuple(range(nb)), final, *refs),
+        lambda *refs: attn_body(blocks, final, *refs),
         out_shape=out_shape,
         grid=(groups,),
         in_specs=specs,
@@ -268,9 +273,9 @@
         scratch_shapes=scratch,
         compiler_params=PARAMS,
         cost_estimate=pl.CostEstimate(
-            flops=4 * W2 * R * KEYS * HS * 2 * groups * 4,
+            flops=4 * W2 * rows * KEYS * HS * 2 * groups * 4,
             bytes_accessed=12 * 2**20,
-            transcendentals=W2 * R * W1 * 2 * groups,
+            transcendentals=W2 * rows * W1 * 2 * groups,
         ),
     )(*args)
 
@@ -305,8 +310,11 @@
 
 
 def add_body(*refs):
-    x = [r[...].astype(F32) for r in refs[:-1]]
-    refs[-1][...] = (x[0] + x[1] + x[2] + x[3]).astype(BF16)
+    out = refs[-1]
+    rows = out.shape[0] // 2
+    for part in range(2):
+        x = [r[...].astype(F32) for r in refs[4 * part : 4 * part + 4]]
+        out[part * rows : (part + 1) * rows, :] = (x[0] + x[1] + x[2] + x[3]).astype(BF16)
 
 
 def local(queries, first_key_rows, first_value_rows, second_key_rows, second_value_rows, out_weight):
@@ -339,21 +347,23 @@
     p4b = behind(kvsend, 4)
     x0b = swap(sendb)
     common = (shard, me, queries, second_key_rows, second_value_rows)
-    done = attend(0, *common, (kva, x0a, p2a, x2a, p4a, x4a))
+    done = attend(0, None, *common, (kva, x0a, p2a, x2a, p4a, x4a))
     x2b = swap(p2b)
     x4b = swap(p4b)
-    pieces = attend(1, *common, (kvb, x0b, p2b, x2b, p4b, x4b), done, out_weight)
-    got = [pieces[0]]
-    for d in (2, 1, 3):
-        got.append(lax.ppermute(pieces[d], "head", [(i, (i + d) % 4) for i in range(4)]))
-    cols = queries.shape[1] // 2
-    block = pl.BlockSpec((R, cols), lambda i: (0, i))
+    last = (kvb, x0b, p2b, x2b, p4b, x4b)
+    halves = [attend(1, 0, *common, last, done, out_weight)]
+    halves.append(attend(1, 1, *common, last, done, out_weight))
+    got = []
+    for pieces in halves:
+        got.append(pieces[0])
+        for d in (2, 1, 3):
+            got.append(lax.ppermute(pieces[d], "head", [(i, (i + d) % 4) for i in range(4)]))
     return pl.pallas_call(
         add_body,
         out_shape=jax.ShapeDtypeStruct(queries.shape, BF16),
-        grid=(2,),
-        in_specs=[block] * 4,
-        out_specs=block,
+        grid=(1,),
+        in_specs=[pl.BlockSpec((R // 2, queries.shape[1]), lambda i: (0, 0))] * 8,
+        out_specs=pl.BlockSpec(queries.shape, lambda i: (0, 0)),
         compiler_params=SMALL,
         name="add",
     )(*got)

time: 93.8 us -> 92.1 us (0.982)
  waiting for transfers between devices: 36 us -> 25.6 us
  starting transfers between devices: 22.5 us -> 27.3 us
  Pallas kernels: 35.1 us -> 38.9 us
    ppermute x3 -> x6, waiting for transfers between devices: 20.6 us -> 10.3 us  [local(): lax.ppermute(pieces[d], 'head', [(i, (i + d) % 4) for i in range(4)])]
    ppermute x3 -> x6, starting transfers between devices: 9.89 us -> 14.7 us  [local(): lax.ppermute(pieces[d], 'head', [(i, (i + d) % 4) for i in range(4)])]
    pallas_call x2 -> x3, Pallas kernels: 33.2 us -> 37 us  [attend(): pl.pallas_call(lambda *refs: attn_body(blocks, final, *refs), out_shape=o...]
  transfers between devices with their start and end apart: 13 -> 16, of which waited for: 5 -> 5; matrix products, arithmetic and copies ran while one was open for 0% -> 0% of each run, Pallas kernels for 17% -> 29%
where the time goes in v5:
time: 92.1 us; the launch traced here: 91.9 us
  Pallas kernels  38.9 us (42%)
  starting transfers between devices  27.3 us (30%)
  waiting for transfers between devices  25.6 us (28%)
    pallas_call x3, Pallas kernels, attend(): pl.pallas_call(lambda *refs: attn_body(blocks, final, *refs), out_shape=o...  37 us
    ppermute x4, waiting for transfers between devices, behind(): return lax.ppermute(x, 'seq', [(i, (i + by) % seq) for i in range(seq)])  15.3 us
    ppermute x6, starting transfers between devices, local(): lax.ppermute(pieces[d], 'head', [(i, (i + d) % 4) for i in range(4)])  14.7 us
    ppermute x6, waiting for transfers between devices, local(): lax.ppermute(pieces[d], 'head', [(i, (i + d) % 4) for i in range(4)])  10.3 us
    ppermute x6, starting transfers between devices, swap(): return lax.ppermute(x, 'seq', [(i, i ^ 1) for i in range(seq)])  6.85 us
    ppermute x4, starting transfers between devices, behind(): return lax.ppermute(x, 'seq', [(i, (i + by) % seq) for i in range(seq)])  5.75 us
  transfers between devices with their start and end apart: 16, of which 5 were waited for; matrix products, arithmetic and copies ran while one was open for 0% of the time, Pallas kernels for 29%

profile of v5, /device:TPU:1, one launch (start us, length us, event | category | flops | bytes accessed | tf_op | source)
XLA Modules:
  0.0 91.9 jit_solution(14907592765764851630)
XLA Ops:
  0.0 1.0 %pack.1 = (bf16[256,256]{1,0:T(8,128)(2,1)S(1)}, bf16[320,256]{1,0:T(8,128)(2,1)S(1)}, bf16[256,256]{1,0:T(8,128)(2,1)S(1)}, bf16[320,256]{1,0:T(8,128)(2,1)S(1)}) custom-call(bf16[128,512]{1,0:T(8,128)(2,1)} %k_ref.1, bf16[128,512]{1,0:T(8,128)(2,1)} %v_ref.1, bf16[128,512]{1,0:T(8,128)(2,1)} %refs_3_.5, bf16[128,512]{1,0:T(8,128)(2,1)} %refs_4_.5), custom_call_target="tpu_custom_call" | custom-call | tf_op jit(solution)/shard_map/pack/pallas_call | solution.py:301
  1.0 2.1 %collective-permute-start = (bf16[320,256]{1,0:T(8,128)(2,1)S(1)}, bf16[320,256]{1,0:T(8,128)(2,1)S(1)}, u32[]{:S(2)}, u32[]{:S(2)}) collective-permute-start(bf16[320,256]{1,0:T(8,128)(2,1)S(1)} %get-tuple-element.21), channel_id=1, source_target_pairs={{0,8},{4,12},{8,16},{12,20},{16,24},{20,28},{24,32},{28,36},{32,40... | collective-permute-start | bytes 491528 | tf_op jit(solution)/shard_map/ppermute | solution.py:326
  3.1 2.5 %collective-permute-start.1 = (bf16[256,256]{1,0:T(8,128)(2,1)S(1)}, bf16[256,256]{1,0:T(8,128)(2,1)S(1)}, u32[]{:S(2)}, u32[]{:S(2)}) collective-permute-start(bf16[256,256]{1,0:T(8,128)(2,1)S(1)} %get-tuple-element.22.refs_9_.refs_10_), channel_id=1, source_target_pairs={{0,16},{4,20},{8,24},{12,28},{16,32},{20,36},{24,40},{28,44},{32,4... | collective-permute-start | bytes 393224 | tf_op jit(solution)/shard_map/ppermute | solution.py:326
  5.6 1.2 %collective-permute-start.7 = (bf16[320,256]{1,0:T(8,128)(2,1)S(1)}, bf16[320,256]{1,0:T(8,128)(2,1)S(1)}, u32[]{:S(2)}, u32[]{:S(2)}) collective-permute-start(bf16[320,256]{1,0:T(8,128)(2,1)S(1)} %get-tuple-element.21), channel_id=1, source_target_pairs={{0,4},{4,0},{8,12},{12,8},{16,20},{20,16},{24,28},{28,24},{32,36},... | collective-permute-start | bytes 491528 | tf_op jit(solution)/shard_map/ppermute | solution.py:329
  6.8 5.8 %collective-permute-done.1.refs_17_.refs_18_ = bf16[256,256]{1,0:T(8,128)(2,1)S(1)} collective-permute-done((bf16[256,256]{1,0:T(8,128)(2,1)S(1)}, bf16[256,256]{1,0:T(8,128)(2,1)S(1)}, u32[]{:S(2)}, u32[]{:S(2)}) %collective-permute-start.1) | collective-permute-done | bytes 131104 | tf_op jit(solution)/shard_map/ppermute | solution.py:326
  12.6 0.0 collective-permute-done.refs_13_.refs_14_
  12.6 1.2 %collective-permute-start.3 = (bf16[320,256]{1,0:T(8,128)(2,1)S(1)}, bf16[320,256]{1,0:T(8,128)(2,1)S(1)}, u32[]{:S(2)}, u32[]{:S(2)}) collective-permute-start(bf16[320,256]{1,0:T(8,128)(2,1)S(1)} %get-tuple-element.25), channel_id=1, source_target_pairs={{0,8},{4,12},{8,16},{12,20},{16,24},{20,28},{24,32},{28,36},{32,40... | collective-permute-start | bytes 491528 | tf_op jit(solution)/shard_map/ppermute | solution.py:326
  13.8 3.9 %collective-permute-start.8 = (bf16[320,256]{1,0:T(8,128)(2,1)S(1)}, bf16[320,256]{1,0:T(8,128)(2,1)S(1)}, u32[]{:S(2)}, u32[]{:S(2)}) collective-permute-start(bf16[320,256]{1,0:T(8,128)(2,1)S(1)} %collective-permute-done.refs_13_.refs_14_), channel_id=1, source_target_pairs={{0,4},{4,0},{8,12},{12,8},{16,20},{20,16},{24,28},{28,24},{32,36},... | collective-permute-start | bytes 491528 | tf_op jit(solution)/shard_map/ppermute | solution.py:329
  17.8 0.0 collective-permute-start.5
  17.8 0.0 collective-permute-start.9
  17.8 0.0 collective-permute-done.7.refs_5_.refs_6_.refs_11_.refs_12_
  17.8 0.5 collective-permute-start.2
  18.3 9.5 %collective-permute-done.5.refs_17_.refs_18_ = bf16[256,256]{1,0:T(8,128)(2,1)S(1)} collective-permute-done((bf16[256,256]{1,0:T(8,128)(2,1)S(1)}, bf16[256,256]{1,0:T(8,128)(2,1)S(1)}, u32[]{:S(2)}, u32[]{:S(2)}) %collective-permute-start.5) | collective-permute-done | bytes 131104 | tf_op jit(solution)/shard_map/ppermute | solution.py:326
  27.8 1.2 %collective-permute-start.6 = (bf16[256,256]{1,0:T(8,128)(2,1)S(1)}, bf16[256,256]{1,0:T(8,128)(2,1)S(1)}, u32[]{:S(2)}, u32[]{:S(2)}) collective-permute-start(bf16[256,256]{1,0:T(8,128)(2,1)S(1)} %collective-permute-done.5.refs_17_.refs_18_), channel_id=1, source_target_pairs={{0,4},{4,0},{8,12},{12,8},{16,20},{20,16},{24,28},{28,24},{32,36},... | collective-permute-start | bytes 393224 | tf_op jit(solution)/shard_map/ppermute | solution.py:329
  28.9 0.0 collective-permute-done.3.refs_13_.refs_14_
  28.9 0.0 collective-permute-start.4
  28.9 0.0 collective-permute-done.9.refs_19_.refs_20_
  28.9 0.0 collective-permute-done.8.refs_7_.refs_8_.refs_15_.refs_16_
  29.0 15.8 %shard_map.64.refs_21_ = bf16[128,512]{1,0:T(8,128)(2,1)S(1)} custom-call(s32[1]{0:T(128)} %bitcast.refs_0_, s32[1]{0:T(128)} %bitcast.1.refs_1_, bf16[128,1024]{1,0:T(8,128)(2,1)} %refs_2_.5, bf16[128,512]{1,0:T(8,128)(2,1)} %refs_3_.5, bf16[128,512]{1,0:T(8,128)(2,1)} %refs_4_.5, ...), custom_call_target="tpu_custom_call" | custom-call | flops 21474836480 | bytes 12582912 | tf_op jit(solution)/shard_map/pallas_call | solution.py:267
  44.8 0.0 collective-permute-done.2.refs_5_.refs_6_.refs_11_.refs_12_
  44.8 0.0 collective-permute-done.6.refs_19_.refs_20_
  44.8 0.0 collective-permute-done.4.refs_7_.refs_8_.refs_15_.refs_16_
  44.8 10.6 %shard_map.66 = (bf16[64,1024]{1,0:T(8,128)(2,1)S(1)}, bf16[64,1024]{1,0:T(8,128)(2,1)S(1)}, bf16[64,1024]{1,0:T(8,128)(2,1)S(1)}, bf16[64,1024]{1,0:T(8,128)(2,1)S(1)}) custom-call(s32[1]{0:T(128)} %bitcast.refs_0_, s32[1]{0:T(128)} %bitcast.1.refs_1_, bf16[128,1024]{1,0:T(8,128)(2,1)} %refs_2_.5, bf16[128,512]{1,0:T(8,128)(2,1)} %refs_3_.5, ...), custom_call_target="tpu_custom_call" | custom-call | flops 10737418240 | bytes 12582912 | tf_op jit(solution)/shard_map/pallas_call | solution.py:267
  55.4 6.5 %collective-permute-start.13 = (bf16[64,1024]{1,0:T(8,128)(2,1)S(1)}, bf16[64,1024]{1,0:T(8,128)(2,1)S(1)}, u32[]{:S(2)}, u32[]{:S(2)}) collective-permute-start(bf16[64,1024]{1,0:T(8,128)(2,1)S(1)} %get-tuple-element.34), channel_id=1, source_target_pairs={{0,2},{1,3},{2,0},{3,1},{4,6},{5,7},{6,4},{7,5},{8,10},{9,11},{10,... | collective-permute-start | bytes 393224 | tf_op jit(solution)/shard_map/ppermute | solution.py:360
  62.0 1.2 %collective-permute-start.14 = (bf16[64,1024]{1,0:T(8,128)(2,1)S(1)}, bf16[64,1024]{1,0:T(8,128)(2,1)S(1)}, u32[]{:S(2)}, u32[]{:S(2)}) collective-permute-start(bf16[64,1024]{1,0:T(8,128)(2,1)S(1)} %get-tuple-element.35), channel_id=1, source_target_pairs={{0,1},{1,2},{2,3},{3,0},{4,5},{5,6},{6,7},{7,4},{8,9},{9,10},{10,1... | collective-permute-start | bytes 393224 | tf_op jit(solution)/shard_map/ppermute | solution.py:360
  63.2 2.4 %collective-permute-start.15 = (bf16[64,1024]{1,0:T(8,128)(2,1)S(1)}, bf16[64,1024]{1,0:T(8,128)(2,1)S(1)}, u32[]{:S(2)}, u32[]{:S(2)}) collective-permute-start(bf16[64,1024]{1,0:T(8,128)(2,1)S(1)} %get-tuple-element.36), channel_id=1, source_target_pairs={{0,3},{1,0},{2,1},{3,2},{4,7},{5,4},{6,5},{7,6},{8,11},{9,8},{10,9... | collective-permute-start | bytes 393224 | tf_op jit(solution)/shard_map/ppermute | solution.py:360
  65.6 10.6 %shard_map.65 = (bf16[64,1024]{1,0:T(8,128)(2,1)S(1)}, bf16[64,1024]{1,0:T(8,128)(2,1)S(1)}, bf16[64,1024]{1,0:T(8,128)(2,1)S(1)}, bf16[64,1024]{1,0:T(8,128)(2,1)S(1)}) custom-call(s32[1]{0:T(128)} %bitcast.refs_0_, s32[1]{0:T(128)} %bitcast.1.refs_1_, bf16[128,1024]{1,0:T(8,128)(2,1)} %refs_2_.5, bf16[128,512]{1,0:T(8,128)(2,1)} %refs_3_.5, ...), custom_call_target="tpu_custom_call" | custom-call | flops 10737418240 | bytes 12582912 | tf_op jit(solution)/shard_map/pallas_call | solution.py:267
  76.1 1.0 %collective-permute-start.10 = (bf16[64,1024]{1,0:T(8,128)(2,1)S(1)}, bf16[64,1024]{1,0:T(8,128)(2,1)S(1)}, u32[]{:S(2)}, u32[]{:S(2)}) collective-permute-start(bf16[64,1024]{1,0:T(8,128)(2,1)S(1)} %get-tuple-element.30), channel_id=1, source_target_pairs={{0,2},{1,3},{2,0},{3,1},{4,6},{5,7},{6,4},{7,5},{8,10},{9,11},{10,... | collective-permute-start | bytes 393224 | tf_op jit(solution)/shard_map/ppermute | solution.py:360
  77.1 1.2 %collective-permute-start.11 = (bf16[64,1024]{1,0:T(8,128)(2,1)S(1)}, bf16[64,1024]{1,0:T(8,128)(2,1)S(1)}, u32[]{:S(2)}, u32[]{:S(2)}) collective-permute-start(bf16[64,1024]{1,0:T(8,128)(2,1)S(1)} %get-tuple-element.31), channel_id=1, source_target_pairs={{0,1},{1,2},{2,3},{3,0},{4,5},{5,6},{6,7},{7,4},{8,9},{9,10},{10,1... | collective-permute-start | bytes 393224 | tf_op jit(solution)/shard_map/ppermute | solution.py:360
  78.3 0.0 collective-permute-done.13.refs_5_
  78.3 2.4 %collective-permute-start.12 = (bf16[64,1024]{1,0:T(8,128)(2,1)S(1)}, bf16[64,1024]{1,0:T(8,128)(2,1)S(1)}, u32[]{:S(2)}, u32[]{:S(2)}) collective-permute-start(bf16[64,1024]{1,0:T(8,128)(2,1)S(1)} %get-tuple-element.32), channel_id=1, source_target_pairs={{0,3},{1,0},{2,1},{3,2},{4,7},{5,4},{6,5},{7,6},{8,11},{9,8},{10,9... | collective-permute-start | bytes 393224 | tf_op jit(solution)/shard_map/ppermute | solution.py:360
  80.7 0.0 collective-permute-done.14.refs_6_
  80.7 0.0 collective-permute-done.15.refs_7_
  80.7 5.7 %collective-permute-done.10.refs_1_ = bf16[64,1024]{1,0:T(8,128)(2,1)S(1)} collective-permute-done((bf16[64,1024]{1,0:T(8,128)(2,1)S(1)}, bf16[64,1024]{1,0:T(8,128)(2,1)S(1)}, u32[]{:S(2)}, u32[]{:S(2)}) %collective-permute-start.10) | collective-permute-done | bytes 131104 | tf_op jit(solution)/shard_map/ppermute | solution.py:360
  86.4 0.6 collective-permute-done.11.refs_2_
  87.0 4.0 %collective-permute-done.12.refs_3_ = bf16[64,1024]{1,0:T(8,128)(2,1)S(1)} collective-permute-done((bf16[64,1024]{1,0:T(8,128)(2,1)S(1)}, bf16[64,1024]{1,0:T(8,128)(2,1)S(1)}, u32[]{:S(2)}, u32[]{:S(2)}) %collective-permute-start.12) | collective-permute-done | bytes 131104 | tf_op jit(solution)/shard_map/ppermute | solution.py:360
  91.0 0.8 add.1
Async XLA Ops:
  1.0 11.6 %collective-permute-start = (bf16[320,256]{1,0:T(8,128)(2,1)S(1)}, bf16[320,256]{1,0:T(8,128)(2,1)S(1)}, u32[]{:S(2)}, u32[]{:S(2)}) collective-permute-start(bf16[320,256]{1,0:T(8,128)(2,1)S(1)} %get-tuple-element.21), channel_id=1, source_target_pairs={{0,8},{4,12},{8,16},{12,20},{16,24},{20,28},{24,32},{28,36},{32,40... | collective-permute-start | bytes 491528 | tf_op jit(solution)/shard_map/ppermute | solution.py:326
  3.1 9.5 %collective-permute-start.1 = (bf16[256,256]{1,0:T(8,128)(2,1)S(1)}, bf16[256,256]{1,0:T(8,128)(2,1)S(1)}, u32[]{:S(2)}, u32[]{:S(2)}) collective-permute-start(bf16[256,256]{1,0:T(8,128)(2,1)S(1)} %get-tuple-element.22.refs_9_.refs_10_), channel_id=1, source_target_pairs={{0,16},{4,20},{8,24},{12,28},{16,32},{20,36},{24,40},{28,44},{32,4... | collective-permute-start | bytes 393224 | tf_op jit(solution)/shard_map/ppermute | solution.py:326
  5.6 12.2 %collective-permute-start.7 = (bf16[320,256]{1,0:T(8,128)(2,1)S(1)}, bf16[320,256]{1,0:T(8,128)(2,1)S(1)}, u32[]{:S(2)}, u32[]{:S(2)}) collective-permute-start(bf16[320,256]{1,0:T(8,128)(2,1)S(1)} %get-tuple-element.21), channel_id=1, source_target_pairs={{0,4},{4,0},{8,12},{12,8},{16,20},{20,16},{24,28},{28,24},{32,36},... | collective-permute-start | bytes 491528 | tf_op jit(solution)/shard_map/ppermute | solution.py:329
  12.6 16.3 %collective-permute-start.3 = (bf16[320,256]{1,0:T(8,128)(2,1)S(1)}, bf16[320,256]{1,0:T(8,128)(2,1)S(1)}, u32[]{:S(2)}, u32[]{:S(2)}) collective-permute-start(bf16[320,256]{1,0:T(8,128)(2,1)S(1)} %get-tuple-element.25), channel_id=1, source_target_pairs={{0,8},{4,12},{8,16},{12,20},{16,24},{20,28},{24,32},{28,36},{32,40... | collective-permute-start | bytes 491528 | tf_op jit(solution)/shard_map/ppermute | solution.py:326
  13.8 15.1 %collective-permute-start.8 = (bf16[320,256]{1,0:T(8,128)(2,1)S(1)}, bf16[320,256]{1,0:T(8,128)(2,1)S(1)}, u32[]{:S(2)}, u32[]{:S(2)}) collective-permute-start(bf16[320,256]{1,0:T(8,128)(2,1)S(1)} %collective-permute-done.refs_13_.refs_14_), channel_id=1, source_target_pairs={{0,4},{4,0},{8,12},{12,8},{16,20},{20,16},{24,28},{28,24},{32,36},... | collective-permute-start | bytes 491528 | tf_op jit(solution)/shard_map/ppermute | solution.py:329
  17.8 10.0 %collective-permute-start.5 = (bf16[256,256]{1,0:T(8,128)(2,1)S(1)}, bf16[256,256]{1,0:T(8,128)(2,1)S(1)}, u32[]{:S(2)}, u32[]{:S(2)}) collective-permute-start(bf16[256,256]{1,0:T(8,128)(2,1)S(1)} %get-tuple-element.26.refs_9_.refs_10_), channel_id=1, source_target_pairs={{0,16},{4,20},{8,24},{12,28},{16,32},{20,36},{24,40},{28,44},{32,4... | collective-permute-start | bytes 393224 | tf_op jit(solution)/shard_map/ppermute | solution.py:326
  17.8 11.2 %collective-permute-start.9 = (bf16[256,256]{1,0:T(8,128)(2,1)S(1)}, bf16[256,256]{1,0:T(8,128)(2,1)S(1)}, u32[]{:S(2)}, u32[]{:S(2)}) collective-permute-start(bf16[256,256]{1,0:T(8,128)(2,1)S(1)} %collective-permute-done.1.refs_17_.refs_18_), channel_id=1, source_target_pairs={{0,4},{4,0},{8,12},{12,8},{16,20},{20,16},{24,28},{28,24},{32,36},... | collective-permute-start | bytes 393224 | tf_op jit(solution)/shard_map/ppermute | solution.py:329
  17.8 27.0 %collective-permute-start.2 = (bf16[320,256]{1,0:T(8,128)(2,1)S(1)}, bf16[320,256]{1,0:T(8,128)(2,1)S(1)}, u32[]{:S(2)}, u32[]{:S(2)}) collective-permute-start(bf16[320,256]{1,0:T(8,128)(2,1)S(1)} %get-tuple-element.25), channel_id=1, source_target_pairs={{0,4},{4,0},{8,12},{12,8},{16,20},{20,16},{24,28},{28,24},{32,36},... | collective-permute-start | bytes 491528 | tf_op jit(solution)/shard_map/ppermute | solution.py:329
  27.8 17.0 %collective-permute-start.6 = (bf16[256,256]{1,0:T(8,128)(2,1)S(1)}, bf16[256,256]{1,0:T(8,128)(2,1)S(1)}, u32[]{:S(2)}, u32[]{:S(2)}) collective-permute-start(bf16[256,256]{1,0:T(8,128)(2,1)S(1)} %collective-permute-done.5.refs_17_.refs_18_), channel_id=1, source_target_pairs={{0,4},{4,0},{8,12},{12,8},{16,20},{20,16},{24,28},{28,24},{32,36},... | collective-permute-start | bytes 393224 | tf_op jit(solution)/shard_map/ppermute | solution.py:329
  28.9 15.9 %collective-permute-start.4 = (bf16[320,256]{1,0:T(8,128)(2,1)S(1)}, bf16[320,256]{1,0:T(8,128)(2,1)S(1)}, u32[]{:S(2)}, u32[]{:S(2)}) collective-permute-start(bf16[320,256]{1,0:T(8,128)(2,1)S(1)} %collective-permute-done.3.refs_13_.refs_14_), channel_id=1, source_target_pairs={{0,4},{4,0},{8,12},{12,8},{16,20},{20,16},{24,28},{28,24},{32,36},... | collective-permute-start | bytes 491528 | tf_op jit(solution)/shard_map/ppermute | solution.py:329
  55.4 22.9 %collective-permute-start.13 = (bf16[64,1024]{1,0:T(8,128)(2,1)S(1)}, bf16[64,1024]{1,0:T(8,128)(2,1)S(1)}, u32[]{:S(2)}, u32[]{:S(2)}) collective-permute-start(bf16[64,1024]{1,0:T(8,128)(2,1)S(1)} %get-tuple-element.34), channel_id=1, source_target_pairs={{0,2},{1,3},{2,0},{3,1},{4,6},{5,7},{6,4},{7,5},{8,10},{9,11},{10,... | collective-permute-start | bytes 393224 | tf_op jit(solution)/shard_map/ppermute | solution.py:360
  62.0 18.7 %collective-permute-start.14 = (bf16[64,1024]{1,0:T(8,128)(2,1)S(1)}, bf16[64,1024]{1,0:T(8,128)(2,1)S(1)}, u32[]{:S(2)}, u32[]{:S(2)}) collective-permute-start(bf16[64,1024]{1,0:T(8,128)(2,1)S(1)} %get-tuple-element.35), channel_id=1, source_target_pairs={{0,1},{1,2},{2,3},{3,0},{4,5},{5,6},{6,7},{7,4},{8,9},{9,10},{10,1... | collective-permute-start | bytes 393224 | tf_op jit(solution)/shard_map/ppermute | solution.py:360
  63.2 17.5 %collective-permute-start.15 = (bf16[64,1024]{1,0:T(8,128)(2,1)S(1)}, bf16[64,1024]{1,0:T(8,128)(2,1)S(1)}, u32[]{:S(2)}, u32[]{:S(2)}) collective-permute-start(bf16[64,1024]{1,0:T(8,128)(2,1)S(1)} %get-tuple-element.36), channel_id=1, source_target_pairs={{0,3},{1,0},{2,1},{3,2},{4,7},{5,4},{6,5},{7,6},{8,11},{9,8},{10,9... | collective-permute-start | bytes 393224 | tf_op jit(solution)/shard_map/ppermute | solution.py:360
  76.1 10.3 %collective-permute-start.10 = (bf16[64,1024]{1,0:T(8,128)(2,1)S(1)}, bf16[64,1024]{1,0:T(8,128)(2,1)S(1)}, u32[]{:S(2)}, u32[]{:S(2)}) collective-permute-start(bf16[64,1024]{1,0:T(8,128)(2,1)S(1)} %get-tuple-element.30), channel_id=1, source_target_pairs={{0,2},{1,3},{2,0},{3,1},{4,6},{5,7},{6,4},{7,5},{8,10},{9,11},{10,... | collective-permute-start | bytes 393224 | tf_op jit(solution)/shard_map/ppermute | solution.py:360
  77.1 9.9 %collective-permute-start.11 = (bf16[64,1024]{1,0:T(8,128)(2,1)S(1)}, bf16[64,1024]{1,0:T(8,128)(2,1)S(1)}, u32[]{:S(2)}, u32[]{:S(2)}) collective-permute-start(bf16[64,1024]{1,0:T(8,128)(2,1)S(1)} %get-tuple-element.31), channel_id=1, source_target_pairs={{0,1},{1,2},{2,3},{3,0},{4,5},{5,6},{6,7},{7,4},{8,9},{9,10},{10,1... | collective-permute-start | bytes 393224 | tf_op jit(solution)/shard_map/ppermute | solution.py:360
  78.3 12.7 %collective-permute-start.12 = (bf16[64,1024]{1,0:T(8,128)(2,1)S(1)}, bf16[64,1024]{1,0:T(8,128)(2,1)S(1)}, u32[]{:S(2)}, u32[]{:S(2)}) collective-permute-start(bf16[64,1024]{1,0:T(8,128)(2,1)S(1)} %get-tuple-element.32), channel_id=1, source_target_pairs={{0,3},{1,0},{2,1},{3,2},{4,7},{5,4},{6,5},{7,6},{8,11},{9,8},{10,9... | collective-permute-start | bytes 393224 | tf_op jit(solution)/shard_map/ppermute | solution.py:360
